TPU v7x, 32 devices: a whole 2x2x4 slice. The times are simulated.
32 devices in a mesh: dp: 4 (over z), ctx: 2 (over x), tp: 4 (over y, core).
Axes of the slice: x: 2, y: 2, z: 4, core: 2. Of those that a mesh axis runs over, the one named last changes fastest.
Arguments:
- q_long: bfloat16 [4, 512, 4096], P('dp', 'ctx', 'tp'), may hold values from -24 to 24
- long_key_value: bfloat16 [4, 2, 512, 512], P('dp', None, 'ctx', 'tp'), may hold values from -24 to 24
- q_short: bfloat16 [8, 128, 4096], P(('dp', 'ctx'), None, 'tp'), may hold values from -24 to 24
- short_key_value: bfloat16 [8, 2, 128, 512], P(('dp', 'ctx'), None, None, 'tp'), may hold values from -24 to 24
- doc_ids: int32 [8, 128], P(('dp', 'ctx')), may hold values from 0 to 15, as said below
- live_counts: int32 [8], P(('dp', 'ctx')), may hold values from 64 to 128, as said below
- rescale: float32 [64], replicated, may hold values from 1 to 32
- output_weight: bfloat16 [4, 1024, 8192], P('tp', 'dp', 'ctx'), may hold values from -0.09375 to 0.09375
Outputs:
- projected: bfloat16 [4, 704, 8192], P('dp', 'tp', 'ctx')
Inputs may be any that keep to these rules, and one draw needn't show every extreme that they name: `doc_ids`: along each slab the document number starts at 0, never falls, rises by at most one, and rises only at slots that are multiples of 8. `live_counts`: multiples of 8; the counts of the slabs of one document group sum to 96 times their number.
All inputs are finite; a program needn't handle non-finite values.
Results may differ from a plain program's by a relative error of at most 0.009.
Values may be sent and summed in bfloat16 or wider, within the bound.
No kernel may reach another device: no remote copies, remote signals or barrier semaphores. Data moves between devices by JAX's collectives and lax.ppermute only.
A program may use at most 128 MiB of HBM per device.

v0:
```python
import math

import jax
import jax.numpy as jnp
from jax import lax
from jax.sharding import PartitionSpec as P

NEGATIVE_FILL = -1e30
ROPE_BASE = 500000.0


def apply_head_rotation(value_tensor, positions, rescale):
    head_size = value_tensor.shape[-1]
    half_size = head_size // 2
    exponents = jnp.arange(half_size, dtype=jnp.float32) * (2.0 / head_size)
    inverse = jnp.exp(-exponents * math.log(ROPE_BASE)) / rescale
    angles = positions.astype(jnp.float32)[:, None] * inverse[None, :]
    cosine = jnp.cos(angles)[:, None, :]
    sine = jnp.sin(angles)[:, None, :]
    first_half = value_tensor[..., :half_size]
    second_half = value_tensor[..., half_size:]
    return jnp.concatenate(
        [first_half * cosine - second_half * sine, second_half * cosine + first_half * sine],
        axis=-1,
    )


def absorb(running, query_rows, query_positions, key_rows, value_rows, key_positions, score_scale):
    row_max, row_sum, weighted = running
    scores = (
        jnp.einsum("qhd,kd->qhk", query_rows, key_rows, preferred_element_type=jnp.float32)
        * score_scale
    )
    visible = key_positions[None, None, :] <= query_positions[:, None, None]
    scores = jnp.where(visible, scores, NEGATIVE_FILL)
    new_max = jnp.maximum(row_max, jnp.max(scores, axis=-1))
    weights = jnp.where(visible, jnp.exp(scores - new_max[..., None]), 0.0)
    rescaling = jnp.exp(row_max - new_max)
    row_sum = rescaling * row_sum + jnp.sum(weights, axis=-1)
    weighted = rescaling[..., None] * weighted + jnp.einsum(
        "qhk,kd->qhd", weights.astype(jnp.bfloat16), value_rows, preferred_element_type=jnp.float32
    )
    return (new_max, row_sum, weighted)


def local(
    q_long, long_key_value, q_short, short_key_value, doc_ids, live_counts, rescale, output_weight
):
    head_size = rescale.shape[0] * 2
    group_heads = q_long.shape[2] // head_size
    long_rows = q_long.shape[1]
    half_rows = long_rows // 2
    short_rows = q_short.shape[1]
    slot_rows = long_rows + short_rows
    score_scale = 1.0 / math.sqrt(head_size)
    ctx_index = lax.axis_index("ctx")
    ctx_count = lax.axis_size("ctx")
    own_positions = ctx_index * long_rows + jnp.arange(long_rows, dtype=jnp.int32)
    rotated_queries = apply_head_rotation(
        q_long[0].astype(jnp.float32).reshape(long_rows, group_heads, head_size),
        own_positions,
        rescale,
    ).astype(jnp.bfloat16)
    long_key_rows = (
        apply_head_rotation(
            long_key_value[0, 0].astype(jnp.float32).reshape(long_rows, 1, head_size),
            own_positions,
            rescale,
        )
        .reshape(long_rows, head_size)
        .astype(jnp.bfloat16)
    )
    rotated_pairs = jnp.stack([long_key_rows, long_key_value[0, 1]], axis=0)
    query_halves = rotated_queries.reshape(2, half_rows, group_heads, head_size)
    position_halves = own_positions.reshape(2, half_rows)

    def fold_keys(running, pieces):
        total_rows = pieces.shape[1]
        key_block = math.gcd(total_rows, 512)
        results = []
        for half_id in range(2):
            sub_state = (running[0][half_id], running[1][half_id], running[2][half_id])

            def one_block(block_id, partial_state, half_id=half_id):
                key_rows = lax.dynamic_slice_in_dim(pieces[0], block_id * key_block, key_block, 0)
                value_rows = lax.dynamic_slice_in_dim(pieces[1], block_id * key_block, key_block, 0)
                key_positions = block_id * key_block + jnp.arange(key_block, dtype=jnp.int32)
                return absorb(
                    partial_state,
                    query_halves[half_id],
                    position_halves[half_id],
                    key_rows,
                    value_rows,
                    key_positions,
                    score_scale,
                )

            def full_fold(partial_state, one_block=one_block):
                return lax.fori_loop(0, total_rows // key_block, one_block, partial_state)

            result_state = full_fold(sub_state)
            results.append(result_state)
        return tuple(
            (jnp.stack([results[0][member], results[1][member]], axis=0) for member in range(3))
        )

    start_state = (
        jnp.full((2, half_rows, group_heads), NEGATIVE_FILL, jnp.float32),
        jnp.zeros((2, half_rows, group_heads), jnp.float32),
        jnp.zeros((2, half_rows, group_heads, head_size), jnp.float32),
    )
    row_max, row_sum, weighted = fold_keys(
        start_state, lax.all_gather(rotated_pairs, "ctx", axis=1, tiled=True)
    )
    computed_attn = (
        (weighted / row_sum[..., None])
        .reshape(long_rows, group_heads * head_size)
        .astype(jnp.bfloat16)
    )
    row_index = jnp.arange(short_rows, dtype=jnp.int32)
    doc_row = doc_ids[0]
    changes = jnp.concatenate([jnp.ones((1,), dtype=bool), doc_row[1:] != doc_row[:-1]])
    first_rows = lax.cummax(jnp.where(changes, row_index, 0), axis=0)
    short_token_positions = row_index - first_rows
    short_queries = apply_head_rotation(
        q_short[0].astype(jnp.float32).reshape(short_rows, group_heads, head_size),
        short_token_positions,
        rescale,
    ).astype(jnp.bfloat16)
    short_key_rows = (
        apply_head_rotation(
            short_key_value[0, 0].astype(jnp.float32).reshape(short_rows, 1, head_size),
            short_token_positions,
            rescale,
        )
        .reshape(short_rows, head_size)
        .astype(jnp.bfloat16)
    )
    visible_short = (doc_row[None, :] == doc_row[:, None]) & (
        row_index[None, :] <= row_index[:, None]
    )
    short_scores = (
        jnp.einsum("qhd,kd->qhk", short_queries, short_key_rows, preferred_element_type=jnp.float32)
        * score_scale
    )
    short_scores = jnp.where(visible_short[:, None, :], short_scores, NEGATIVE_FILL)
    short_peak = jnp.max(short_scores, axis=-1, keepdims=True)
    short_weights = jnp.where(visible_short[:, None, :], jnp.exp(short_scores - short_peak), 0.0)
    short_total = jnp.sum(short_weights, axis=-1, keepdims=True)
    short_weighted = jnp.einsum(
        "qhk,kd->qhd",
        short_weights.astype(jnp.bfloat16),
        short_key_value[0, 1],
        preferred_element_type=jnp.float32,
    )
    short_attn = (
        (short_weighted / short_total)
        .reshape(short_rows, group_heads * head_size)
        .astype(jnp.bfloat16)
    )
    packed = jnp.concatenate([computed_attn, short_attn], axis=0)
    all_counts = lax.all_gather(live_counts, "ctx", axis=0, tiled=True)
    live_rows = long_rows + all_counts
    offsets = jnp.cumsum(live_rows) - live_rows
    group_rows = ctx_count * (long_rows + 3 * short_rows // 4)
    slot_index = jnp.arange(slot_rows, dtype=jnp.int32)
    w_rows = lax.all_gather(output_weight, "dp", axis=1, tiled=True)[0]

    def place_rows(target_rows, source_rows, source_id):
        live_mask = slot_index < live_rows[source_id]
        masked = jnp.where(live_mask[:, None], source_rows, jnp.zeros((), source_rows.dtype))
        window = lax.dynamic_slice_in_dim(target_rows, offsets[source_id], slot_rows, 0)
        return lax.dynamic_update_slice_in_dim(target_rows, window + masked, offsets[source_id], 0)

    empty_rows = jnp.zeros((group_rows + slot_rows, packed.shape[1]), jnp.bfloat16)
    pieces = lax.all_gather(packed, "ctx", axis=0, tiled=True)
    count_here = pieces.shape[0] // slot_rows

    def one_slab(slab_id, current_rows):
        source_rows = lax.dynamic_slice_in_dim(pieces, slab_id * slot_rows, slot_rows, 0)
        return place_rows(current_rows, source_rows, slab_id)

    dense_rows = lax.fori_loop(0, count_here, one_slab, empty_rows)
    summed = lax.psum_scatter(
        jnp.dot(
            lax.slice_in_dim(
                dense_rows, 0, lax.axis_size("tp") * (group_rows // lax.axis_size("tp")), axis=0
            ),
            w_rows,
            preferred_element_type=jnp.float32,
        ).astype(jnp.bfloat16),
        "tp",
        scatter_dimension=0,
        tiled=True,
    ).astype(jnp.float32)
    return summed.astype(jnp.bfloat16).reshape(1, summed.shape[0], summed.shape[1])


def solution(mesh):
    in_specs = (
        P("dp", "ctx", "tp"),
        P("dp", None, "ctx", "tp"),
        P(("dp", "ctx"), None, "tp"),
        P(("dp", "ctx"), None, None, "tp"),
        P(("dp", "ctx"), None),
        P(("dp", "ctx")),
        P(),
        P("tp", "dp", "ctx"),
    )
    out_specs = P("dp", "tp", "ctx")
    return jax.shard_map(local, mesh=mesh, in_specs=in_specs, out_specs=out_specs, check_vma=False)
```

profile of v0, /device:TPU:0, one launch (start us, length us, event | category | flops | bytes accessed | tf_op | source)
XLA Modules:
  0.0 281.1 jit_solution(13380109034070507763)
XLA Ops:
  6.5 0.7 exponential_divide_fusion
  7.2 0.8 compare_bitcast_fusion
  8.0 0.8 fusion.51
  8.8 0.8 slice.95
  10.7 1.1 copy.34
  14.8 7.1 %all_gather.13 = bf16[2,512,128]{1,2,0:T(8,128)(2,1)S(1)} all-gather(bf16[2,256,128]{1,2,0:T(8,128)(2,1)S(1)} %pad_maximum_fusion.3), channel_id=1, replica_groups=mesh['dp'=4,'ctx'=2,'tp'=4] {'ctx'}, dimensions={1}, use_global_device_ids=true | all-gather | bytes 393216 | tf_op jit(solution)/shard_map/all_gather | solution.py:113
  23.7 0.6 fusion.10
  24.3 0.7 fusion.13
  25.0 0.8 fusion.18
  25.8 0.7 fusion.9
  26.5 0.7 fusion.11
  27.2 0.8 fusion.17
  28.8 0.9 pad_maximum_fusion
  29.8 0.7 all-gather.5.cloned.1.call-update
  31.2 0.6 dynamic-slice
  31.8 0.7 dynamic-update-slice
  32.5 4.3 %all-reduce = s32[2]{0:T(128)S(1)} all-reduce(s32[2]{0:T(128)S(1)} %dynamic-update-slice), channel_id=1, replica_groups=mesh['dp'=4,'ctx'=2,'tp'=4] {'ctx'}, use_global_device_ids=true, to_apply=%add | all-reduce | flops 2 | bytes 16
  36.9 21.8 %all-gather.3.cloned.1.call-done = bf16[768,1024]{1,0:T(8,128)(2,1)} async-done(((bf16[384,1024]{1,0:T(8,128)(2,1)}), bf16[768,1024]{1,0:T(8,128)(2,1)}) %all-gather.3.cloned.1.call-update) | async-done | bytes 1572880 | tf_op jit(solution)/shard_map/all_gather | solution.py:176
  58.9 18.9 %while.9 = (s32[]{:T(128)}, bf16[1088,1024]{1,0:T(8,128)(2,1)S(1)}, s32[2]{0:T(128)S(1)}, s32[2]{0:T(128)S(1)}, bf16[768,1024]{1,0:T(8,128)(2,1)}, /*index=5*/s3...) while((s32[]{:T(128)}, bf16[1088,1024]{1,0:T(8,128)(2,1)S(1)}, s32[2]{0:T(128)S(1)}, ...), condition=%wide.region_9.10_spmd.clone, body=%wide.region_8.9_spmd.clone.sunk | while | flops 1966473 | bytes 3933157 | solution.py:183
  59.0 0.6 dynamic_slice.49
  61.5 0.6 dynamic_slice.50
  62.1 0.6 iota_compare_fusion.5
  62.7 1.5 select_add_fusion.2
  64.3 4.1 %dynamic_update_slice.9 = bf16[1088,1024]{1,0:T(8,128)(2,1)S(1)} dynamic-update-slice(bf16[1088,1024]{1,0:T(8,128)(2,1)S(1)} %get-tuple-element.259, bf16[384,1024]{1,0:T(8,128)(2,1)S(1)} %select_add_fusion.2, s32[]{:T(128)S(6)} %select_n.134, s32[]{:T(128)} %constant.101.clone.1..sunk) | dynamic-update-slice | bytes 1572868 | tf_op jit(solution)/shard_map/while/body/eval_jaxpr/dynamic_update_slice | solution.py:173
  68.3 0.6 dynamic_slice.49
  70.9 0.6 dynamic_slice.50
  71.5 0.7 iota_compare_fusion.5
  72.1 1.6 select_add_fusion.2
  73.8 4.1 %dynamic_update_slice.9 = bf16[1088,1024]{1,0:T(8,128)(2,1)S(1)} dynamic-update-slice(bf16[1088,1024]{1,0:T(8,128)(2,1)S(1)} %get-tuple-element.259, bf16[384,1024]{1,0:T(8,128)(2,1)S(1)} %select_add_fusion.2, s32[]{:T(128)S(6)} %select_n.134, s32[]{:T(128)} %constant.101.clone.1..sunk) | dynamic-update-slice | bytes 1572868 | tf_op jit(solution)/shard_map/while/body/eval_jaxpr/dynamic_update_slice | solution.py:173
  77.8 132.1 %all-gather.5.cloned.1.call-done = bf16[1,1024,4096]{2,1,0:T(8,128)(2,1)} async-done(((bf16[1,256,4096]{2,1,0:T(8,128)(2,1)}), bf16[1,1024,4096]{2,1,0:T(8,128)(2,1)}) %all-gather.5.cloned.1.call-update) | async-done | bytes 8388624 | tf_op jit(solution)/shard_map/all_gather | solution.py:167
  210.0 11.4 %fusion.6 = bf16[704,4096]{1,0:T(8,128)(2,1)} fusion(bf16[1,1024,4096]{2,1,0:T(8,128)(2,1)} %all-gather.5.cloned.1.call-done, bf16[1088,1024]{1,0:T(8,128)(2,1)S(1)} %get-tuple-element.162), kind=kOutput, calls=%fused_computation.7 | convolution fusion | flops 5908463616 | bytes 15597568 | tf_op jit(solution)/shard_map/dot_general | solution.py:185
  221.3 53.2 %reduce-scatter.2.cloned.1.call-done = bf16[176,4096]{1,0:T(8,128)(2,1)} async-done(((bf16[704,4096]{1,0:T(8,128)(2,1)}), bf16[176,4096]{1,0:T(8,128)(2,1)}) %reduce-scatter.2.cloned.1.call-update) | async-done | bytes 1441808 | tf_op jit(solution)/shard_map/reduce_scatter | solution.py:184
  (60 shorter events, 7.0 us)
Async XLA Ops:
  6.5 52.1 %all-gather.3.cloned.1.call-start = ((), (), s32[]{:S(2)}) async-start(), calls=%async_computation.1 | async-start | bytes 2359296 | tf_op jit(solution)/shard_map/all_gather | solution.py:176
  12.3 1.3 copy-start.1
  12.5 9.4 %copy-start.2 = (bf16[1,2,128,128]{3,2,1,0:T(8,128)(2,1)S(1)}, bf16[1,2,128,128]{3,2,1,0:T(8,128)(2,1)}, u32[]{:S(2)}) copy-start(bf16[1,2,128,128]{3,2,1,0:T(8,128)(2,1)} %param.13) | copy-start | bytes 196612
  13.8 8.6 %copy-start = (bf16[1,256,1024]{2,1,0:T(8,128)(2,1)S(1)}, bf16[1,256,1024]{2,1,0:T(8,128)(2,1)}, u32[]{:S(2)}) copy-start(bf16[1,256,1024]{2,1,0:T(8,128)(2,1)} %param.10) | copy-start | bytes 1572868
  28.8 2.4 copy-start.3
  29.8 180.2 %all-gather.5.cloned.1.call-start = ((), (), s32[]{:S(2)}) async-start(), calls=%async_computation.2 | async-start | bytes 10485760 | tf_op jit(solution)/shard_map/all_gather | solution.py:167
  30.5 244.1 %reduce-scatter.2.cloned.1.call-start = ((), (), s32[]{:S(2)}) async-start(), calls=%async_computation.3 | async-start | bytes 7208960 | tf_op jit(solution)/shard_map/reduce_scatter | solution.py:184
Sparse Core Ops, SparseCore 0:
  29.9 28.7 all-gather.2
  60.2 149.6 all-gather.4
  221.5 53.0 reduce-scatter.1
where the time goes:
time: 282 us; the launch traced here: 281 us
  waiting for transfers between devices  208 us (74%)
  local copies, waits for them, and re-layouts  16.3 us (6%)
  matrix products  15.4 us (5%)
  between operations  14.1 us (5%)
  other arithmetic  12 us (4%)
  blocking collectives  11.3 us (4%)
  loops' own time  3.99 us (1%)
    all_gather x1, waiting for transfers between devices, local(): w_rows = lax.all_gather(output_weight, 'dp', axis=1, tiled=True)[0]  132 us
    reduce_scatter x1, waiting for transfers between devices, local(): lax.psum_scatter(jnp.dot(lax.slice_in_dim(dense_rows, 0, lax.axis_size('t...  53.2 us
    all_gather x1, waiting for transfers between devices, local(): pieces = lax.all_gather(packed, 'ctx', axis=0, tiled=True)  21.8 us
    dot_general x1, matrix products, local(): jnp.dot(lax.slice_in_dim(dense_rows, 0, lax.axis_size('tp') * (group_rows...  11.4 us
    dynamic_update_slice x2, local copies, waits for them, and re-layouts, place_rows(): lax.dynamic_update_slice_in_dim(target_rows, window + masked, offsets[sou...  8.11 us
    all_gather x1, blocking collectives, local(): lax.all_gather(rotated_pairs, 'ctx', axis=1, tiled=True)  7.09 us
  transfers between devices with their start and end apart: 3, of which 3 were waited for; matrix products, arithmetic and copies ran while one was open for 6% of the time, Pallas kernels for 0%

commit v1 on v0

v1 whole, which is shorter than its diff:
```python
import functools
import math

import jax
import jax.numpy as jnp
from jax import lax
from jax.experimental import pallas as pl
from jax.experimental.pallas import tpu as pltpu
from jax.sharding import PartitionSpec as P

NEGATIVE_FILL = -1e30
ROPE_BASE = 500000.0
COUNT_ROWS = 8
VMEM_LIMIT = 56 * 1024 * 1024
OUT_TO_IN = [(0, 1), (3, 2)]
IN_TO_OUT = [(1, 0), (2, 3)]
INNER = [(1, 2), (2, 1)]

SMEM_SPEC = pl.BlockSpec(memory_space=pltpu.SMEM)


def params():
    return pltpu.CompilerParams(vmem_limit_bytes=VMEM_LIMIT)


def half_turn(x, half):
    return jnp.concatenate([x[:, half:], x[:, :half]], axis=1)


def prepare_kernel(place_ref, kv_ref, doc_ref, rescale_ref, cos_ref, sin_ref, pair_ref):
    long_rows, head = kv_ref.shape[1], kv_ref.shape[2]
    half = head // 2
    slots = doc_ref.shape[1]
    lane = lax.broadcasted_iota(jnp.int32, (1, head), 1)
    frequency = jnp.where(lane < half, lane, lane - half).astype(jnp.float32)
    inverse = jnp.exp(-(frequency * (2.0 / head)) * math.log(ROPE_BASE)) / rescale_ref[...]
    sign = jnp.where(lane < half, -1.0, 1.0)
    row = lax.broadcasted_iota(jnp.int32, (long_rows, 1), 0) + place_ref[0] * long_rows
    angles = row.astype(jnp.float32) * inverse
    cosine, sine = jnp.cos(angles), jnp.sin(angles) * sign
    cos_ref[:long_rows, :] = cosine
    sin_ref[:long_rows, :] = sine
    keys = kv_ref[0].astype(jnp.float32)
    pair_ref[0] = (keys * cosine + half_turn(keys, half) * sine).astype(jnp.bfloat16)
    pair_ref[1] = kv_ref[1]
    docs = jnp.broadcast_to(doc_ref[...].astype(jnp.float32), (slots, slots))
    before = jnp.where(docs < docs.T, 1.0, 0.0)
    first = jnp.sum(before, axis=1, keepdims=True)
    slot = lax.broadcasted_iota(jnp.int32, (slots, 1), 0).astype(jnp.float32)
    short_angles = (slot - first) * inverse
    cos_ref[long_rows:, :] = jnp.cos(short_angles)
    sin_ref[long_rows:, :] = jnp.sin(short_angles) * sign


def prepare(place, kv, doc, rescale):
    slots, rows, head = doc.shape[1], kv.shape[1], kv.shape[2]
    table = jax.ShapeDtypeStruct((rows + slots, head), jnp.float32)
    return pl.pallas_call(
        prepare_kernel,
        in_specs=[SMEM_SPEC] + [pl.BlockSpec(memory_space=pltpu.VMEM)] * 3,
        out_specs=[pl.BlockSpec(memory_space=pltpu.VMEM)] * 3,
        out_shape=[table, table, jax.ShapeDtypeStruct(kv.shape, jnp.bfloat16)],
        compiler_params=params(),
        name="prepare",
    )(place, kv, doc, rescale)


def weigh(scores, visible, values):
    scores = [jnp.where(v, s, NEGATIVE_FILL) for s, v in zip(scores, visible)]
    peak = functools.reduce(jnp.maximum, [jnp.max(s, axis=1, keepdims=True) for s in scores])
    total, weighted = 0.0, 0.0
    for s, v, value in zip(scores, visible, values):
        weights = jnp.where(v, jnp.exp(s - peak), 0.0)
        total = total + jnp.sum(weights, axis=1, keepdims=True)
        weighted = weighted + jnp.dot(
            weights.astype(jnp.bfloat16), value, preferred_element_type=jnp.float32
        )
    return (weighted / total).astype(jnp.bfloat16)


def dot_t(a, b):
    return lax.dot_general(a, b, (((1,), (1,)), ((), ())), preferred_element_type=jnp.float32)


def attend_kernel(n_blocks, base_ref, ql_ref, qs_ref, skv_ref, doc_ref, cos_ref, sin_ref, *rest):
    pairs, out_ref = rest[:n_blocks], rest[n_blocks]
    long_rows, slots = ql_ref.shape[0], qs_ref.shape[0]
    head = cos_ref.shape[1]
    half = head // 2
    scale = 1.0 / math.sqrt(head)
    heads = ql_ref.shape[1] // head
    cosine, sine = cos_ref[...], sin_ref[...]

    def turn(x, first, last):
        return (x * cosine[first:last] + half_turn(x, half) * sine[first:last]).astype(jnp.bfloat16)

    row = lax.broadcasted_iota(jnp.int32, (long_rows, 1), 0) + base_ref[0] * long_rows
    visible = [
        lax.broadcasted_iota(jnp.int32, (long_rows, p.shape[1]), 1) + base_ref[1 + i] <= row
        for i, p in enumerate(pairs)
    ]
    short_keys = turn(skv_ref[0].astype(jnp.float32), long_rows, long_rows + slots)
    docs = jnp.broadcast_to(doc_ref[...].astype(jnp.float32), (slots, slots))
    below = lax.broadcasted_iota(jnp.int32, (slots, slots), 1) <= lax.broadcasted_iota(
        jnp.int32, (slots, slots), 0
    )
    short_visible = [(docs == docs.T) & below]
    short_values = [skv_ref[1]]
    for h in range(heads):
        columns = slice(h * head, (h + 1) * head)
        query = turn(ql_ref[:, columns].astype(jnp.float32), 0, long_rows)
        scores = [dot_t(query, p[0]) * scale for p in pairs]
        out_ref[:long_rows, columns] = weigh(scores, visible, [p[1] for p in pairs])
        query = turn(qs_ref[:, columns].astype(jnp.float32), long_rows, long_rows + slots)
        scores = [dot_t(query, short_keys) * scale]
        out_ref[long_rows : long_rows + slots, columns] = weigh(scores, short_visible, short_values)
    live = jnp.full((COUNT_ROWS, out_ref.shape[1]), base_ref[1 + n_blocks], jnp.int32)
    out_ref[long_rows + slots :, :] = live.astype(jnp.float32).astype(jnp.bfloat16)


def attend(scalars, q_long, q_short, short_kv, doc, cosine, sine, pairs):
    rows = q_long.shape[0] + q_short.shape[0] + COUNT_ROWS
    vmem = pl.BlockSpec(memory_space=pltpu.VMEM)
    return pl.pallas_call(
        functools.partial(attend_kernel, len(pairs)),
        in_specs=[SMEM_SPEC] + [vmem] * (6 + len(pairs)),
        out_specs=vmem,
        out_shape=jax.ShapeDtypeStruct((rows, q_long.shape[1]), jnp.bfloat16),
        compiler_params=params(),
        name="attend",
    )(scalars, q_long, q_short, short_kv, doc, cosine, sine, *pairs)


def pack_kernel(long_rows, slots, group_rows, n_pieces, scalar_ref, *rest):
    pieces, (send_ref, keep_ref, dense) = rest[:-3], rest[-3:]
    piece_rows = long_rows + slots

    def live_of(piece, first):
        tail = piece[pl.ds(first + piece_rows, COUNT_ROWS), :]
        return jnp.max(tail.astype(jnp.float32)).astype(jnp.int32)

    def put(piece, first, offset):
        rows = piece[pl.ds(first, piece_rows), :].astype(jnp.float32)
        dense[pl.ds(pl.multiple_of(offset, 8), piece_rows), :] = rows
        return offset + long_rows + live_of(piece, first)

    if len(pieces) == 1:
        offset = jnp.int32(0)
        for i in range(n_pieces):
            offset = put(pieces[0], i * (piece_rows + COUNT_ROWS), offset)
    else:
        mine, theirs = pieces

        @pl.when(scalar_ref[0] == 0)
        def _():
            put(theirs, 0, put(mine, 0, jnp.int32(0)))

        @pl.when(scalar_ref[0] != 0)
        def _():
            put(mine, 0, put(theirs, 0, jnp.int32(0)))

    quarter = group_rows // 4
    for ref, first in ((send_ref, 1), (keep_ref, 3)):
        for s in range(2):
            start = pl.multiple_of(scalar_ref[first + s] * quarter, 8)
            ref[s * quarter : (s + 1) * quarter, :] = dense[pl.ds(start, quarter), :].astype(
                jnp.bfloat16
            )


def pack(scalars, pieces, long_rows, slots, n_pieces):
    group_rows = n_pieces * (long_rows + 3 * slots // 4)
    columns = pieces[0].shape[1]
    block = columns // 4
    out = jax.ShapeDtypeStruct((group_rows // 2, columns), jnp.bfloat16)
    out_spec = pl.BlockSpec((group_rows // 2, block), lambda j, s: (0, j))
    return pl.pallas_call(
        functools.partial(pack_kernel, long_rows, slots, group_rows, n_pieces),
        grid_spec=pltpu.PrefetchScalarGridSpec(
            num_scalar_prefetch=1,
            grid=(4,),
            in_specs=[pl.BlockSpec((p.shape[0], block), lambda j, s: (0, s[5 + j])) for p in pieces],
            out_specs=[out_spec, out_spec],
            scratch_shapes=[pltpu.VMEM((group_rows + long_rows + slots, block), jnp.float32)],
        ),
        out_shape=[out, out],
        compiler_params=params(),
        name="pack",
    )(scalars, *pieces)


def project_kernel(with_add, inner_ref, own_ref, other_ref, *rest):
    weights, rest = rest[:4], rest[4:]
    rows = own_ref.shape[0]
    depth = weights[0].shape[0]
    for part, a_ref in enumerate((own_ref, other_ref)):
        out_ref, here = (rest[-2 + part], slice(0, rows)) if with_add else (
            rest[-1],
            slice(part * rows, (part + 1) * rows),
        )

        @pl.when(inner_ref[0] != 0)
        def _(part=part, a_ref=a_ref, out_ref=out_ref, here=here):
            total = functools.reduce(
                jnp.add,
                [
                    jnp.dot(
                        a_ref[:, i * depth : (i + 1) * depth],
                        w[...],
                        preferred_element_type=jnp.float32,
                    )
                    for i, w in enumerate(weights)
                ],
            )
            if with_add:
                total = total + rest[0][part * rows : (part + 1) * rows, :].astype(jnp.float32)
            out_ref[here, :] = total.astype(jnp.bfloat16)

        @pl.when(inner_ref[0] == 0)
        def _(out_ref=out_ref, here=here):
            out_ref[here, :] = jnp.zeros((rows, out_ref.shape[1]), jnp.bfloat16)


def project(inner, own, other, weights, received=None):
    rows, width = own.shape
    depth, columns = weights[0].shape
    tile = 512 if columns % 512 == 0 else 128
    full = pl.BlockSpec((rows, width), lambda j: (0, 0), pipeline_mode=pl.Buffered(1))
    both = pl.BlockSpec((2 * rows, tile), lambda j: (0, j))
    one = pl.BlockSpec((rows, tile), lambda j: (0, j))
    in_specs = [SMEM_SPEC, full, full] + [pl.BlockSpec((depth, tile), lambda j: (0, j))] * 4
    args = [inner, own, other, *weights]
    if received is None:
        out_specs = both
        out_shape = jax.ShapeDtypeStruct((2 * rows, columns), jnp.bfloat16)
    else:
        in_specs.append(both)
        args.append(received)
        out_specs = [one, one]
        out_shape = [jax.ShapeDtypeStruct((rows, columns), jnp.bfloat16)] * 2
    return pl.pallas_call(
        functools.partial(project_kernel, received is not None),
        grid=(columns // tile,),
        in_specs=in_specs,
        out_specs=out_specs,
        out_shape=out_shape,
        compiler_params=params(),
        name="project",
    )(*args)


def column_chunks(columns):
    unit = columns // 8
    if unit % 512:
        return [columns]
    return [3 * unit, 3 * unit, 2 * unit]


def local(
    q_long, long_key_value, q_short, short_key_value, doc_ids, live_counts, rescale, output_weight
):
    head = rescale.shape[0] * 2
    long_rows, slots = q_long.shape[1], q_short.shape[1]
    ctx, tp, dp = lax.axis_index("ctx"), lax.axis_index("tp"), lax.axis_index("dp")
    n_ctx = lax.axis_size("ctx")
    is_inner = (dp == 1) | (dp == 2)

    def swap_ctx(x):
        return lax.ppermute(x, "ctx", [(0, 1), (1, 0)])

    weight = output_weight[0]
    chunks, weights = column_chunks(weight.shape[1]), []
    start = 0
    for width in chunks:
        own = lax.slice_in_dim(weight, start, start + width, axis=1)
        start += width
        twin = lax.ppermute(own, "dp", INNER)
        near = lax.ppermute(own, "dp", OUT_TO_IN)
        far = lax.ppermute(near, "dp", INNER)
        weights.append((own, twin, near, far))
    near_plane = jnp.where(dp < 2, 0, 3)
    blocks = [dp, 3 - dp, near_plane, 3 - near_plane]

    cosine, sine, pair = prepare(
        ctx.reshape(1).astype(jnp.int32),
        long_key_value[0],
        doc_ids,
        jnp.concatenate([rescale, rescale]).reshape(1, head),
    )
    if n_ctx == 2:
        pairs = [pair, swap_ctx(pair)]
        bases = [ctx * long_rows, (1 - ctx) * long_rows]
    else:
        pairs = [lax.all_gather(pair, "ctx", axis=1, tiled=True)]
        bases = [jnp.int32(0)]
    rows = attend(
        jnp.stack([ctx, *bases, live_counts[0]]).astype(jnp.int32),
        q_long[0],
        q_short[0],
        short_key_value[0],
        doc_ids,
        cosine,
        sine,
        pairs,
    )

    scalars = jnp.stack(
        [ctx, (tp ^ 2) ^ 1, tp ^ 1, tp ^ 2, tp, *blocks]
    ).astype(jnp.int32)

    def gathered(x):
        if n_ctx == 2:
            return [x, swap_ctx(x)]
        return [lax.all_gather(x, "ctx", axis=0, tiled=True)]

    own_send, own_keep = pack(scalars, gathered(rows), long_rows, slots, n_ctx)
    other_rows = lax.ppermute(rows, "dp", OUT_TO_IN)
    other_send, other_keep = pack(scalars, gathered(other_rows), long_rows, slots, n_ctx)

    inner = is_inner.reshape(1).astype(jnp.int32)
    quarter = own_send.shape[0] // 2
    outputs = []
    for w in weights:
        partial = project(inner, own_send, other_send, w)
        received = lax.ppermute(partial, "tp", [(i, i ^ 1) for i in range(4)])
        own, other = project(inner, own_keep, other_keep, w, received)
        returned = lax.ppermute(other, "dp", IN_TO_OUT)
        summed = jnp.where(is_inner, own, returned)
        crossed = lax.ppermute(summed[:quarter], "tp", [(i, i ^ 2) for i in range(4)])
        outputs.append(
            (summed[quarter:].astype(jnp.float32) + crossed.astype(jnp.float32)).astype(
                jnp.bfloat16
            )
        )
    return jnp.concatenate(outputs, axis=1)[None]


def solution(mesh):
    in_specs = (
        P("dp", "ctx", "tp"),
        P("dp", None, "ctx", "tp"),
        P(("dp", "ctx"), None, "tp"),
        P(("dp", "ctx"), None, None, "tp"),
        P(("dp", "ctx"), None),
        P(("dp", "ctx")),
        P(),
        P("tp", "dp", "ctx"),
    )
    out_specs = P("dp", "tp", "ctx")
    return jax.shard_map(local, mesh=mesh, in_specs=in_specs, out_specs=out_specs, check_vma=False)
```

time: 282 us -> 229 us (0.81)
  waiting for transfers between devices: 208 us -> 135 us
  Pallas kernels: 0 us -> 44.9 us
  starting transfers between devices: 0.08 us -> 35.3 us
  matrix products: 15.4 us -> 0 us
  between operations: 14.1 us -> 0.95 us
  blocking collectives: 11.3 us -> 0 us
  local copies, waits for them, and re-layouts: 16.3 us -> 8.2 us
  other arithmetic: 12 us -> 3.94 us
  loops' own time: 3.99 us -> 0 us
    all_gather x2 -> x0, waiting for transfers between devices: 154 us -> none  [the longest x1 132 us: local(): w_rows = lax.all_gather(output_weight, 'dp', axis=1, tiled=True)[0]]
    ppermute x0 -> x22, waiting for transfers between devices: none -> 135 us  [the longest x3 81.2 us: local(): returned = lax.ppermute(other, 'dp', IN_TO_OUT)]
    reduce_scatter x1 -> x0, waiting for transfers between devices: 53.2 us -> none  [local(): lax.psum_scatter(jnp.dot(lax.slice_in_dim(dense_rows, 0, lax.axis_size('t...]
    pallas_call x0 -> x10, Pallas kernels: none -> 44.9 us  [the longest x6 25.6 us: project(): pl.pallas_call(functools.partial(project_kernel, received is not None), g...]
    ppermute x0 -> x22, starting transfers between devices: none -> 35.3 us  [the longest x3 9.13 us: local(): near = lax.ppermute(own, 'dp', OUT_TO_IN)]
    dot_general x7 -> x0, matrix products: 14.9 us -> none  [the longest x1 11.4 us: local(): jnp.dot(lax.slice_in_dim(dense_rows, 0, lax.axis_size('tp') * (group_rows...]
    dynamic_update_slice x2 -> x0, local copies, waits for them, and re-layouts: 8.11 us -> none  [place_rows(): lax.dynamic_update_slice_in_dim(target_rows, window + masked, offsets[sou...]
    all_gather x1 -> x0, blocking collectives: 7.09 us -> none  [local(): lax.all_gather(rotated_pairs, 'ctx', axis=1, tiled=True)]
  transfers between devices with their start and end apart: 3 -> 22, of which waited for: 3 -> 7; matrix products, arithmetic and copies ran while one was open for 6% -> 1% of each run, Pallas kernels for 0% -> 15%
where the time goes in v1:
time: 229 us; the launch traced here: 228 us
  waiting for transfers between devices  135 us (59%)
  Pallas kernels  44.9 us (20%)
  starting transfers between devices  35.3 us (15%)
  local copies, waits for them, and re-layouts  8.2 us (4%)
  other arithmetic  3.94 us (2%)
    ppermute x3, waiting for transfers between devices, local(): returned = lax.ppermute(other, 'dp', IN_TO_OUT)  81.2 us
    ppermute x3, waiting for transfers between devices, local(): near = lax.ppermute(own, 'dp', OUT_TO_IN)  26.9 us
    pallas_call x6, Pallas kernels, project(): pl.pallas_call(functools.partial(project_kernel, received is not None), g...  25.6 us
    ppermute x3, waiting for transfers between devices, local(): lax.ppermute(summed[:quarter], 'tp', [(i, i ^ 2) for i in range(4)])  12.3 us
    ppermute x1, waiting for transfers between devices, local(): other_rows = lax.ppermute(rows, 'dp', OUT_TO_IN)  12.3 us
    pallas_call x2, Pallas kernels, pack(): pl.pallas_call(functools.partial(pack_kernel, long_rows, slots, group_row...  9.57 us
    ppermute x3, starting transfers between devices, local(): near = lax.ppermute(own, 'dp', OUT_TO_IN)  9.13 us
    unnamed x36, local copies, waits for them, and re-layouts  7.34 us
  transfers between devices with their start and end apart: 22, of which 7 were waited for; matrix products, arithmetic and copies ran while one was open for 1% of the time, Pallas kernels for 15%

profile of v1, /device:TPU:0, one launch (start us, length us, event | category | flops | bytes accessed | tf_op | source)
XLA Modules:
  0.0 228.4 jit_solution(13921557429769069412)
XLA Ops:
  1.3 2.5 %prepare.1 = (f32[384,128]{1,0:T(8,128)}, f32[384,128]{1,0:T(8,128)}, bf16[2,256,128]{2,1,0:T(8,128)(2,1)}) custom-call(s32[1]{0:T(128)} %bitcast.1.place_ref, bf16[2,256,128]{2,1,0:T(8,128)(2,1)} %bitcast.25, s32[1,128]{1,0:T(1,128)} %doc_ref.3, f32[1,128]{1,0:T(1,128)} %maximum_bitcast_fusion.1.rescale_ref), custom_call_target="tpu_custom_call" | custom-call | tf_op jit(solution)/shard_map/prepare/pallas_call | solution.py:58
  3.8 2.9 %collective-permute-start = (bf16[2,256,128]{2,1,0:T(8,128)(2,1)}, bf16[2,256,128]{2,1,0:T(8,128)(2,1)S(1)}, u32[]{:S(2)}, u32[]{:S(2)}) collective-permute-start(bf16[2,256,128]{2,1,0:T(8,128)(2,1)} %get-tuple-element.20.rest_0_), channel_id=1, source_target_pairs={{0,4},{4,0},{1,5},{5,1},{2,6},{6,2},{3,7},{7,3},{8,12},{12,8},{9,1... | collective-permute-start | bytes 393224 | tf_op jit(solution)/shard_map/ppermute | solution.py:269
  8.1 2.4 %collective-permute-done.rest_1_ = bf16[2,256,128]{2,1,0:T(8,128)(2,1)S(1)} collective-permute-done((bf16[2,256,128]{2,1,0:T(8,128)(2,1)}, bf16[2,256,128]{2,1,0:T(8,128)(2,1)S(1)}, u32[]{:S(2)}, u32[]{:S(2)}) %collective-permute-start) | collective-permute-done | bytes 131104 | tf_op jit(solution)/shard_map/ppermute | solution.py:269
  11.1 7.2 %attend.1.rest_0_ = bf16[392,1024]{1,0:T(8,128)(2,1)} custom-call(s32[4]{0:T(128)} %pad_add_fusion.base_ref, bf16[256,1024]{1,0:T(8,128)(2,1)} %bitcast.23, bf16[128,1024]{1,0:T(8,128)(2,1)} %bitcast.24, bf16[2,128,128]{2,1,0:T(8,128)(2,1)} %bitcast.26, s32[1,128]{1,0:T(1,128)} %doc_ref.3, f32[384,128]{1,0:T(8,128)} %get-tuple-element.18.cos_ref, ...), custom_call_target="tpu_custom_call" | custom-call | tf_op jit(solution)/shard_map/attend/pallas_call | solution.py:124
  18.3 3.8 %collective-permute-start.2 = (bf16[392,1024]{1,0:T(8,128)(2,1)}, bf16[392,1024]{1,0:T(8,128)(2,1)S(1)}, u32[]{:S(2)}, u32[]{:S(2)}) collective-permute-start(bf16[392,1024]{1,0:T(8,128)(2,1)} %attend.1.rest_0_), channel_id=1, source_target_pairs={{0,8},{24,16},{1,9},{25,17},{2,10},{26,18},{3,11},{27,19},{4,12},{... | collective-permute-start | bytes 2408456 | tf_op jit(solution)/shard_map/ppermute | solution.py:317
  22.3 2.3 %collective-permute-start.5 = (bf16[256,1536]{1,0:T(8,128)(2,1)S(1)}, bf16[256,1536]{1,0:T(8,128)(2,1)}, u32[]{:S(2)}, u32[]{:S(2)}) collective-permute-start(bf16[256,1536]{1,0:T(8,128)(2,1)S(1)} %get-tuple-element.31.rest_0_), channel_id=1, source_target_pairs={{0,8},{24,16},{1,9},{25,17},{2,10},{26,18},{3,11},{27,19},{4,12},{... | collective-permute-start | bytes 2359304 | tf_op jit(solution)/shard_map/ppermute | solution.py:278
  24.6 2.3 collective-permute-start.11
  26.9 1.5 collective-permute-start.1
  28.4 12.3 %collective-permute-done.2.rest_0_ = bf16[392,1024]{1,0:T(8,128)(2,1)S(1)} collective-permute-done((bf16[392,1024]{1,0:T(8,128)(2,1)}, bf16[392,1024]{1,0:T(8,128)(2,1)S(1)}, u32[]{:S(2)}, u32[]{:S(2)}) %collective-permute-start.2) | collective-permute-done | bytes 802848 | tf_op jit(solution)/shard_map/ppermute | solution.py:317
  40.7 1.5 collective-permute-start.3
  42.2 1.5 collective-permute-start.4
  43.7 13.7 %collective-permute-done.5.rest_2_ = bf16[256,1536]{1,0:T(8,128)(2,1)} collective-permute-done((bf16[256,1536]{1,0:T(8,128)(2,1)S(1)}, bf16[256,1536]{1,0:T(8,128)(2,1)}, u32[]{:S(2)}, u32[]{:S(2)}) %collective-permute-start.5) | collective-permute-done | bytes 786464 | tf_op jit(solution)/shard_map/ppermute | solution.py:278
  57.4 1.6 collective-permute-start.6
  59.1 13.2 %collective-permute-done.11.rest_2_ = bf16[256,1536]{1,0:T(8,128)(2,1)} collective-permute-done((bf16[256,1536]{1,0:T(8,128)(2,1)S(1)}, bf16[256,1536]{1,0:T(8,128)(2,1)}, u32[]{:S(2)}, u32[]{:S(2)}) %collective-permute-start.11) | collective-permute-done | bytes 786464 | tf_op jit(solution)/shard_map/ppermute | solution.py:278
  72.2 4.5 %collective-permute-start.17 = (bf16[256,1024]{1,0:T(8,128)(2,1)S(1)}, bf16[256,1024]{1,0:T(8,128)(2,1)S(1)}, u32[]{:S(2)}, u32[]{:S(2)}) collective-permute-start(bf16[256,1024]{1,0:T(8,128)(2,1)S(1)} %slice.42.rest_0_), channel_id=1, source_target_pairs={{0,8},{24,16},{1,9},{25,17},{2,10},{26,18},{3,11},{27,19},{4,12},{... | collective-permute-start | bytes 1572872 | tf_op jit(solution)/shard_map/ppermute | solution.py:278
  78.6 1.6 collective-permute-start.12
  80.8 4.8 %pack.2 = (bf16[352,1024]{1,0:T(8,128)(2,1)}, bf16[352,1024]{1,0:T(8,128)(2,1)}) custom-call(s32[9]{0:T(128)} %stack.49.scalar_ref, bf16[392,1024]{1,0:T(8,128)(2,1)} %attend.1.rest_0_, bf16[392,1024]{1,0:T(8,128)(2,1)} %copy-done.14), custom_call_target="tpu_custom_call" | custom-call | tf_op jit(solution)/shard_map/pack/pallas_call | solution.py:177
  85.6 4.8 %pack.3 = (bf16[352,1024]{1,0:T(8,128)(2,1)}, bf16[352,1024]{1,0:T(8,128)(2,1)}) custom-call(s32[9]{0:T(128)} %stack.49.scalar_ref, bf16[392,1024]{1,0:T(8,128)(2,1)} %copy-done.13, bf16[392,1024]{1,0:T(8,128)(2,1)} %copy-done.15), custom_call_target="tpu_custom_call" | custom-call | tf_op jit(solution)/shard_map/pack/pallas_call | solution.py:177
  90.4 4.6 %project.6 = bf16[704,1536]{1,0:T(8,128)(2,1)} custom-call(s32[1]{0:T(128)} %bitcast.inner_ref, bf16[352,1024]{1,0:T(8,128)(2,1)} %get-tuple-element.23.own_ref, bf16[352,1024]{1,0:T(8,128)(2,1)} %get-tuple-element.24.other_ref, bf16[256,1536]{1,0:T(8,128)(2,1)} %copy-done.1, bf16[256,1536]{1,0:T(8,128)(2,1)} %collective-permute-done.4.rest_1_, ...), custom_call_target="tpu_custom_call" | custom-call | tf_op jit(solution)/shard_map/project/pallas_call | solution.py:241
  95.7 1.5 collective-permute-start.18
  98.1 4.5 %project.8 = bf16[704,1536]{1,0:T(8,128)(2,1)} custom-call(s32[1]{0:T(128)} %bitcast.inner_ref, bf16[352,1024]{1,0:T(8,128)(2,1)} %get-tuple-element.23.own_ref, bf16[352,1024]{1,0:T(8,128)(2,1)} %get-tuple-element.24.other_ref, bf16[256,1536]{1,0:T(8,128)(2,1)} %copy-done, bf16[256,1536]{1,0:T(8,128)(2,1)} %copy-done.4, ...), custom_call_target="tpu_custom_call" | custom-call | tf_op jit(solution)/shard_map/project/pallas_call | solution.py:241
  104.0 2.9 %project.10 = bf16[704,1024]{1,0:T(8,128)(2,1)} custom-call(s32[1]{0:T(128)} %bitcast.inner_ref, bf16[352,1024]{1,0:T(8,128)(2,1)} %get-tuple-element.23.own_ref, bf16[352,1024]{1,0:T(8,128)(2,1)} %get-tuple-element.24.other_ref, bf16[256,1024]{1,0:T(8,128)(2,1)} %copy-done.2, bf16[256,1024]{1,0:T(8,128)(2,1)} %copy-done.8, bf16[256,1024]{1,0:T(8,128)(2,1)} %copy-done.7, ...), custom_call_target="tpu_custom_call" | custom-call | tf_op jit(solution)/shard_map/project/pallas_call | solution.py:241
  106.9 1.4 copy-done.6
  108.3 5.1 %project.7 = (bf16[352,1536]{1,0:T(8,128)(2,1)}, bf16[352,1536]{1,0:T(8,128)(2,1)}) custom-call(s32[1]{0:T(128)} %bitcast.inner_ref, bf16[352,1024]{1,0:T(8,128)(2,1)} %get-tuple-element.21.own_ref, bf16[352,1024]{1,0:T(8,128)(2,1)} %get-tuple-element.22.other_ref, bf16[256,1536]{1,0:T(8,128)(2,1)} %copy-done.1, ...), custom_call_target="tpu_custom_call" | custom-call | tf_op jit(solution)/shard_map/project/pallas_call | solution.py:241
  115.8 3.4 %project.11 = (bf16[352,1024]{1,0:T(8,128)(2,1)}, bf16[352,1024]{1,0:T(8,128)(2,1)}) custom-call(s32[1]{0:T(128)} %bitcast.inner_ref, bf16[352,1024]{1,0:T(8,128)(2,1)} %get-tuple-element.21.own_ref, bf16[352,1024]{1,0:T(8,128)(2,1)} %get-tuple-element.22.other_ref, bf16[256,1024]{1,0:T(8,128)(2,1)} %copy-done.2, bf16[256,1024]{1,0:T(8,128)(2,1)} %copy-done.8, ...), custom_call_target="tpu_custom_call" | custom-call | tf_op jit(solution)/shard_map/project/pallas_call | solution.py:241
  119.2 1.4 collective-permute-start.20
  122.0 5.1 %project.9 = (bf16[352,1536]{1,0:T(8,128)(2,1)}, bf16[352,1536]{1,0:T(8,128)(2,1)}) custom-call(s32[1]{0:T(128)} %bitcast.inner_ref, bf16[352,1024]{1,0:T(8,128)(2,1)} %get-tuple-element.21.own_ref, bf16[352,1024]{1,0:T(8,128)(2,1)} %get-tuple-element.22.other_ref, bf16[256,1536]{1,0:T(8,128)(2,1)} %copy-done, bf16[256,1536]{1,0:T(8,128)(2,1)} %copy-done.4, ...), custom_call_target="tpu_custom_call" | custom-call | tf_op jit(solution)/shard_map/project/pallas_call | solution.py:241
  128.4 61.3 %collective-permute-done.20 = bf16[352,1024]{1,0:T(8,128)(2,1)S(1)} collective-permute-done((bf16[352,1024]{1,0:T(8,128)(2,1)}, bf16[352,1024]{1,0:T(8,128)(2,1)S(1)}, u32[]{:S(2)}, u32[]{:S(2)}) %collective-permute-start.20) | collective-permute-done | bytes 720928 | tf_op jit(solution)/shard_map/ppermute | solution.py:327
  189.7 1.6 collective-permute-start.21
  192.7 19.9 %collective-permute-done.14 = bf16[352,1536]{1,0:T(8,128)(2,1)S(1)} collective-permute-done((bf16[352,1536]{1,0:T(8,128)(2,1)}, bf16[352,1536]{1,0:T(8,128)(2,1)S(1)}, u32[]{:S(2)}, u32[]{:S(2)}) %collective-permute-start.14) | collective-permute-done | bytes 1081376 | tf_op jit(solution)/shard_map/ppermute | solution.py:327
  212.8 1.6 collective-permute-start.15
  214.7 12.3 %collective-permute-done.15 = bf16[176,1536]{1,0:T(8,128)(2,1)S(1)} collective-permute-done((bf16[176,1536]{1,0:T(8,128)(2,1)S(1)}, bf16[176,1536]{1,0:T(8,128)(2,1)S(1)}, u32[]{:S(2)}, u32[]{:S(2)}) %collective-permute-start.15) | collective-permute-done | bytes 540704 | tf_op jit(solution)/shard_map/ppermute | solution.py:329
  (73 shorter events, 16.4 us)
Async XLA Ops:
  3.8 6.6 %collective-permute-start = (bf16[2,256,128]{2,1,0:T(8,128)(2,1)}, bf16[2,256,128]{2,1,0:T(8,128)(2,1)S(1)}, u32[]{:S(2)}, u32[]{:S(2)}) collective-permute-start(bf16[2,256,128]{2,1,0:T(8,128)(2,1)} %get-tuple-element.20.rest_0_), channel_id=1, source_target_pairs={{0,4},{4,0},{1,5},{5,1},{2,6},{6,2},{3,7},{7,3},{8,12},{12,8},{9,1... | collective-permute-start | bytes 393224 | tf_op jit(solution)/shard_map/ppermute | solution.py:269
  11.1 11.0 %copy-start.9 = (bf16[1,256,4096]{2,1,0:T(8,128)(2,1)S(1)}, bf16[1,256,4096]{2,1,0:T(8,128)(2,1)}, u32[]{:S(2)}) copy-start(bf16[1,256,4096]{2,1,0:T(8,128)(2,1)} %param.15) | copy-start | bytes 6291460
  18.3 22.4 %collective-permute-start.2 = (bf16[392,1024]{1,0:T(8,128)(2,1)}, bf16[392,1024]{1,0:T(8,128)(2,1)S(1)}, u32[]{:S(2)}, u32[]{:S(2)}) collective-permute-start(bf16[392,1024]{1,0:T(8,128)(2,1)} %attend.1.rest_0_), channel_id=1, source_target_pairs={{0,8},{24,16},{1,9},{25,17},{2,10},{26,18},{3,11},{27,19},{4,12},{... | collective-permute-start | bytes 2408456 | tf_op jit(solution)/shard_map/ppermute | solution.py:317
  22.1 4.8 %copy-start.3 = (bf16[392,1024]{1,0:T(8,128)(2,1)S(1)}, bf16[392,1024]{1,0:T(8,128)(2,1)}, u32[]{:S(2)}) copy-start(bf16[392,1024]{1,0:T(8,128)(2,1)} %attend.1.rest_0_) | copy-start | bytes 2408452
  22.3 63.3 %copy-start = (bf16[256,1536]{1,0:T(8,128)(2,1)}, bf16[256,1536]{1,0:T(8,128)(2,1)S(1)}, u32[]{:S(2)}) copy-start(bf16[256,1536]{1,0:T(8,128)(2,1)S(1)} %get-tuple-element.32.rest_0_) | copy-start | bytes 2359300
  22.3 63.3 %copy-start.1 = (bf16[256,1536]{1,0:T(8,128)(2,1)}, bf16[256,1536]{1,0:T(8,128)(2,1)S(1)}, u32[]{:S(2)}) copy-start(bf16[256,1536]{1,0:T(8,128)(2,1)S(1)} %get-tuple-element.31.rest_0_) | copy-start | bytes 2359300
  22.3 35.2 %collective-permute-start.5 = (bf16[256,1536]{1,0:T(8,128)(2,1)S(1)}, bf16[256,1536]{1,0:T(8,128)(2,1)}, u32[]{:S(2)}, u32[]{:S(2)}) collective-permute-start(bf16[256,1536]{1,0:T(8,128)(2,1)S(1)} %get-tuple-element.31.rest_0_), channel_id=1, source_target_pairs={{0,8},{24,16},{1,9},{25,17},{2,10},{26,18},{3,11},{27,19},{4,12},{... | collective-permute-start | bytes 2359304 | tf_op jit(solution)/shard_map/ppermute | solution.py:278
  24.6 47.6 %collective-permute-start.11 = (bf16[256,1536]{1,0:T(8,128)(2,1)S(1)}, bf16[256,1536]{1,0:T(8,128)(2,1)}, u32[]{:S(2)}, u32[]{:S(2)}) collective-permute-start(bf16[256,1536]{1,0:T(8,128)(2,1)S(1)} %get-tuple-element.32.rest_0_), channel_id=1, source_target_pairs={{0,8},{24,16},{1,9},{25,17},{2,10},{26,18},{3,11},{27,19},{4,12},{... | collective-permute-start | bytes 2359304 | tf_op jit(solution)/shard_map/ppermute | solution.py:278
  26.9 49.9 %collective-permute-start.1 = (bf16[392,1024]{1,0:T(8,128)(2,1)S(1)}, bf16[392,1024]{1,0:T(8,128)(2,1)S(1)}, u32[]{:S(2)}, u32[]{:S(2)}) collective-permute-start(bf16[392,1024]{1,0:T(8,128)(2,1)S(1)} %copy-done.3), channel_id=1, source_target_pairs={{0,4},{4,0},{1,5},{5,1},{2,6},{6,2},{3,7},{7,3},{8,12},{12,8},{9,1... | collective-permute-start | bytes 2408456 | tf_op jit(solution)/shard_map/ppermute | solution.py:269
  40.7 36.1 %copy-start.13 = (bf16[392,1024]{1,0:T(8,128)(2,1)}, bf16[392,1024]{1,0:T(8,128)(2,1)S(1)}, u32[]{:S(2)}) copy-start(bf16[392,1024]{1,0:T(8,128)(2,1)S(1)} %collective-permute-done.2.rest_0_) | copy-start | bytes 2408452
  40.7 36.8 %collective-permute-start.3 = (bf16[392,1024]{1,0:T(8,128)(2,1)S(1)}, bf16[392,1024]{1,0:T(8,128)(2,1)S(1)}, u32[]{:S(2)}, u32[]{:S(2)}) collective-permute-start(bf16[392,1024]{1,0:T(8,128)(2,1)S(1)} %collective-permute-done.2.rest_0_), channel_id=1, source_target_pairs={{0,4},{4,0},{1,5},{5,1},{2,6},{6,2},{3,7},{7,3},{8,12},{12,8},{9,1... | collective-permute-start | bytes 2408456 | tf_op jit(solution)/shard_map/ppermute | solution.py:269
  42.2 48.2 %collective-permute-start.4 = (bf16[256,1536]{1,0:T(8,128)(2,1)S(1)}, bf16[256,1536]{1,0:T(8,128)(2,1)}, u32[]{:S(2)}, u32[]{:S(2)}) collective-permute-start(bf16[256,1536]{1,0:T(8,128)(2,1)S(1)} %get-tuple-element.31.rest_0_), channel_id=1, source_target_pairs={{8,16},{16,8},{9,17},{17,9},{10,18},{18,10},{11,19},{19,11},{12,20... | collective-permute-start | bytes 2359304 | tf_op jit(solution)/shard_map/ppermute | solution.py:277
  57.4 32.9 %collective-permute-start.6 = (bf16[256,1536]{1,0:T(8,128)(2,1)}, bf16[256,1536]{1,0:T(8,128)(2,1)}, u32[]{:S(2)}, u32[]{:S(2)}) collective-permute-start(bf16[256,1536]{1,0:T(8,128)(2,1)} %collective-permute-done.5.rest_2_), channel_id=1, source_target_pairs={{8,16},{16,8},{9,17},{17,9},{10,18},{18,10},{11,19},{19,11},{12,20... | collective-permute-start | bytes 2359304 | tf_op jit(solution)/shard_map/ppermute | solution.py:279
  59.1 35.9 %copy-start.2 = (bf16[256,1024]{1,0:T(8,128)(2,1)}, bf16[256,1024]{1,0:T(8,128)(2,1)S(1)}, u32[]{:S(2)}) copy-start(bf16[256,1024]{1,0:T(8,128)(2,1)S(1)} %slice.42.rest_0_) | copy-start | bytes 1572868
  72.2 23.5 %collective-permute-start.17 = (bf16[256,1024]{1,0:T(8,128)(2,1)S(1)}, bf16[256,1024]{1,0:T(8,128)(2,1)S(1)}, u32[]{:S(2)}, u32[]{:S(2)}) collective-permute-start(bf16[256,1024]{1,0:T(8,128)(2,1)S(1)} %slice.42.rest_0_), channel_id=1, source_target_pairs={{0,8},{24,16},{1,9},{25,17},{2,10},{26,18},{3,11},{27,19},{4,12},{... | collective-permute-start | bytes 1572872 | tf_op jit(solution)/shard_map/ppermute | solution.py:278
  76.8 20.4 %collective-permute-start.10 = (bf16[256,1536]{1,0:T(8,128)(2,1)S(1)}, bf16[256,1536]{1,0:T(8,128)(2,1)S(1)}, u32[]{:S(2)}, u32[]{:S(2)}) collective-permute-start(bf16[256,1536]{1,0:T(8,128)(2,1)S(1)} %get-tuple-element.32.rest_0_), channel_id=1, source_target_pairs={{8,16},{16,8},{9,17},{17,9},{10,18},{18,10},{11,19},{19,11},{12,20... | collective-permute-start | bytes 2359304 | tf_op jit(solution)/shard_map/ppermute | solution.py:277
  78.6 18.6 %collective-permute-start.12 = (bf16[256,1536]{1,0:T(8,128)(2,1)}, bf16[256,1536]{1,0:T(8,128)(2,1)}, u32[]{:S(2)}, u32[]{:S(2)}) collective-permute-start(bf16[256,1536]{1,0:T(8,128)(2,1)} %collective-permute-done.11.rest_2_), channel_id=1, source_target_pairs={{8,16},{16,8},{9,17},{17,9},{10,18},{18,10},{11,19},{19,11},{12,20... | collective-permute-start | bytes 2359304 | tf_op jit(solution)/shard_map/ppermute | solution.py:279
  95.0 11.9 %collective-permute-start.7 = (bf16[704,1536]{1,0:T(8,128)(2,1)}, bf16[704,1536]{1,0:T(8,128)(2,1)S(1)}, u32[]{:S(2)}, u32[]{:S(2)}) collective-permute-start(bf16[704,1536]{1,0:T(8,128)(2,1)} %project.6), channel_id=1, source_target_pairs={{0,1},{1,0},{2,3},{3,2},{4,5},{5,4},{6,7},{7,6},{8,9},{9,8},{10,11... | collective-permute-start | bytes 6488072 | tf_op jit(solution)/shard_map/ppermute | solution.py:325
  95.0 8.2 %collective-permute-start.16 = (bf16[256,1024]{1,0:T(8,128)(2,1)S(1)}, bf16[256,1024]{1,0:T(8,128)(2,1)S(1)}, u32[]{:S(2)}, u32[]{:S(2)}) collective-permute-start(bf16[256,1024]{1,0:T(8,128)(2,1)S(1)} %slice.42.rest_0_), channel_id=1, source_target_pairs={{8,16},{16,8},{9,17},{17,9},{10,18},{18,10},{11,19},{19,11},{12,20... | collective-permute-start | bytes 1572872 | tf_op jit(solution)/shard_map/ppermute | solution.py:277
  95.7 7.0 %copy-start.7 = (bf16[256,1024]{1,0:T(8,128)(2,1)}, bf16[256,1024]{1,0:T(8,128)(2,1)S(1)}, u32[]{:S(2)}) copy-start(bf16[256,1024]{1,0:T(8,128)(2,1)S(1)} %collective-permute-done.17.rest_2_) | copy-start | bytes 1572868
  95.7 7.5 %collective-permute-start.18 = (bf16[256,1024]{1,0:T(8,128)(2,1)S(1)}, bf16[256,1024]{1,0:T(8,128)(2,1)}, u32[]{:S(2)}, u32[]{:S(2)}) collective-permute-start(bf16[256,1024]{1,0:T(8,128)(2,1)S(1)} %collective-permute-done.17.rest_2_), channel_id=1, source_target_pairs={{8,16},{16,8},{9,17},{17,9},{10,18},{18,10},{11,19},{19,11},{12,20... | collective-permute-start | bytes 1572872 | tf_op jit(solution)/shard_map/ppermute | solution.py:279
  102.7 17.9 %collective-permute-start.13 = (bf16[704,1536]{1,0:T(8,128)(2,1)}, bf16[704,1536]{1,0:T(8,128)(2,1)S(1)}, u32[]{:S(2)}, u32[]{:S(2)}) collective-permute-start(bf16[704,1536]{1,0:T(8,128)(2,1)} %project.8), channel_id=1, source_target_pairs={{0,1},{1,0},{2,3},{3,2},{4,5},{5,4},{6,7},{7,6},{8,9},{9,8},{10,11... | collective-permute-start | bytes 6488072 | tf_op jit(solution)/shard_map/ppermute | solution.py:325
  106.9 7.8 %collective-permute-start.19 = (bf16[704,1024]{1,0:T(8,128)(2,1)}, bf16[704,1024]{1,0:T(8,128)(2,1)S(1)}, u32[]{:S(2)}, u32[]{:S(2)}) collective-permute-start(bf16[704,1024]{1,0:T(8,128)(2,1)} %project.10), channel_id=1, source_target_pairs={{0,1},{1,0},{2,3},{3,2},{4,5},{5,4},{6,7},{7,6},{8,9},{9,8},{10,11... | collective-permute-start | bytes 4325384 | tf_op jit(solution)/shard_map/ppermute | solution.py:325
  113.4 78.0 %collective-permute-start.8 = (bf16[352,1536]{1,0:T(8,128)(2,1)}, bf16[352,1536]{1,0:T(8,128)(2,1)S(1)}, u32[]{:S(2)}, u32[]{:S(2)}) collective-permute-start(bf16[352,1536]{1,0:T(8,128)(2,1)} %get-tuple-element.26), channel_id=1, source_target_pairs={{8,0},{16,24},{9,1},{17,25},{10,2},{18,26},{11,3},{19,27},{12,4},{... | collective-permute-start | bytes 3244040 | tf_op jit(solution)/shard_map/ppermute | solution.py:327
  119.1 70.5 %copy-start.16 = (bf16[352,1024]{1,0:T(8,128)(2,1)S(1)}, bf16[352,1024]{1,0:T(8,128)(2,1)}, u32[]{:S(2)}) copy-start(bf16[352,1024]{1,0:T(8,128)(2,1)} %get-tuple-element.29) | copy-start | bytes 2162692
  119.2 70.5 %collective-permute-start.20 = (bf16[352,1024]{1,0:T(8,128)(2,1)}, bf16[352,1024]{1,0:T(8,128)(2,1)S(1)}, u32[]{:S(2)}, u32[]{:S(2)}) collective-permute-start(bf16[352,1024]{1,0:T(8,128)(2,1)} %get-tuple-element.30), channel_id=1, source_target_pairs={{8,0},{16,24},{9,1},{17,25},{10,2},{18,26},{11,3},{19,27},{12,4},{... | collective-permute-start | bytes 2162696 | tf_op jit(solution)/shard_map/ppermute | solution.py:327
  127.1 85.5 %collective-permute-start.14 = (bf16[352,1536]{1,0:T(8,128)(2,1)}, bf16[352,1536]{1,0:T(8,128)(2,1)S(1)}, u32[]{:S(2)}, u32[]{:S(2)}) collective-permute-start(bf16[352,1536]{1,0:T(8,128)(2,1)} %get-tuple-element.28), channel_id=1, source_target_pairs={{8,0},{16,24},{9,1},{17,25},{10,2},{18,26},{11,3},{19,27},{12,4},{... | collective-permute-start | bytes 3244040 | tf_op jit(solution)/shard_map/ppermute | solution.py:327
  189.6 1.7 copy-start.11
  189.7 24.6 %collective-permute-start.21 = (bf16[176,1024]{1,0:T(8,128)(2,1)S(1)}, bf16[176,1024]{1,0:T(8,128)(2,1)S(1)}, u32[]{:S(2)}, u32[]{:S(2)}) collective-permute-start(bf16[176,1024]{1,0:T(8,128)(2,1)S(1)} %slice.44), channel_id=1, source_target_pairs={{0,2},{1,3},{2,0},{3,1},{4,6},{5,7},{6,4},{7,5},{8,10},{9,11},{10,... | collective-permute-start | bytes 1081352 | tf_op jit(solution)/shard_map/ppermute | solution.py:329
  191.5 21.1 %copy-start.12 = (bf16[352,1536]{1,0:T(8,128)(2,1)S(1)}, bf16[352,1536]{1,0:T(8,128)(2,1)}, u32[]{:S(2)}) copy-start(bf16[352,1536]{1,0:T(8,128)(2,1)} %get-tuple-element.27) | copy-start | bytes 3244036
  191.6 23.0 %collective-permute-start.9 = (bf16[176,1536]{1,0:T(8,128)(2,1)S(1)}, bf16[176,1536]{1,0:T(8,128)(2,1)S(1)}, u32[]{:S(2)}, u32[]{:S(2)}) collective-permute-start(bf16[176,1536]{1,0:T(8,128)(2,1)S(1)} %slice.38), channel_id=1, source_target_pairs={{0,2},{1,3},{2,0},{3,1},{4,6},{5,7},{6,4},{7,5},{8,10},{9,11},{10,... | collective-permute-start | bytes 1622024 | tf_op jit(solution)/shard_map/ppermute | solution.py:329
  212.8 14.2 %collective-permute-start.15 = (bf16[176,1536]{1,0:T(8,128)(2,1)S(1)}, bf16[176,1536]{1,0:T(8,128)(2,1)S(1)}, u32[]{:S(2)}, u32[]{:S(2)}) collective-permute-start(bf16[176,1536]{1,0:T(8,128)(2,1)S(1)} %slice.41), channel_id=1, source_target_pairs={{0,2},{1,3},{2,0},{3,1},{4,6},{5,7},{6,4},{7,5},{8,10},{9,11},{10,... | collective-permute-start | bytes 1622024 | tf_op jit(solution)/shard_map/ppermute | solution.py:329
  (8 other events, 8.1 us)

commit v2 on v1

v2 whole, which is shorter than its diff:
```python
import functools
import math

import jax
import jax.numpy as jnp
from jax import lax
from jax.experimental import pallas as pl
from jax.experimental.pallas import tpu as pltpu
from jax.sharding import PartitionSpec as P

NEGATIVE_FILL = -1e30
ROPE_BASE = 500000.0
COUNT_ROWS = 8
FIRST_ROW, BASE, LIVE, CTX, HALVES, PLANE = 0, 1, 3, 4, 5, 7
VMEM_LIMIT = 56 * 1024 * 1024
SMALL_LIMIT = 12 * 1024 * 1024
OUT_TO_IN = [(0, 1), (3, 2)]
IN_TO_OUT = [(1, 0), (2, 3)]
INNER = [(1, 2), (2, 1)]
CORE = [(i, i ^ 1) for i in range(4)]
CROSS = [(i, i ^ 2) for i in range(4)]

SMEM_SPEC = pl.BlockSpec(memory_space=pltpu.SMEM)


def params(rows=0):
    limit = VMEM_LIMIT if rows > 512 else SMALL_LIMIT
    return pltpu.CompilerParams(vmem_limit_bytes=limit)


def send(x, axis, pairs, name):
    with jax.named_scope(name):
        return lax.ppermute(x, axis, pairs)


def after(value, *done):
    return lax.optimization_barrier((value, *done))[0]


def half_turn(x, half):
    return jnp.concatenate([x[:, half:], x[:, :half]], axis=1)


def prepare_kernel(n_blocks, base_ref, doc_ref, rescale_ref, *tables):
    slots = doc_ref.shape[1]
    head = rescale_ref.shape[1]
    half = head // 2
    lane = lax.broadcasted_iota(jnp.int32, (1, head), 1)
    frequency = jnp.where(lane < half, lane, lane - half).astype(jnp.float32)
    inverse = jnp.exp(-(frequency * (2.0 / head)) * math.log(ROPE_BASE)) / rescale_ref[...]
    sign = jnp.where(lane < half, -1.0, 1.0)
    docs = jnp.broadcast_to(doc_ref[...].astype(jnp.float32), (slots, slots))
    first = jnp.sum(jnp.where(docs < docs.T, 1.0, 0.0), axis=1, keepdims=True)
    slot = lax.broadcasted_iota(jnp.int32, (slots, 1), 0).astype(jnp.float32)
    for i in range(n_blocks + 1):
        cos_ref, sin_ref = tables[2 * i], tables[2 * i + 1]
        if i == n_blocks:
            position = slot - first
        else:
            rows = lax.broadcasted_iota(jnp.int32, (cos_ref.shape[0], 1), 0)
            position = (rows + base_ref[BASE + i]).astype(jnp.float32)
        angles = position * inverse
        cos_ref[...] = jnp.cos(angles)
        sin_ref[...] = jnp.sin(angles) * sign


def prepare(bases, block_rows, doc, rescale):
    vmem = pl.BlockSpec(memory_space=pltpu.VMEM)
    shapes = [
        jax.ShapeDtypeStruct((rows, rescale.shape[1]), jnp.float32)
        for rows in [*block_rows, doc.shape[1]]
        for _ in range(2)
    ]
    return pl.pallas_call(
        functools.partial(prepare_kernel, len(block_rows)),
        in_specs=[SMEM_SPEC, vmem, vmem],
        out_specs=[vmem] * len(shapes),
        out_shape=shapes,
        compiler_params=params(),
        name="prepare",
    )(bases, doc, rescale)


def weigh(scores, visible, values, scale):
    scores = [jnp.where(v, s, NEGATIVE_FILL) for s, v in zip(scores, visible)]
    peak = functools.reduce(jnp.maximum, [jnp.max(s, axis=1, keepdims=True) for s in scores])
    total, weighted = 0.0, 0.0
    for s, value in zip(scores, values):
        weights = jnp.exp2((s - peak) * (scale * math.log2(math.e)))
        total = total + jnp.sum(weights, axis=1, keepdims=True)
        weighted = weighted + jnp.dot(
            weights.astype(jnp.bfloat16), value, preferred_element_type=jnp.float32
        )
    return (weighted / total).astype(jnp.bfloat16)


def dot_t(a, b):
    return lax.dot_general(a, b, (((1,), (1,)), ((), ())), preferred_element_type=jnp.float32)


def turn(x, cosine, sine):
    x = x.astype(jnp.float32)
    return (x * cosine + half_turn(x, x.shape[1] // 2) * sine).astype(jnp.bfloat16)


def attend_kernel(n_blocks, n_tables, scalar_ref, ql_ref, qs_ref, skv_ref, doc_ref, *rest):
    tables, rest = rest[:n_tables], rest[n_tables:]
    pairs, rest = rest[:n_blocks], rest[n_blocks:]
    out_ref = rest[-1]
    long_rows, slots = ql_ref.shape[0], qs_ref.shape[0]
    head = skv_ref.shape[2]
    scale = 1.0 / math.sqrt(head)
    heads = ql_ref.shape[1] // head
    if n_tables == 2 * n_blocks + 2:
        own_table = (tables[0][...], tables[1][...])
    else:
        own_table = (tables[-4][...], tables[-3][...])
    slab_table = (tables[-2][...], tables[-1][...])
    keys = [turn(p[0], tables[2 * i][...], tables[2 * i + 1][...]) for i, p in enumerate(pairs)]
    values = [p[1] for p in pairs]
    row = lax.broadcasted_iota(jnp.int32, (long_rows, 1), 0) + scalar_ref[FIRST_ROW]
    visible = [
        lax.broadcasted_iota(jnp.int32, (long_rows, p.shape[1]), 1) + scalar_ref[BASE + i] <= row
        for i, p in enumerate(pairs)
    ]
    short_keys = turn(skv_ref[0], *slab_table)
    docs = jnp.broadcast_to(doc_ref[...].astype(jnp.float32), (slots, slots))
    below = lax.broadcasted_iota(jnp.int32, (slots, slots), 1) <= lax.broadcasted_iota(
        jnp.int32, (slots, slots), 0
    )
    short_visible = [(docs == docs.T) & below]
    short_values = [skv_ref[1]]
    for h in range(heads):
        columns = slice(h * head, (h + 1) * head)
        query = turn(ql_ref[:, columns], *own_table)
        scores = [dot_t(query, k) for k in keys]
        out_ref[:long_rows, columns] = weigh(scores, visible, values, scale)
        query = turn(qs_ref[:, columns], *slab_table)
        out_ref[long_rows : long_rows + slots, columns] = weigh(
            [dot_t(query, short_keys)], short_visible, short_values, scale
        )
    live = jnp.full((COUNT_ROWS, out_ref.shape[1]), scalar_ref[LIVE], jnp.int32)
    out_ref[long_rows + slots :, :] = live.astype(jnp.float32).astype(jnp.bfloat16)


def attend(scalars, q_long, q_short, short_kv, doc, tables, pairs):
    rows = q_long.shape[0] + q_short.shape[0] + COUNT_ROWS
    vmem = pl.BlockSpec(memory_space=pltpu.VMEM)
    return pl.pallas_call(
        functools.partial(attend_kernel, len(pairs), len(tables)),
        in_specs=[SMEM_SPEC] + [vmem] * (4 + len(tables) + len(pairs)),
        out_specs=vmem,
        out_shape=jax.ShapeDtypeStruct((rows, q_long.shape[1]), jnp.bfloat16),
        compiler_params=params(sum(p.shape[1] for p in pairs)),
        name="attend",
    )(scalars, q_long, q_short, short_kv, doc, *tables, *pairs)


def pack_kernel(long_rows, slots, group_rows, n_pieces, scalar_ref, *rest):
    pieces, (out_ref, dense) = rest[:-2], rest[-2:]
    piece_rows = long_rows + slots

    def live_of(piece, first):
        tail = piece[pl.ds(first + piece_rows, COUNT_ROWS), :]
        return jnp.max(tail.astype(jnp.float32)).astype(jnp.int32)

    def put(piece, first, offset):
        rows = piece[pl.ds(first, piece_rows), :].astype(jnp.float32)
        dense[pl.ds(pl.multiple_of(offset, 8), piece_rows), :] = rows
        return offset + long_rows + live_of(piece, first)

    if len(pieces) == 1:
        offset = jnp.int32(0)
        for i in range(n_pieces):
            offset = put(pieces[0], i * (piece_rows + COUNT_ROWS), offset)
    else:
        mine, theirs = pieces

        @pl.when(scalar_ref[CTX] == 0)
        def _():
            put(theirs, 0, put(mine, 0, jnp.int32(0)))

        @pl.when(scalar_ref[CTX] != 0)
        def _():
            put(mine, 0, put(theirs, 0, jnp.int32(0)))

    half = group_rows // 2
    for s in range(2):
        start = pl.multiple_of(scalar_ref[HALVES + s] * half, 8)
        out_ref[s * half : (s + 1) * half, :] = dense[pl.ds(start, half), :].astype(jnp.bfloat16)


def pack(place, pieces, long_rows, slots, n_pieces):
    group_rows = n_pieces * (long_rows + 3 * slots // 4)
    columns = pieces[0].shape[1]
    block = min(columns, 512 if n_pieces == 2 else 256)
    return pl.pallas_call(
        functools.partial(pack_kernel, long_rows, slots, group_rows, n_pieces),
        grid_spec=pltpu.PrefetchScalarGridSpec(
            num_scalar_prefetch=1,
            grid=(columns // block,),
            in_specs=[pl.BlockSpec((p.shape[0], block), lambda j, s: (0, j)) for p in pieces],
            out_specs=pl.BlockSpec((group_rows, block), lambda j, s: (0, j)),
            scratch_shapes=[pltpu.VMEM((group_rows + long_rows + slots, block), jnp.float32)],
        ),
        out_shape=jax.ShapeDtypeStruct((group_rows, columns), jnp.bfloat16),
        compiler_params=params(group_rows // 2),
        name="pack",
    )(place, *pieces)


def project_kernel(at, width, straight, plane_ref, *refs):
    rows, weights, outs = refs[:4], refs[4:8], refs[8:]
    depth = weights[0].shape[0] // 2
    half = rows[0].shape[0] // 2

    def block(i, part, a, b):
        here = slice(part * depth, (part + 1) * depth)
        return weights[i][here, a:b] if i == 3 else weights[i][here, at + a : at + b]

    for plane, order in ((1, (2, 0, 1, 3)), (2, (3, 1, 0, 2))):

        @pl.when(plane_ref[PLANE] == plane)
        def _(order=order):
            for first in range(0, width, 512):
                last = min(width, first + 512)
                for bounds in ((first, min(last, straight)), (max(first, straight), last)):
                    a, b = bounds
                    if a >= b:
                        continue
                    weight = jnp.concatenate(
                        [block(i, part, a, b) for part in range(2) for i in order], axis=0
                    )
                    for group in range(2):
                        left = jnp.concatenate([rows[2 * group][...], rows[2 * group + 1][...]], axis=1)
                        total = jnp.dot(left, weight, preferred_element_type=jnp.float32)
                        total = total.astype(jnp.bfloat16)
                        if b <= straight:
                            outs[group][:, a:b] = total
                        else:
                            here = slice(a - straight, b - straight)
                            there = slice(group * half, (group + 1) * half)
                            outs[-2][there, here] = total[:half]
                            outs[-1][there, here] = total[half:]

    @pl.when((plane_ref[PLANE] != 1) & (plane_ref[PLANE] != 2))
    def _():
        for out in outs:
            out[...] = jnp.zeros(out.shape, jnp.bfloat16)


def project(plane, rows, weights, at, width, straight):
    count = rows[0].shape[0]
    vmem = pl.BlockSpec(memory_space=pltpu.VMEM)
    shapes = [jax.ShapeDtypeStruct((count, w), jnp.bfloat16) for w in (straight, width - straight) if w for _ in range(2)]
    grid, row_spec, out_spec = (), vmem, vmem
    if count > 1024 and width == straight:
        block = count // 8
        grid = (8,)
        row_spec = pl.BlockSpec((block, rows[0].shape[1]), lambda i: (i, 0))
        out_spec = pl.BlockSpec((block, width), lambda i: (i, 0))
    return pl.pallas_call(
        functools.partial(project_kernel, at, width, straight),
        grid=grid,
        in_specs=[SMEM_SPEC] + [row_spec] * 4 + [vmem] * len(weights),
        out_specs=[out_spec] * len(shapes),
        out_shape=shapes,
        compiler_params=params(count // 2),
        name="project",
    )(plane, *rows, *weights)


def column_chunks(columns):
    unit = columns // 16
    if unit % 128:
        return [columns], [columns]
    return [7 * unit, 5 * unit, 4 * unit], [4 * unit, 2 * unit, 2 * unit]


def local(
    q_long, long_key_value, q_short, short_key_value, doc_ids, live_counts, rescale, output_weight
):
    head = rescale.shape[0] * 2
    long_rows, slots = q_long.shape[1], q_short.shape[1]
    ctx, tp, dp = lax.axis_index("ctx"), lax.axis_index("tp"), lax.axis_index("dp")
    n_ctx = lax.axis_size("ctx")
    own_base = ctx * long_rows
    bases = [own_base, (1 - ctx) * long_rows] if n_ctx == 2 else [jnp.int32(0), own_base]
    place = jnp.stack(
        [own_base, *bases, live_counts[0], ctx, 1 - (tp >> 1), tp >> 1, dp]
    ).astype(jnp.int32)
    weight = output_weight[0]
    width = weight.shape[1] // 2
    place, is_inner, is_left, keep_at, give_at, weight, doubled = lax.optimization_barrier(
        (
            place,
            (dp == 1) | (dp == 2),
            (tp & 1) == 0,
            (tp & 1) * width,
            (1 - (tp & 1)) * width,
            weight,
            jnp.concatenate([rescale, rescale]).reshape(1, head),
        )
    )

    def swap_ctx(x, name):
        return send(x, "ctx", [(0, 1), (1, 0)], name)

    widths, straight = column_chunks(width)
    n = len(widths)
    given = lax.dynamic_slice_in_dim(weight, give_at, width, 1)
    kept = lax.dynamic_slice_in_dim(weight, keep_at, width, 1)

    def trade(a, b, name):
        theirs = send(given[:, a:b], "tp", CORE, name)
        return jnp.concatenate([kept[:, a:b], theirs], axis=0)

    near, far = {}, {}
    both = [trade(0, widths[0], "trade0")]
    near[0] = send(both[0], "dp", OUT_TO_IN, "near0")
    twin = [send(both[0], "dp", INNER, "twin0")]
    if n > 1:
        both.append(trade(widths[0], width, "trade1"))

    def forward(i, source):
        far[i] = send(source, "dp", INNER, f"far{i}")

    raw = long_key_value[0]
    if n_ctx == 2:
        pairs = [raw, swap_ctx(raw, "keys")]
        block_rows = [long_rows, long_rows]
    else:
        pairs = [lax.all_gather(raw, "ctx", axis=1, tiled=True)]
        block_rows = [n_ctx * long_rows, long_rows]
    tables = prepare(place, block_rows, doc_ids, doubled)
    inputs = (place, q_long[0], q_short[0], short_key_value[0], doc_ids, tables, pairs)
    if n > 1:
        inputs = (after(place, both[1]), *inputs[1:])
    rows = attend(*inputs)
    forward(0, after(near[0], rows))
    rows = after(rows, near[0], twin[0])

    def gathered(x, name):
        if n_ctx == 2:
            return [x, swap_ctx(x, name)]
        return [lax.all_gather(x, "ctx", axis=0, tiled=True)]

    handed = send(rows, "dp", OUT_TO_IN, "hand")
    pieces = gathered(rows, "rows")
    other_pieces = gathered(handed, "other")
    if n > 1:
        rest = after(both[1], handed, far[0])
        twin.append(send(rest, "dp", INNER, "twin1"))
        near[1] = send(rest, "dp", OUT_TO_IN, "near1")
    pieces[-1] = after(pieces[-1], handed, far[0])
    own = pack(place, pieces, long_rows, slots, n_ctx)
    own_theirs = send(own, "tp", CORE, "own_rows")
    if n > 1:
        other_pieces[-1] = after(other_pieces[-1], near[1], own_theirs, twin[1])
        at = 0
        for i in range(1, n):
            forward(i, near[1][:, at : at + widths[i]])
            at += widths[i]
    other = pack(place, other_pieces, long_rows, slots, n_ctx)
    other_theirs = send(other, "tp", CORE, "other_rows")
    group = (own, own_theirs, other, other_theirs)

    def add(a, b):
        return (a.astype(jnp.float32) + b.astype(jnp.float32)).astype(jnp.bfloat16)

    def first_hop(i):
        part = min(i, 1)
        at = sum(widths[1:i])
        weights = (both[part], twin[part], near[part], far[i])
        outs = project(place, group, weights, at, widths[i], straight[i])
        hop = {}
        if straight[i]:
            hop["mine"], other_part = outs[0], outs[1]
            hop["returned"] = send(other_part, "dp", IN_TO_OUT, f"return{i}")
        if straight[i] < widths[i]:
            hop["kept"] = outs[-1]
            hop["crossed"] = send(outs[-2], "tp", CROSS, f"cross{i}")
        return hop, outs[0]

    def second_hop(i, hop, *gates):
        done = {}
        if "returned" in hop:
            summed = jnp.where(is_inner, hop["mine"], after(hop["returned"], *gates))
            done["kept"] = summed[half:]
            done["crossed"] = send(summed[:half], "tp", CROSS, f"cross_after{i}")
        if "crossed" in hop:
            summed = add(hop["kept"], after(hop["crossed"], *gates))
            done["mine"] = summed[:half]
            done["returned"] = send(summed[half:], "dp", IN_TO_OUT, f"return_after{i}")
        return done

    def finish(done):
        parts = []
        if "crossed" in done:
            parts.append(add(done["kept"], done["crossed"]))
        if "returned" in done:
            parts.append(jnp.where(is_inner, done["mine"], done["returned"]))
        return parts

    half = own.shape[0] // 2
    hops, seconds = [], []
    for i in range(n):
        if i:
            far[i] = after(far[i], gate)
        hop, gate = first_hop(i)
        hops.append(hop)
        if i:
            seconds.append(second_hop(i - 1, hops[i - 1], gate))
    gates = list(seconds[-1].values()) if seconds else []
    seconds.append(second_hop(n - 1, hops[-1], *gates))
    quarter = half // 2
    mine, theirs = [], []
    for i, done in enumerate(seconds):
        x = jnp.concatenate(finish(done), axis=1)
        mine.append(jnp.where(is_left, x[:quarter], x[quarter:]))
        theirs.append(
            send(jnp.where(is_left, x[quarter:], x[:quarter]), "tp", CORE, f"rest{i}")
        )
    mine, theirs = jnp.concatenate(mine, axis=1), jnp.concatenate(theirs, axis=1)
    left = jnp.where(is_left, mine, theirs)
    right = jnp.where(is_left, theirs, mine)
    return jnp.concatenate([left, right], axis=1)[None]


def solution(mesh):
    in_specs = (
        P("dp", "ctx", "tp"),
        P("dp", None, "ctx", "tp"),
        P(("dp", "ctx"), None, "tp"),
        P(("dp", "ctx"), None, None, "tp"),
        P(("dp", "ctx"), None),
        P(("dp", "ctx")),
        P(),
        P("tp", "dp", "ctx"),
    )
    out_specs = P("dp", "tp", "ctx")
    return jax.shard_map(local, mesh=mesh, in_specs=in_specs, out_specs=out_specs, check_vma=False)
```

time: 229 us -> 176 us (0.77)
  Pallas kernels: 44.9 us -> 12.5 us
  waiting for transfers between devices: 135 us -> 113 us
  starting transfers between devices: 35.3 us -> 41.7 us
  local copies, waits for them, and re-layouts: 8.2 us -> 3.32 us
    pallas_call x8 -> x5, Pallas kernels: 35.3 us -> 9.68 us  [the longest x1 5.33 us: attend(): pl.pallas_call(functools.partial(attend_kernel, len(pairs), len(tables)),...]
    ppermute x22 -> x30, waiting for transfers between devices: 135 us -> 113 us  [send(): return lax.ppermute(x, axis, pairs)]
    unnamed x36 -> x14, local copies, waits for them, and re-layouts: 7.34 us -> 0.1 us
    pallas_call x2, Pallas kernels: 9.57 us -> 2.84 us  [pack(): pl.pallas_call(functools.partial(pack_kernel, long_rows, slots, group_row...]
    ppermute x22 -> x30, starting transfers between devices: 35.3 us -> 41.7 us  [send(): return lax.ppermute(x, axis, pairs)]
    slice x5 -> x10, local copies, waits for them, and re-layouts: 0.26 us -> 3.12 us  [the longest x2 2.9 us: trade(): return jnp.concatenate([kept[:, a:b], theirs], axis=0)]
  transfers between devices with their start and end apart: 22 -> 30, of which waited for: 7 -> 15; matrix products, arithmetic and copies ran while one was open for 1% -> 1% of each run, Pallas kernels for 15% -> 6%
where the time goes in v2:
time: 176 us; the launch traced here: 175 us
  waiting for transfers between devices  113 us (64%)
  starting transfers between devices  41.7 us (24%)
  Pallas kernels  12.5 us (7%)
  other arithmetic  3.6 us (2%)
  local copies, waits for them, and re-layouts  3.32 us (2%)
    ppermute x30, waiting for transfers between devices, send(): return lax.ppermute(x, axis, pairs)  113 us
    ppermute x30, starting transfers between devices, send(): return lax.ppermute(x, axis, pairs)  41.7 us
    pallas_call x1, Pallas kernels, attend(): pl.pallas_call(functools.partial(attend_kernel, len(pairs), len(tables)),...  5.33 us
  transfers between devices with their start and end apart: 30, of which 15 were waited for; matrix products, arithmetic and copies ran while one was open for 1% of the time, Pallas kernels for 6%

profile of v2, /device:TPU:0, one launch (start us, length us, event | category | flops | bytes accessed | tf_op | source)
XLA Modules:
  0.0 175.2 jit_solution(11802035988080952417)
XLA Ops:
  1.6 2.0 %constant_dynamic-slice_fusion.3 = (bf16[256,896]{1,0:T(8,128)(2,1)S(1)}, bf16[256,896]{1,0:T(8,128)(2,1)S(1)}) fusion(bf16[256,4096]{1,0:T(8,128)(2,1)} %bitcast.20, s32[]{:T(128)S(6)} %select_n.97, s32[]{:T(128)S(6)} %select_n.98), kind=kLoop, calls=%fused_computation.42 | loop fusion | bytes 1835016 | tf_op jit(solution)/shard_map/slice | solution.py:316
  4.1 1.4 collective-permute-done.2
  5.6 5.0 %collective-permute-start.3 = (bf16[512,896]{1,0:T(8,128)(2,1)S(1)}, bf16[512,896]{1,0:T(8,128)(2,1)S(1)}, u32[]{:S(2)}, u32[]{:S(2)}) collective-permute-start(bf16[512,896]{1,0:T(8,128)(2,1)S(1)} %pad_maximum_fusion.1.refs_4_), channel_id=1, source_target_pairs={{0,8},{24,16},{1,9},{25,17},{2,10},{26,18},{3,11},{27,19},{4,12},{... | collective-permute-start | bytes 2752520 | tf_op jit(solution)/shard_map/near0/ppermute | solution.py:33
  12.6 1.6 collective-permute-start.1
  14.1 1.8 %prepare.1 = (f32[256,128]{1,0:T(8,128)S(1)}, f32[256,128]{1,0:T(8,128)S(1)}, f32[256,128]{1,0:T(8,128)S(1)}, f32[256,128]{1,0:T(8,128)S(1)}, f32[128,128]{1,0:T(8,128)S(1)}, /*index=5*/f32[128,128]{1,0:T(8,128)S(1)}) custom-call(s32[8]{0:T(128)S(1)} %stack.28.base_ref.scalar_ref.plane_ref, s32[1,128]{1,0:T(1,128)S(1)} %copy-done.4, ...), custom_call_target="tpu_custom_call" | custom-call | tf_op jit(solution)/shard_map/prepare/pallas_call | solution.py:74
  16.1 2.3 %collective-permute-done.1.rest_7_ = bf16[2,256,128]{2,1,0:T(8,128)(2,1)S(1)} collective-permute-done((bf16[2,256,128]{2,1,0:T(8,128)(2,1)S(1)}, bf16[2,256,128]{2,1,0:T(8,128)(2,1)S(1)}, u32[]{:S(2)}, u32[]{:S(2)}) %collective-permute-start.1) | collective-permute-done | bytes 131104 | tf_op jit(solution)/shard_map/keys/ppermute | solution.py:33
  18.4 5.3 %attend.1.rest_0_ = bf16[392,1024]{1,0:T(8,128)(2,1)S(1)} custom-call(s32[8]{0:T(128)S(1)} %stack.28.base_ref.scalar_ref.plane_ref, bf16[256,1024]{1,0:T(8,128)(2,1)S(1)} %bitcast.15, bf16[128,1024]{1,0:T(8,128)(2,1)S(1)} %bitcast.16, bf16[2,128,128]{2,1,0:T(8,128)(2,1)S(1)} %bitcast.19, s32[1,128]{1,0:T(1,128)S(1)} %copy-done.4, ...), custom_call_target="tpu_custom_call" | custom-call | tf_op jit(solution)/shard_map/attend/pallas_call | solution.py:149
  23.7 6.7 %collective-permute-done.3.refs_6_ = bf16[512,896]{1,0:T(8,128)(2,1)S(1)} collective-permute-done((bf16[512,896]{1,0:T(8,128)(2,1)S(1)}, bf16[512,896]{1,0:T(8,128)(2,1)S(1)}, u32[]{:S(2)}, u32[]{:S(2)}) %collective-permute-start.3) | collective-permute-done | bytes 917536 | tf_op jit(solution)/shard_map/near0/ppermute | solution.py:33
  31.2 1.6 collective-permute-start.5
  32.8 7.2 %collective-permute-start.6 = (bf16[392,1024]{1,0:T(8,128)(2,1)S(1)}, bf16[392,1024]{1,0:T(8,128)(2,1)S(1)}, u32[]{:S(2)}, u32[]{:S(2)}) collective-permute-start(bf16[392,1024]{1,0:T(8,128)(2,1)S(1)} %attend.1.rest_0_), channel_id=1, source_target_pairs={{0,8},{24,16},{1,9},{25,17},{2,10},{26,18},{3,11},{27,19},{4,12},{... | collective-permute-start | bytes 2408456 | tf_op jit(solution)/shard_map/hand/ppermute | solution.py:33
  40.0 10.4 %collective-permute-done.5.rest_1_ = bf16[392,1024]{1,0:T(8,128)(2,1)S(1)} collective-permute-done((bf16[392,1024]{1,0:T(8,128)(2,1)S(1)}, bf16[392,1024]{1,0:T(8,128)(2,1)S(1)}, u32[]{:S(2)}, u32[]{:S(2)}) %collective-permute-start.5) | collective-permute-done | bytes 802848 | tf_op jit(solution)/shard_map/rows/ppermute | solution.py:33
  50.4 5.6 %collective-permute-done.6.rest_0_ = bf16[392,1024]{1,0:T(8,128)(2,1)S(1)} collective-permute-done((bf16[392,1024]{1,0:T(8,128)(2,1)S(1)}, bf16[392,1024]{1,0:T(8,128)(2,1)S(1)}, u32[]{:S(2)}, u32[]{:S(2)}) %collective-permute-start.6) | collective-permute-done | bytes 802848 | tf_op jit(solution)/shard_map/hand/ppermute | solution.py:33
  56.0 1.4 pack.2.refs_0_
  57.5 4.5 %collective-permute-start.10 = (bf16[512,1152]{1,0:T(8,128)(2,1)S(1)}, bf16[512,1152]{1,0:T(8,128)(2,1)S(1)}, u32[]{:S(2)}, u32[]{:S(2)}) collective-permute-start(bf16[512,1152]{1,0:T(8,128)(2,1)S(1)} %pad_maximum_fusion.refs_4_), channel_id=1, source_target_pairs={{0,8},{24,16},{1,9},{25,17},{2,10},{26,18},{3,11},{27,19},{4,12},{... | collective-permute-start | bytes 3538952 | tf_op jit(solution)/shard_map/near1/ppermute | solution.py:33
  63.3 19.5 %collective-permute-done.9.rest_1_ = bf16[392,1024]{1,0:T(8,128)(2,1)S(1)} collective-permute-done((bf16[392,1024]{1,0:T(8,128)(2,1)S(1)}, bf16[392,1024]{1,0:T(8,128)(2,1)S(1)}, u32[]{:S(2)}, u32[]{:S(2)}) %collective-permute-start.9) | collective-permute-done | bytes 802848 | tf_op jit(solution)/shard_map/other/ppermute | solution.py:33
  82.8 5.0 %collective-permute-done.10.refs_6_ = bf16[512,1152]{1,0:T(8,128)(2,1)S(1)} collective-permute-done((bf16[512,1152]{1,0:T(8,128)(2,1)S(1)}, bf16[512,1152]{1,0:T(8,128)(2,1)S(1)}, u32[]{:S(2)}, u32[]{:S(2)}) %collective-permute-start.10) | collective-permute-done | bytes 1179680 | tf_op jit(solution)/shard_map/near1/ppermute | solution.py:33
  87.7 1.4 pack.3.refs_2_
  90.8 1.7 collective-permute-done.12.refs_3_
  94.3 1.3 collective-permute-start.18
  95.6 1.6 collective-permute-start.16
  99.7 1.6 collective-permute-start.25
  101.3 27.2 %collective-permute-done.18 = bf16[704,256]{1,0:T(8,128)(2,1)S(1)} collective-permute-done((bf16[704,256]{1,0:T(8,128)(2,1)S(1)}, bf16[704,256]{1,0:T(8,128)(2,1)S(1)}, u32[]{:S(2)}, u32[]{:S(2)}) %collective-permute-start.18) | collective-permute-done | bytes 360480 | tf_op jit(solution)/shard_map/return1/ppermute | solution.py:33
  129.9 1.6 collective-permute-start.20
  131.6 1.3 collective-permute-start.17
  133.1 2.3 %collective-permute-done.20 = bf16[352,256]{1,0:T(8,128)(2,1)S(1)} collective-permute-done((bf16[352,256]{1,0:T(8,128)(2,1)S(1)}, bf16[352,256]{1,0:T(8,128)(2,1)S(1)}, u32[]{:S(2)}, u32[]{:S(2)}) %collective-permute-start.20) | collective-permute-done | bytes 180256 | tf_op jit(solution)/shard_map/cross_after1/ppermute | solution.py:33
  135.4 1.3 collective-permute-start.22
  136.8 7.2 %collective-permute-done.13 = bf16[704,512]{1,0:T(8,128)(2,1)S(1)} collective-permute-done((bf16[704,512]{1,0:T(8,128)(2,1)S(1)}, bf16[704,512]{1,0:T(8,128)(2,1)S(1)}, u32[]{:S(2)}, u32[]{:S(2)}) %collective-permute-start.13) | collective-permute-done | bytes 720928 | tf_op jit(solution)/shard_map/return0/ppermute | solution.py:33
  144.1 1.6 collective-permute-start.15
  145.6 16.6 %collective-permute-done.22 = bf16[352,384]{1,0:T(8,128)(2,1)S(1)} collective-permute-done((bf16[352,384]{1,0:T(8,128)(2,1)S(1)}, bf16[352,384]{1,0:T(8,128)(2,1)S(1)}, u32[]{:S(2)}, u32[]{:S(2)}) %collective-permute-start.22) | collective-permute-done | bytes 270368 | tf_op jit(solution)/shard_map/return_after1/ppermute | solution.py:33
  162.6 1.3 collective-permute-start.26
  164.0 1.6 collective-permute-start.24
  165.6 5.8 %collective-permute-done.26 = bf16[352,256]{1,0:T(8,128)(2,1)S(1)} collective-permute-done((bf16[352,256]{1,0:T(8,128)(2,1)S(1)}, bf16[352,256]{1,0:T(8,128)(2,1)S(1)}, u32[]{:S(2)}, u32[]{:S(2)}) %collective-permute-start.26) | collective-permute-done | bytes 180256 | tf_op jit(solution)/shard_map/return_after2/ppermute | solution.py:33
  (81 shorter events, 17.4 us)
Async XLA Ops:
  1.6 9.1 %copy-start.5 = (bf16[1,256,4096]{2,1,0:T(8,128)(2,1)S(1)}, bf16[1,256,4096]{2,1,0:T(8,128)(2,1)}, u32[]{:S(2)}) copy-start(bf16[1,256,4096]{2,1,0:T(8,128)(2,1)} %param.15) | copy-start | bytes 6291460
  3.5 2.0 %collective-permute-start.2 = (bf16[256,896]{1,0:T(8,128)(2,1)S(1)}, bf16[256,896]{1,0:T(8,128)(2,1)S(1)}, u32[]{:S(2)}, u32[]{:S(2)}) collective-permute-start(bf16[256,896]{1,0:T(8,128)(2,1)S(1)} %get-tuple-element.84), channel_id=1, source_target_pairs={{0,1},{1,0},{2,3},{3,2},{4,5},{5,4},{6,7},{7,6},{8,9},{9,8},{10,11... | collective-permute-start | bytes 1376264 | tf_op jit(solution)/shard_map/trade0/ppermute | solution.py:33
  5.6 8.5 %copy-start.4 = (s32[1,128]{1,0:T(1,128)S(1)}, s32[1,128]{1,0:T(1,128)}, u32[]{:S(2)}) copy-start(s32[1,128]{1,0:T(1,128)} %doc_ref.3) | copy-start | bytes 1540
  5.6 24.9 %collective-permute-start.3 = (bf16[512,896]{1,0:T(8,128)(2,1)S(1)}, bf16[512,896]{1,0:T(8,128)(2,1)S(1)}, u32[]{:S(2)}, u32[]{:S(2)}) collective-permute-start(bf16[512,896]{1,0:T(8,128)(2,1)S(1)} %pad_maximum_fusion.1.refs_4_), channel_id=1, source_target_pairs={{0,8},{24,16},{1,9},{25,17},{2,10},{26,18},{3,11},{27,19},{4,12},{... | collective-permute-start | bytes 2752520 | tf_op jit(solution)/shard_map/near0/ppermute | solution.py:33
  11.6 4.4 %collective-permute-start = (bf16[256,1152]{1,0:T(8,128)(2,1)S(1)}, bf16[256,1152]{1,0:T(8,128)(2,1)S(1)}, u32[]{:S(2)}, u32[]{:S(2)}) collective-permute-start(bf16[256,1152]{1,0:T(8,128)(2,1)S(1)} %get-tuple-element.86), channel_id=1, source_target_pairs={{0,1},{1,0},{2,3},{3,2},{4,5},{5,4},{6,7},{7,6},{8,9},{9,8},{10,11... | collective-permute-start | bytes 1769480 | tf_op jit(solution)/shard_map/trade1/ppermute | solution.py:33
  11.7 19.5 %collective-permute-start.4 = (bf16[512,896]{1,0:T(8,128)(2,1)S(1)}, bf16[512,896]{1,0:T(8,128)(2,1)S(1)}, u32[]{:S(2)}, u32[]{:S(2)}) collective-permute-start(bf16[512,896]{1,0:T(8,128)(2,1)S(1)} %pad_maximum_fusion.1.refs_4_), channel_id=1, source_target_pairs={{8,16},{16,8},{9,17},{17,9},{10,18},{18,10},{11,19},{19,11},{12,20... | collective-permute-start | bytes 2752520 | tf_op jit(solution)/shard_map/twin0/ppermute | solution.py:33
  12.6 5.8 %collective-permute-start.1 = (bf16[2,256,128]{2,1,0:T(8,128)(2,1)S(1)}, bf16[2,256,128]{2,1,0:T(8,128)(2,1)S(1)}, u32[]{:S(2)}, u32[]{:S(2)}) collective-permute-start(bf16[2,256,128]{2,1,0:T(8,128)(2,1)S(1)} %bitcast.17), channel_id=1, source_target_pairs={{0,4},{4,0},{1,5},{5,1},{2,6},{6,2},{3,7},{7,3},{8,12},{12,8},{9,1... | collective-permute-start | bytes 393224 | tf_op jit(solution)/shard_map/keys/ppermute | solution.py:33
  30.5 25.5 %collective-permute-start.7 = (bf16[512,896]{1,0:T(8,128)(2,1)S(1)}, bf16[512,896]{1,0:T(8,128)(2,1)S(1)}, u32[]{:S(2)}, u32[]{:S(2)}) collective-permute-start(bf16[512,896]{1,0:T(8,128)(2,1)S(1)} %collective-permute-done.3.refs_6_), channel_id=1, source_target_pairs={{8,16},{16,8},{9,17},{17,9},{10,18},{18,10},{11,19},{19,11},{12,20... | collective-permute-start | bytes 2752520 | tf_op jit(solution)/shard_map/far0/ppermute | solution.py:33
  31.2 19.2 %collective-permute-start.5 = (bf16[392,1024]{1,0:T(8,128)(2,1)S(1)}, bf16[392,1024]{1,0:T(8,128)(2,1)S(1)}, u32[]{:S(2)}, u32[]{:S(2)}) collective-permute-start(bf16[392,1024]{1,0:T(8,128)(2,1)S(1)} %attend.1.rest_0_), channel_id=1, source_target_pairs={{0,4},{4,0},{1,5},{5,1},{2,6},{6,2},{3,7},{7,3},{8,12},{12,8},{9,1... | collective-permute-start | bytes 2408456 | tf_op jit(solution)/shard_map/rows/ppermute | solution.py:33
  32.8 23.2 %collective-permute-start.6 = (bf16[392,1024]{1,0:T(8,128)(2,1)S(1)}, bf16[392,1024]{1,0:T(8,128)(2,1)S(1)}, u32[]{:S(2)}, u32[]{:S(2)}) collective-permute-start(bf16[392,1024]{1,0:T(8,128)(2,1)S(1)} %attend.1.rest_0_), channel_id=1, source_target_pairs={{0,8},{24,16},{1,9},{25,17},{2,10},{26,18},{3,11},{27,19},{4,12},{... | collective-permute-start | bytes 2408456 | tf_op jit(solution)/shard_map/hand/ppermute | solution.py:33
  57.4 30.3 %collective-permute-start.8 = (bf16[704,1024]{1,0:T(8,128)(2,1)S(1)}, bf16[704,1024]{1,0:T(8,128)(2,1)S(1)}, u32[]{:S(2)}, u32[]{:S(2)}) collective-permute-start(bf16[704,1024]{1,0:T(8,128)(2,1)S(1)} %pack.2.refs_0_), channel_id=1, source_target_pairs={{0,1},{1,0},{2,3},{3,2},{4,5},{5,4},{6,7},{7,6},{8,9},{9,8},{10,11... | collective-permute-start | bytes 4325384 | tf_op jit(solution)/shard_map/own_rows/ppermute | solution.py:33
  57.5 30.3 %collective-permute-start.10 = (bf16[512,1152]{1,0:T(8,128)(2,1)S(1)}, bf16[512,1152]{1,0:T(8,128)(2,1)S(1)}, u32[]{:S(2)}, u32[]{:S(2)}) collective-permute-start(bf16[512,1152]{1,0:T(8,128)(2,1)S(1)} %pad_maximum_fusion.refs_4_), channel_id=1, source_target_pairs={{0,8},{24,16},{1,9},{25,17},{2,10},{26,18},{3,11},{27,19},{4,12},{... | collective-permute-start | bytes 3538952 | tf_op jit(solution)/shard_map/near1/ppermute | solution.py:33
  61.9 25.8 %collective-permute-start.11 = (bf16[512,1152]{1,0:T(8,128)(2,1)S(1)}, bf16[512,1152]{1,0:T(8,128)(2,1)S(1)}, u32[]{:S(2)}, u32[]{:S(2)}) collective-permute-start(bf16[512,1152]{1,0:T(8,128)(2,1)S(1)} %pad_maximum_fusion.refs_4_), channel_id=1, source_target_pairs={{8,16},{16,8},{9,17},{17,9},{10,18},{18,10},{11,19},{19,11},{12,20... | collective-permute-start | bytes 3538952 | tf_op jit(solution)/shard_map/twin1/ppermute | solution.py:33
  62.7 20.1 %collective-permute-start.9 = (bf16[392,1024]{1,0:T(8,128)(2,1)S(1)}, bf16[392,1024]{1,0:T(8,128)(2,1)S(1)}, u32[]{:S(2)}, u32[]{:S(2)}) collective-permute-start(bf16[392,1024]{1,0:T(8,128)(2,1)S(1)} %collective-permute-done.6.rest_0_), channel_id=1, source_target_pairs={{0,4},{4,0},{1,5},{5,1},{2,6},{6,2},{3,7},{7,3},{8,12},{12,8},{9,1... | collective-permute-start | bytes 2408456 | tf_op jit(solution)/shard_map/other/ppermute | solution.py:33
  89.2 3.3 %collective-permute-start.12 = (bf16[704,1024]{1,0:T(8,128)(2,1)S(1)}, bf16[704,1024]{1,0:T(8,128)(2,1)S(1)}, u32[]{:S(2)}, u32[]{:S(2)}) collective-permute-start(bf16[704,1024]{1,0:T(8,128)(2,1)S(1)} %pack.3.refs_2_), channel_id=1, source_target_pairs={{0,1},{1,0},{2,3},{3,2},{4,5},{5,4},{6,7},{7,6},{8,9},{9,8},{10,11... | collective-permute-start | bytes 4325384 | tf_op jit(solution)/shard_map/other_rows/ppermute | solution.py:33
  89.3 4.1 %collective-permute-start.14 = (bf16[512,640]{1,0:T(8,128)(2,1)S(1)}, bf16[512,640]{1,0:T(8,128)(2,1)S(1)}, u32[]{:S(2)}, u32[]{:S(2)}) collective-permute-start(bf16[512,640]{1,0:T(8,128)(2,1)S(1)} %slice.102), channel_id=1, source_target_pairs={{8,16},{16,8},{9,17},{17,9},{10,18},{18,10},{11,19},{19,11},{12,20... | collective-permute-start | bytes 1966088 | tf_op jit(solution)/shard_map/far1/ppermute | solution.py:33
  90.1 9.0 %collective-permute-start.19 = (bf16[512,512]{1,0:T(8,128)(2,1)S(1)}, bf16[512,512]{1,0:T(8,128)(2,1)S(1)}, u32[]{:S(2)}, u32[]{:S(2)}) collective-permute-start(bf16[512,512]{1,0:T(8,128)(2,1)S(1)} %slice.109), channel_id=1, source_target_pairs={{8,16},{16,8},{9,17},{17,9},{10,18},{18,10},{11,19},{19,11},{12,20... | collective-permute-start | bytes 1572872 | tf_op jit(solution)/shard_map/far2/ppermute | solution.py:33
  94.3 34.2 %collective-permute-start.18 = (bf16[704,256]{1,0:T(8,128)(2,1)S(1)}, bf16[704,256]{1,0:T(8,128)(2,1)S(1)}, u32[]{:S(2)}, u32[]{:S(2)}) collective-permute-start(bf16[704,256]{1,0:T(8,128)(2,1)S(1)} %get-tuple-element.71), channel_id=1, source_target_pairs={{8,0},{16,24},{9,1},{17,25},{10,2},{18,26},{11,3},{19,27},{12,4},{... | collective-permute-start | bytes 1081352 | tf_op jit(solution)/shard_map/return1/ppermute | solution.py:33
  95.6 34.2 %collective-permute-start.16 = (bf16[704,384]{1,0:T(8,128)(2,1)S(1)}, bf16[704,384]{1,0:T(8,128)(2,1)S(1)}, u32[]{:S(2)}, u32[]{:S(2)}) collective-permute-start(bf16[704,384]{1,0:T(8,128)(2,1)S(1)} %get-tuple-element.69), channel_id=1, source_target_pairs={{0,2},{1,3},{2,0},{3,1},{4,6},{5,7},{6,4},{7,5},{8,10},{9,11},{10,... | collective-permute-start | bytes 1622024 | tf_op jit(solution)/shard_map/cross0/ppermute | solution.py:33
  97.2 46.7 %collective-permute-start.13 = (bf16[704,512]{1,0:T(8,128)(2,1)S(1)}, bf16[704,512]{1,0:T(8,128)(2,1)S(1)}, u32[]{:S(2)}, u32[]{:S(2)}) collective-permute-start(bf16[704,512]{1,0:T(8,128)(2,1)S(1)} %get-tuple-element.64), channel_id=1, source_target_pairs={{8,0},{16,24},{9,1},{17,25},{10,2},{18,26},{11,3},{19,27},{12,4},{... | collective-permute-start | bytes 2162696 | tf_op jit(solution)/shard_map/return0/ppermute | solution.py:33
  98.5 33.1 %collective-permute-start.21 = (bf16[704,384]{1,0:T(8,128)(2,1)S(1)}, bf16[704,384]{1,0:T(8,128)(2,1)S(1)}, u32[]{:S(2)}, u32[]{:S(2)}) collective-permute-start(bf16[704,384]{1,0:T(8,128)(2,1)S(1)} %get-tuple-element.76), channel_id=1, source_target_pairs={{0,2},{1,3},{2,0},{3,1},{4,6},{5,7},{6,4},{7,5},{8,10},{9,11},{10,... | collective-permute-start | bytes 1622024 | tf_op jit(solution)/shard_map/cross1/ppermute | solution.py:33
  99.7 62.7 %collective-permute-start.25 = (bf16[704,256]{1,0:T(8,128)(2,1)S(1)}, bf16[704,256]{1,0:T(8,128)(2,1)S(1)}, u32[]{:S(2)}, u32[]{:S(2)}) collective-permute-start(bf16[704,256]{1,0:T(8,128)(2,1)S(1)} %get-tuple-element.81), channel_id=1, source_target_pairs={{0,2},{1,3},{2,0},{3,1},{4,6},{5,7},{6,4},{7,5},{8,10},{9,11},{10,... | collective-permute-start | bytes 1081352 | tf_op jit(solution)/shard_map/cross2/ppermute | solution.py:33
  128.5 35.4 %collective-permute-start.23 = (bf16[704,256]{1,0:T(8,128)(2,1)S(1)}, bf16[704,256]{1,0:T(8,128)(2,1)S(1)}, u32[]{:S(2)}, u32[]{:S(2)}) collective-permute-start(bf16[704,256]{1,0:T(8,128)(2,1)S(1)} %get-tuple-element.78), channel_id=1, source_target_pairs={{8,0},{16,24},{9,1},{17,25},{10,2},{18,26},{11,3},{19,27},{12,4},{... | collective-permute-start | bytes 1081352 | tf_op jit(solution)/shard_map/return2/ppermute | solution.py:33
  129.9 5.6 %collective-permute-start.20 = (bf16[352,256]{1,0:T(8,128)(2,1)S(1)}, bf16[352,256]{1,0:T(8,128)(2,1)S(1)}, u32[]{:S(2)}, u32[]{:S(2)}) collective-permute-start(bf16[352,256]{1,0:T(8,128)(2,1)S(1)} %fusion.4), channel_id=1, source_target_pairs={{0,2},{1,3},{2,0},{3,1},{4,6},{5,7},{6,4},{7,5},{8,10},{9,11},{10,... | collective-permute-start | bytes 540680 | tf_op jit(solution)/shard_map/cross_after1/ppermute | solution.py:33
  131.6 33.9 %collective-permute-start.17 = (bf16[352,384]{1,0:T(8,128)(2,1)S(1)}, bf16[352,384]{1,0:T(8,128)(2,1)S(1)}, u32[]{:S(2)}, u32[]{:S(2)}) collective-permute-start(bf16[352,384]{1,0:T(8,128)(2,1)S(1)} %slice.106), channel_id=1, source_target_pairs={{8,0},{16,24},{9,1},{17,25},{10,2},{18,26},{11,3},{19,27},{12,4},{... | collective-permute-start | bytes 811016 | tf_op jit(solution)/shard_map/return_after0/ppermute | solution.py:33
  135.4 26.8 %collective-permute-start.22 = (bf16[352,384]{1,0:T(8,128)(2,1)S(1)}, bf16[352,384]{1,0:T(8,128)(2,1)S(1)}, u32[]{:S(2)}, u32[]{:S(2)}) collective-permute-start(bf16[352,384]{1,0:T(8,128)(2,1)S(1)} %slice.113), channel_id=1, source_target_pairs={{8,0},{16,24},{9,1},{17,25},{10,2},{18,26},{11,3},{19,27},{12,4},{... | collective-permute-start | bytes 811016 | tf_op jit(solution)/shard_map/return_after1/ppermute | solution.py:33
  144.1 27.4 %collective-permute-start.15 = (bf16[352,512]{1,0:T(8,128)(2,1)S(1)}, bf16[352,512]{1,0:T(8,128)(2,1)S(1)}, u32[]{:S(2)}, u32[]{:S(2)}) collective-permute-start(bf16[352,512]{1,0:T(8,128)(2,1)S(1)} %slice.104), channel_id=1, source_target_pairs={{0,2},{1,3},{2,0},{3,1},{4,6},{5,7},{6,4},{7,5},{8,10},{9,11},{10,... | collective-permute-start | bytes 1081352 | tf_op jit(solution)/shard_map/cross_after0/ppermute | solution.py:33
  162.4 11.0 %collective-permute-start.28 = (bf16[176,640]{1,0:T(8,128)(2,1)S(1)}, bf16[176,640]{1,0:T(8,128)(2,1)S(1)}, u32[]{:S(2)}, u32[]{:S(2)}) collective-permute-start(bf16[176,640]{1,0:T(8,128)(2,1)S(1)} %get-tuple-element.94), channel_id=1, source_target_pairs={{0,1},{1,0},{2,3},{3,2},{4,5},{5,4},{6,7},{7,6},{8,9},{9,8},{10,11... | collective-permute-start | bytes 675848 | tf_op jit(solution)/shard_map/rest1/ppermute | solution.py:33
  162.6 8.8 %collective-permute-start.26 = (bf16[352,256]{1,0:T(8,128)(2,1)S(1)}, bf16[352,256]{1,0:T(8,128)(2,1)S(1)}, u32[]{:S(2)}, u32[]{:S(2)}) collective-permute-start(bf16[352,256]{1,0:T(8,128)(2,1)S(1)} %slice.119), channel_id=1, source_target_pairs={{8,0},{16,24},{9,1},{17,25},{10,2},{18,26},{11,3},{19,27},{12,4},{... | collective-permute-start | bytes 540680 | tf_op jit(solution)/shard_map/return_after2/ppermute | solution.py:33
  164.0 7.8 %collective-permute-start.24 = (bf16[352,256]{1,0:T(8,128)(2,1)S(1)}, bf16[352,256]{1,0:T(8,128)(2,1)S(1)}, u32[]{:S(2)}, u32[]{:S(2)}) collective-permute-start(bf16[352,256]{1,0:T(8,128)(2,1)S(1)} %slice.117), channel_id=1, source_target_pairs={{0,2},{1,3},{2,0},{3,1},{4,6},{5,7},{6,4},{7,5},{8,10},{9,11},{10,... | collective-permute-start | bytes 540680 | tf_op jit(solution)/shard_map/cross_after2/ppermute | solution.py:33
  171.7 1.7 collective-permute-start.27
  171.9 1.7 collective-permute-start.29
  (4 other events, 27.4 us)

commit v3 on v2

--- a/solution.py
+++ b/solution.py
@@ -11,6 +11,7 @@
 NEGATIVE_FILL = -1e30
 ROPE_BASE = 500000.0
 COUNT_ROWS = 8
+DEEP = 2
 FIRST_ROW, BASE, LIVE, CTX, HALVES, PLANE = 0, 1, 3, 4, 5, 7
 VMEM_LIMIT = 56 * 1024 * 1024
 SMALL_LIMIT = 12 * 1024 * 1024
@@ -210,13 +211,23 @@
 
 
 def project_kernel(at, width, straight, plane_ref, *refs):
-    rows, weights, outs = refs[:4], refs[4:8], refs[8:]
+    pieces = 2 if straight < width else 1
+    count = 2 * pieces + 2
+    rows, weights, outs = refs[:4], refs[4 : 4 + count], refs[4 + count :]
     depth = weights[0].shape[0] // 2
     half = rows[0].shape[0] // 2
 
     def block(i, part, a, b):
         here = slice(part * depth, (part + 1) * depth)
-        return weights[i][here, a:b] if i == 3 else weights[i][here, at + a : at + b]
+        if i > 1:
+            return weights[2 * pieces + i - 2][here, a:b]
+        sides, first = [], 0
+        for ref in weights[i * pieces : (i + 1) * pieces]:
+            x, y = max(at + a, first), min(at + b, first + ref.shape[1])
+            if x < y:
+                sides.append(ref[here, x - first : y - first])
+            first += ref.shape[1]
+        return sides[0] if len(sides) == 1 else jnp.concatenate(sides, axis=1)
 
     for plane, order in ((1, (2, 0, 1, 3)), (2, (3, 1, 0, 2))):
 
@@ -274,7 +285,7 @@
     unit = columns // 16
     if unit % 128:
         return [columns], [columns]
-    return [7 * unit, 5 * unit, 4 * unit], [4 * unit, 2 * unit, 2 * unit]
+    return [4 * unit, 6 * unit, 6 * unit], [2 * unit, 3 * unit, 3 * unit]
 
 
 def local(
@@ -316,14 +327,29 @@
         return jnp.concatenate([kept[:, a:b], theirs], axis=0)
 
     near, far = {}, {}
-    both = [trade(0, widths[0], "trade0")]
-    near[0] = send(both[0], "dp", OUT_TO_IN, "near0")
+    cut = width // 2 if n > 1 else width
+    both = [trade(0, cut, "trade0")]
+    columns = [sum(widths[:i]) for i in range(n)]
+
+    def fetch_near(i, *gates):
+        if i < n:
+            a, b = columns[i], columns[i] + widths[i]
+            sides = []
+            if a < cut:
+                sides.append(both[0][:, a : min(b, cut)])
+            if b > cut:
+                sides.append(both[1][:, max(a, cut) - cut : b - cut])
+            source = sides[0] if len(sides) == 1 else jnp.concatenate(sides, axis=1)
+            near[i] = send(after(source, *gates), "dp", OUT_TO_IN, f"near{i}")
+
+    fetch_near(0, place)
     twin = [send(both[0], "dp", INNER, "twin0")]
     if n > 1:
-        both.append(trade(widths[0], width, "trade1"))
-
-    def forward(i, source):
-        far[i] = send(source, "dp", INNER, f"far{i}")
+        both.append(trade(cut, width, "trade1"))
+
+    def forward(i, *gates):
+        if i < n:
+            far[i] = send(after(near[i], *gates), "dp", INNER, f"far{i}")
 
     raw = long_key_value[0]
     if n_ctx == 2:
@@ -337,8 +363,8 @@
     if n > 1:
         inputs = (after(place, both[1]), *inputs[1:])
     rows = attend(*inputs)
-    forward(0, after(near[0], rows))
-    rows = after(rows, near[0], twin[0])
+    forward(0, rows)
+    rows = after(rows, near[0])
 
     def gathered(x, name):
         if n_ctx == 2:
@@ -349,30 +375,26 @@
     pieces = gathered(rows, "rows")
     other_pieces = gathered(handed, "other")
     if n > 1:
-        rest = after(both[1], handed, far[0])
-        twin.append(send(rest, "dp", INNER, "twin1"))
-        near[1] = send(rest, "dp", OUT_TO_IN, "near1")
-    pieces[-1] = after(pieces[-1], handed, far[0])
+        twin.append(send(after(both[1], handed, twin[0]), "dp", INNER, "twin1"))
+    fetch_near(1, handed, twin[0])
+    pieces[-1] = after(pieces[-1], handed, far[0], twin[0])
     own = pack(place, pieces, long_rows, slots, n_ctx)
     own_theirs = send(own, "tp", CORE, "own_rows")
     if n > 1:
         other_pieces[-1] = after(other_pieces[-1], near[1], own_theirs, twin[1])
-        at = 0
-        for i in range(1, n):
-            forward(i, near[1][:, at : at + widths[i]])
-            at += widths[i]
     other = pack(place, other_pieces, long_rows, slots, n_ctx)
     other_theirs = send(other, "tp", CORE, "other_rows")
+    forward(1, other)
+    fetch_near(2, other)
     group = (own, own_theirs, other, other_theirs)
 
     def add(a, b):
         return (a.astype(jnp.float32) + b.astype(jnp.float32)).astype(jnp.bfloat16)
 
     def first_hop(i):
-        part = min(i, 1)
-        at = sum(widths[1:i])
-        weights = (both[part], twin[part], near[part], far[i])
-        outs = project(place, group, weights, at, widths[i], straight[i])
+        outs = project(
+            place, group, (*both, *twin, near[i], far[i]), columns[i], widths[i], straight[i]
+        )
         hop = {}
         if straight[i]:
             hop["mine"], other_part = outs[0], outs[1]
@@ -406,13 +428,17 @@
     hops, seconds = [], []
     for i in range(n):
         if i:
-            far[i] = after(far[i], gate)
+            gates = list(seconds[-1].values()) if i > 1 and i < DEEP else []
+            seconds.append(second_hop(i - 1, hops[i - 1], *gates)) if i < DEEP else None
+            leaving = [seconds[-1][k] for k in ("kept", "mine") if k in seconds[-1]]
+            later = [near[i + 1]] if i + 1 < n else []
+            far[i] = after(far[i], *leaving, *later)
+            forward(i + 1)
         hop, gate = first_hop(i)
         hops.append(hop)
-        if i:
-            seconds.append(second_hop(i - 1, hops[i - 1], gate))
-    gates = list(seconds[-1].values()) if seconds else []
-    seconds.append(second_hop(n - 1, hops[-1], *gates))
+    for i in range(len(seconds), n):
+        gates = list(seconds[-1].values()) if i else []
+        seconds.append(second_hop(i, hops[i], gate, *gates))
     quarter = half // 2
     mine, theirs = [], []
     for i, done in enumerate(seconds):

time: 176 us -> 166 us (0.943)
  waiting for transfers between devices: 113 us -> 98.2 us
  starting transfers between devices: 41.7 us -> 47 us
    ppermute x30 -> x31, waiting for transfers between devices: 113 us -> 98.2 us  [send(): return lax.ppermute(x, axis, pairs)]
    ppermute x30 -> x31, starting transfers between devices: 41.7 us -> 47 us  [send(): return lax.ppermute(x, axis, pairs)]
  transfers between devices with their start and end apart: 30 -> 31, of which waited for: 15 -> 12; matrix products, arithmetic and copies ran while one was open for 1% -> 1% of each run, Pallas kernels for 6% -> 6%
where the time goes in v3:
time: 166 us
  waiting for transfers between devices  98.2 us (59%)
  starting transfers between devices  47 us (28%)
  Pallas kernels  12.6 us (8%)
  other arithmetic  3.8 us (2%)
  local copies, waits for them, and re-layouts  2.94 us (2%)
    ppermute x31, waiting for transfers between devices, send(): return lax.ppermute(x, axis, pairs)  98.2 us
    ppermute x31, starting transfers between devices, send(): return lax.ppermute(x, axis, pairs)  47 us
    pallas_call x1, Pallas kernels, attend(): pl.pallas_call(functools.partial(attend_kernel, len(pairs), len(tables)),...  5.35 us
  transfers between devices with their start and end apart: 31, of which 12 were waited for; matrix products, arithmetic and copies ran while one was open for 1% of the time, Pallas kernels for 6%

profile of v3, /device:TPU:0, one launch (start us, length us, event | category | flops | bytes accessed | tf_op | source)
XLA Modules:
  0.0 165.8 jit_solution(364456959212019583)
XLA Ops:
  1.6 2.6 %constant_dynamic-slice_fusion.2 = (bf16[256,1024]{1,0:T(8,128)(2,1)S(1)}, bf16[256,1024]{1,0:T(8,128)(2,1)S(1)}, bf16[256,1024]{1,0:T(8,128)(2,1)S(1)}, bf16[256,1024]{1,0:T(8,128)(2,1)S(1)}) fusion(bf16[256,4096]{1,0:T(8,128)(2,1)} %bitcast.20, s32[]{:T(128)S(6)} %select_n.94, s32[]{:T(128)S(6)} %add.33, s32[]{:T(128)S(6)} %add.32, s32[]{:T(128)S(6)} %select_n.93), kind=kLoop, calls=%fused_computation.54 | loop fusion | bytes 4194320 | tf_op jit(solution)/shard_map/slice | solution.py:326
  4.8 1.5 collective-permute-done.2
  6.3 5.0 %collective-permute-start.3 = (bf16[512,512]{1,0:T(8,128)(2,1)S(1)}, bf16[512,512]{1,0:T(8,128)(2,1)S(1)}, u32[]{:S(2)}, u32[]{:S(2)}) collective-permute-start(bf16[512,512]{1,0:T(8,128)(2,1)S(1)} %get-tuple-element.60), channel_id=1, source_target_pairs={{0,8},{24,16},{1,9},{25,17},{2,10},{26,18},{3,11},{27,19},{4,12},{... | collective-permute-start | bytes 1572872 | tf_op jit(solution)/shard_map/near0/ppermute | solution.py:34
  12.4 1.6 collective-permute-start.1
  13.9 1.8 %prepare.1 = (f32[256,128]{1,0:T(8,128)S(1)}, f32[256,128]{1,0:T(8,128)S(1)}, f32[256,128]{1,0:T(8,128)S(1)}, f32[256,128]{1,0:T(8,128)S(1)}, f32[128,128]{1,0:T(8,128)S(1)}, /*index=5*/f32[128,128]{1,0:T(8,128)S(1)}) custom-call(s32[8]{0:T(128)S(1)} %stack.28.base_ref.scalar_ref.plane_ref, s32[1,128]{1,0:T(1,128)S(1)} %copy-done.4, ...), custom_call_target="tpu_custom_call" | custom-call | tf_op jit(solution)/shard_map/prepare/pallas_call | solution.py:75
  15.9 1.8 %collective-permute-done.1.rest_7_ = bf16[2,256,128]{2,1,0:T(8,128)(2,1)S(1)} collective-permute-done((bf16[2,256,128]{2,1,0:T(8,128)(2,1)S(1)}, bf16[2,256,128]{2,1,0:T(8,128)(2,1)S(1)}, u32[]{:S(2)}, u32[]{:S(2)}) %collective-permute-start.1) | collective-permute-done | bytes 131104 | tf_op jit(solution)/shard_map/keys/ppermute | solution.py:34
  17.7 5.3 %attend.1.rest_0_ = bf16[392,1024]{1,0:T(8,128)(2,1)S(1)} custom-call(s32[8]{0:T(128)S(1)} %stack.28.base_ref.scalar_ref.plane_ref, bf16[256,1024]{1,0:T(8,128)(2,1)S(1)} %bitcast.15, bf16[128,1024]{1,0:T(8,128)(2,1)S(1)} %bitcast.16, bf16[2,128,128]{2,1,0:T(8,128)(2,1)S(1)} %bitcast.19, s32[1,128]{1,0:T(1,128)S(1)} %copy-done.4, ...), custom_call_target="tpu_custom_call" | custom-call | tf_op jit(solution)/shard_map/attend/pallas_call | solution.py:150
  23.1 4.2 %collective-permute-start.5 = (bf16[392,1024]{1,0:T(8,128)(2,1)S(1)}, bf16[392,1024]{1,0:T(8,128)(2,1)S(1)}, u32[]{:S(2)}, u32[]{:S(2)}) collective-permute-start(bf16[392,1024]{1,0:T(8,128)(2,1)S(1)} %attend.1.rest_0_), channel_id=1, source_target_pairs={{0,8},{24,16},{1,9},{25,17},{2,10},{26,18},{3,11},{27,19},{4,12},{... | collective-permute-start | bytes 2408456 | tf_op jit(solution)/shard_map/hand/ppermute | solution.py:34
  27.2 1.6 collective-permute-start.4
  29.5 14.3 %collective-permute-done.5.rest_0_ = bf16[392,1024]{1,0:T(8,128)(2,1)S(1)} collective-permute-done((bf16[392,1024]{1,0:T(8,128)(2,1)S(1)}, bf16[392,1024]{1,0:T(8,128)(2,1)S(1)}, u32[]{:S(2)}, u32[]{:S(2)}) %collective-permute-start.5) | collective-permute-done | bytes 802848 | tf_op jit(solution)/shard_map/hand/ppermute | solution.py:34
  43.8 2.3 %collective-permute-done.4.rest_1_ = bf16[392,1024]{1,0:T(8,128)(2,1)S(1)} collective-permute-done((bf16[392,1024]{1,0:T(8,128)(2,1)S(1)}, bf16[392,1024]{1,0:T(8,128)(2,1)S(1)}, u32[]{:S(2)}, u32[]{:S(2)}) %collective-permute-start.4) | collective-permute-done | bytes 802848 | tf_op jit(solution)/shard_map/rows/ppermute | solution.py:34
  46.1 1.4 pack.2.refs_0_
  48.4 1.6 collective-permute-start.9
  50.0 7.9 %collective-permute-start.10 = (bf16[512,768]{1,0:T(8,128)(2,1)S(1)}, bf16[512,768]{1,0:T(8,128)(2,1)S(1)}, u32[]{:S(2)}, u32[]{:S(2)}) collective-permute-start(bf16[512,768]{1,0:T(8,128)(2,1)S(1)} %pad_maximum_fusion.2), channel_id=1, source_target_pairs={{0,8},{24,16},{1,9},{25,17},{2,10},{26,18},{3,11},{27,19},{4,12},{... | collective-permute-start | bytes 2359304 | tf_op jit(solution)/shard_map/near1/ppermute | solution.py:34
  57.9 16.8 %collective-permute-done.10.refs_8_ = bf16[512,768]{1,0:T(8,128)(2,1)S(1)} collective-permute-done((bf16[512,768]{1,0:T(8,128)(2,1)S(1)}, bf16[512,768]{1,0:T(8,128)(2,1)S(1)}, u32[]{:S(2)}, u32[]{:S(2)}) %collective-permute-start.10) | collective-permute-done | bytes 786464 | tf_op jit(solution)/shard_map/near1/ppermute | solution.py:34
  74.8 1.4 pack.3.refs_2_
  76.3 5.5 %collective-permute-start.18 = (bf16[512,768]{1,0:T(8,128)(2,1)S(1)}, bf16[512,768]{1,0:T(8,128)(2,1)S(1)}, u32[]{:S(2)}, u32[]{:S(2)}) collective-permute-start(bf16[512,768]{1,0:T(8,128)(2,1)S(1)} %fusion), channel_id=1, source_target_pairs={{0,8},{24,16},{1,9},{25,17},{2,10},{26,18},{3,11},{27,19},{4,12},{... | collective-permute-start | bytes 2359304 | tf_op jit(solution)/shard_map/near2/ppermute | solution.py:34
  82.7 1.6 collective-permute-start.15
  86.2 12.9 %collective-permute-done.18.refs_8_ = bf16[512,768]{1,0:T(8,128)(2,1)S(1)} collective-permute-done((bf16[512,768]{1,0:T(8,128)(2,1)S(1)}, bf16[512,768]{1,0:T(8,128)(2,1)S(1)}, u32[]{:S(2)}, u32[]{:S(2)}) %collective-permute-start.18) | collective-permute-done | bytes 786464 | tf_op jit(solution)/shard_map/near2/ppermute | solution.py:34
  100.0 1.3 collective-permute-start.16
  101.4 9.3 %collective-permute-done.16 = bf16[352,256]{1,0:T(8,128)(2,1)S(1)} collective-permute-done((bf16[352,256]{1,0:T(8,128)(2,1)S(1)}, bf16[352,256]{1,0:T(8,128)(2,1)S(1)}, u32[]{:S(2)}, u32[]{:S(2)}) %collective-permute-start.16) | collective-permute-done | bytes 180256 | tf_op jit(solution)/shard_map/return_after0/ppermute | solution.py:34
  111.5 1.3 collective-permute-start.19
  112.8 1.6 collective-permute-start.22
  115.9 1.3 collective-permute-start.24
  117.2 1.6 collective-permute-start.26
  118.7 13.2 %collective-permute-done.14 = bf16[352,256]{1,0:T(8,128)(2,1)S(1)} collective-permute-done((bf16[352,256]{1,0:T(8,128)(2,1)S(1)}, bf16[352,256]{1,0:T(8,128)(2,1)S(1)}, u32[]{:S(2)}, u32[]{:S(2)}) %collective-permute-start.14) | collective-permute-done | bytes 180256 | tf_op jit(solution)/shard_map/cross_after0/ppermute | solution.py:34
  132.2 1.3 collective-permute-start.23
  133.6 1.6 collective-permute-start.21
  135.3 17.8 %collective-permute-done.23 = bf16[352,384]{1,0:T(8,128)(2,1)S(1)} collective-permute-done((bf16[352,384]{1,0:T(8,128)(2,1)S(1)}, bf16[352,384]{1,0:T(8,128)(2,1)S(1)}, u32[]{:S(2)}, u32[]{:S(2)}) %collective-permute-start.23) | collective-permute-done | bytes 270368 | tf_op jit(solution)/shard_map/return_after1/ppermute | solution.py:34
  155.7 4.5 %collective-permute-done.25 = bf16[352,384]{1,0:T(8,128)(2,1)S(1)} collective-permute-done((bf16[352,384]{1,0:T(8,128)(2,1)S(1)}, bf16[352,384]{1,0:T(8,128)(2,1)S(1)}, u32[]{:S(2)}, u32[]{:S(2)}) %collective-permute-start.25) | collective-permute-done | bytes 270368 | tf_op jit(solution)/shard_map/cross_after2/ppermute | solution.py:34
  160.2 2.2 %collective-permute-done.27 = bf16[352,384]{1,0:T(8,128)(2,1)S(1)} collective-permute-done((bf16[352,384]{1,0:T(8,128)(2,1)S(1)}, bf16[352,384]{1,0:T(8,128)(2,1)S(1)}, u32[]{:S(2)}, u32[]{:S(2)}) %collective-permute-start.27) | collective-permute-done | bytes 270368 | tf_op jit(solution)/shard_map/return_after2/ppermute | solution.py:34
  162.7 1.5 collective-permute-done.30
  (82 shorter events, 15.0 us)
Async XLA Ops:
  4.2 2.1 %collective-permute-start.2 = (bf16[256,1024]{1,0:T(8,128)(2,1)S(1)}, bf16[256,1024]{1,0:T(8,128)(2,1)S(1)}, u32[]{:S(2)}, u32[]{:S(2)}) collective-permute-start(bf16[256,1024]{1,0:T(8,128)(2,1)S(1)} %get-tuple-element.87), channel_id=1, source_target_pairs={{0,1},{1,0},{2,3},{3,2},{4,5},{5,4},{6,7},{7,6},{8,9},{9,8},{10,11... | collective-permute-start | bytes 1572872 | tf_op jit(solution)/shard_map/trade0/ppermute | solution.py:34
  4.7 11.1 %collective-permute-start = (bf16[256,1024]{1,0:T(8,128)(2,1)S(1)}, bf16[256,1024]{1,0:T(8,128)(2,1)S(1)}, u32[]{:S(2)}, u32[]{:S(2)}) collective-permute-start(bf16[256,1024]{1,0:T(8,128)(2,1)S(1)} %get-tuple-element.88), channel_id=1, source_target_pairs={{0,1},{1,0},{2,3},{3,2},{4,5},{5,4},{6,7},{7,6},{8,9},{9,8},{10,11... | collective-permute-start | bytes 1572872 | tf_op jit(solution)/shard_map/trade1/ppermute | solution.py:34
  6.3 7.6 %copy-start.4 = (s32[1,128]{1,0:T(1,128)S(1)}, s32[1,128]{1,0:T(1,128)}, u32[]{:S(2)}) copy-start(s32[1,128]{1,0:T(1,128)} %doc_ref.3) | copy-start | bytes 1540
  6.3 16.7 %collective-permute-start.3 = (bf16[512,512]{1,0:T(8,128)(2,1)S(1)}, bf16[512,512]{1,0:T(8,128)(2,1)S(1)}, u32[]{:S(2)}, u32[]{:S(2)}) collective-permute-start(bf16[512,512]{1,0:T(8,128)(2,1)S(1)} %get-tuple-element.60), channel_id=1, source_target_pairs={{0,8},{24,16},{1,9},{25,17},{2,10},{26,18},{3,11},{27,19},{4,12},{... | collective-permute-start | bytes 1572872 | tf_op jit(solution)/shard_map/near0/ppermute | solution.py:34
  11.5 18.0 %collective-permute-start.7 = (bf16[512,1024]{1,0:T(8,128)(2,1)S(1)}, bf16[512,1024]{1,0:T(8,128)(2,1)S(1)}, u32[]{:S(2)}, u32[]{:S(2)}) collective-permute-start(bf16[512,1024]{1,0:T(8,128)(2,1)S(1)} %pad_maximum_fusion.1.refs_4_), channel_id=1, source_target_pairs={{8,16},{16,8},{9,17},{17,9},{10,18},{18,10},{11,19},{19,11},{12,20... | collective-permute-start | bytes 3145736 | tf_op jit(solution)/shard_map/twin0/ppermute | solution.py:34
  12.4 5.3 %collective-permute-start.1 = (bf16[2,256,128]{2,1,0:T(8,128)(2,1)S(1)}, bf16[2,256,128]{2,1,0:T(8,128)(2,1)S(1)}, u32[]{:S(2)}, u32[]{:S(2)}) collective-permute-start(bf16[2,256,128]{2,1,0:T(8,128)(2,1)S(1)} %bitcast.17), channel_id=1, source_target_pairs={{0,4},{4,0},{1,5},{5,1},{2,6},{6,2},{3,7},{7,3},{8,12},{12,8},{9,1... | collective-permute-start | bytes 393224 | tf_op jit(solution)/shard_map/keys/ppermute | solution.py:34
  23.1 20.7 %collective-permute-start.5 = (bf16[392,1024]{1,0:T(8,128)(2,1)S(1)}, bf16[392,1024]{1,0:T(8,128)(2,1)S(1)}, u32[]{:S(2)}, u32[]{:S(2)}) collective-permute-start(bf16[392,1024]{1,0:T(8,128)(2,1)S(1)} %attend.1.rest_0_), channel_id=1, source_target_pairs={{0,8},{24,16},{1,9},{25,17},{2,10},{26,18},{3,11},{27,19},{4,12},{... | collective-permute-start | bytes 2408456 | tf_op jit(solution)/shard_map/hand/ppermute | solution.py:34
  27.2 18.9 %collective-permute-start.4 = (bf16[392,1024]{1,0:T(8,128)(2,1)S(1)}, bf16[392,1024]{1,0:T(8,128)(2,1)S(1)}, u32[]{:S(2)}, u32[]{:S(2)}) collective-permute-start(bf16[392,1024]{1,0:T(8,128)(2,1)S(1)} %attend.1.rest_0_), channel_id=1, source_target_pairs={{0,4},{4,0},{1,5},{5,1},{2,6},{6,2},{3,7},{7,3},{8,12},{12,8},{9,1... | collective-permute-start | bytes 2408456 | tf_op jit(solution)/shard_map/rows/ppermute | solution.py:34
  28.8 0.7 collective-permute-start.6
  47.5 27.2 %collective-permute-start.8 = (bf16[704,1024]{1,0:T(8,128)(2,1)S(1)}, bf16[704,1024]{1,0:T(8,128)(2,1)S(1)}, u32[]{:S(2)}, u32[]{:S(2)}) collective-permute-start(bf16[704,1024]{1,0:T(8,128)(2,1)S(1)} %pack.2.refs_0_), channel_id=1, source_target_pairs={{0,1},{1,0},{2,3},{3,2},{4,5},{5,4},{6,7},{7,6},{8,9},{9,8},{10,11... | collective-permute-start | bytes 4325384 | tf_op jit(solution)/shard_map/own_rows/ppermute | solution.py:34
  47.6 27.1 %collective-permute-start.11 = (bf16[512,1024]{1,0:T(8,128)(2,1)S(1)}, bf16[512,1024]{1,0:T(8,128)(2,1)S(1)}, u32[]{:S(2)}, u32[]{:S(2)}) collective-permute-start(bf16[512,1024]{1,0:T(8,128)(2,1)S(1)} %pad_maximum_fusion.refs_5_), channel_id=1, source_target_pairs={{8,16},{16,8},{9,17},{17,9},{10,18},{18,10},{11,19},{19,11},{12,20... | collective-permute-start | bytes 3145736 | tf_op jit(solution)/shard_map/twin1/ppermute | solution.py:34
  48.4 26.3 %collective-permute-start.9 = (bf16[392,1024]{1,0:T(8,128)(2,1)S(1)}, bf16[392,1024]{1,0:T(8,128)(2,1)S(1)}, u32[]{:S(2)}, u32[]{:S(2)}) collective-permute-start(bf16[392,1024]{1,0:T(8,128)(2,1)S(1)} %collective-permute-done.5.rest_0_), channel_id=1, source_target_pairs={{0,4},{4,0},{1,5},{5,1},{2,6},{6,2},{3,7},{7,3},{8,12},{12,8},{9,1... | collective-permute-start | bytes 2408456 | tf_op jit(solution)/shard_map/other/ppermute | solution.py:34
  50.0 24.7 %collective-permute-start.10 = (bf16[512,768]{1,0:T(8,128)(2,1)S(1)}, bf16[512,768]{1,0:T(8,128)(2,1)S(1)}, u32[]{:S(2)}, u32[]{:S(2)}) collective-permute-start(bf16[512,768]{1,0:T(8,128)(2,1)S(1)} %pad_maximum_fusion.2), channel_id=1, source_target_pairs={{0,8},{24,16},{1,9},{25,17},{2,10},{26,18},{3,11},{27,19},{4,12},{... | collective-permute-start | bytes 2359304 | tf_op jit(solution)/shard_map/near1/ppermute | solution.py:34
  76.2 5.6 %collective-permute-start.12 = (bf16[704,1024]{1,0:T(8,128)(2,1)S(1)}, bf16[704,1024]{1,0:T(8,128)(2,1)S(1)}, u32[]{:S(2)}, u32[]{:S(2)}) collective-permute-start(bf16[704,1024]{1,0:T(8,128)(2,1)S(1)} %pack.3.refs_2_), channel_id=1, source_target_pairs={{0,1},{1,0},{2,3},{3,2},{4,5},{5,4},{6,7},{7,6},{8,9},{9,8},{10,11... | collective-permute-start | bytes 4325384 | tf_op jit(solution)/shard_map/other_rows/ppermute | solution.py:34
  76.3 22.9 %collective-permute-start.18 = (bf16[512,768]{1,0:T(8,128)(2,1)S(1)}, bf16[512,768]{1,0:T(8,128)(2,1)S(1)}, u32[]{:S(2)}, u32[]{:S(2)}) collective-permute-start(bf16[512,768]{1,0:T(8,128)(2,1)S(1)} %fusion), channel_id=1, source_target_pairs={{0,8},{24,16},{1,9},{25,17},{2,10},{26,18},{3,11},{27,19},{4,12},{... | collective-permute-start | bytes 2359304 | tf_op jit(solution)/shard_map/near2/ppermute | solution.py:34
  82.7 17.2 %collective-permute-start.15 = (bf16[704,256]{1,0:T(8,128)(2,1)S(1)}, bf16[704,256]{1,0:T(8,128)(2,1)S(1)}, u32[]{:S(2)}, u32[]{:S(2)}) collective-permute-start(bf16[704,256]{1,0:T(8,128)(2,1)S(1)} %get-tuple-element.70), channel_id=1, source_target_pairs={{0,2},{1,3},{2,0},{3,1},{4,6},{5,7},{6,4},{7,5},{8,10},{9,11},{10,... | collective-permute-start | bytes 1081352 | tf_op jit(solution)/shard_map/cross0/ppermute | solution.py:34
  84.2 17.1 %collective-permute-start.13 = (bf16[704,256]{1,0:T(8,128)(2,1)S(1)}, bf16[704,256]{1,0:T(8,128)(2,1)S(1)}, u32[]{:S(2)}, u32[]{:S(2)}) collective-permute-start(bf16[704,256]{1,0:T(8,128)(2,1)S(1)} %get-tuple-element.68), channel_id=1, source_target_pairs={{8,0},{16,24},{9,1},{17,25},{10,2},{18,26},{11,3},{19,27},{12,4},{... | collective-permute-start | bytes 1081352 | tf_op jit(solution)/shard_map/return0/ppermute | solution.py:34
  85.5 25.2 %collective-permute-start.17 = (bf16[512,768]{1,0:T(8,128)(2,1)S(1)}, bf16[512,768]{1,0:T(8,128)(2,1)S(1)}, u32[]{:S(2)}, u32[]{:S(2)}) collective-permute-start(bf16[512,768]{1,0:T(8,128)(2,1)S(1)} %collective-permute-done.10.refs_8_), channel_id=1, source_target_pairs={{8,16},{16,8},{9,17},{17,9},{10,18},{18,10},{11,19},{19,11},{12,20... | collective-permute-start | bytes 2359304 | tf_op jit(solution)/shard_map/far1/ppermute | solution.py:34
  99.2 15.7 %collective-permute-start.20 = (bf16[512,768]{1,0:T(8,128)(2,1)S(1)}, bf16[512,768]{1,0:T(8,128)(2,1)S(1)}, u32[]{:S(2)}, u32[]{:S(2)}) collective-permute-start(bf16[512,768]{1,0:T(8,128)(2,1)S(1)} %collective-permute-done.18.refs_8_), channel_id=1, source_target_pairs={{8,16},{16,8},{9,17},{17,9},{10,18},{18,10},{11,19},{19,11},{12,20... | collective-permute-start | bytes 2359304 | tf_op jit(solution)/shard_map/far2/ppermute | solution.py:34
  100.0 10.7 %collective-permute-start.16 = (bf16[352,256]{1,0:T(8,128)(2,1)S(1)}, bf16[352,256]{1,0:T(8,128)(2,1)S(1)}, u32[]{:S(2)}, u32[]{:S(2)}) collective-permute-start(bf16[352,256]{1,0:T(8,128)(2,1)S(1)} %slice.119), channel_id=1, source_target_pairs={{8,0},{16,24},{9,1},{17,25},{10,2},{18,26},{11,3},{19,27},{12,4},{... | collective-permute-start | bytes 540680 | tf_op jit(solution)/shard_map/return_after0/ppermute | solution.py:34
  111.5 20.5 %collective-permute-start.19 = (bf16[704,384]{1,0:T(8,128)(2,1)S(1)}, bf16[704,384]{1,0:T(8,128)(2,1)S(1)}, u32[]{:S(2)}, u32[]{:S(2)}) collective-permute-start(bf16[704,384]{1,0:T(8,128)(2,1)S(1)} %get-tuple-element.75), channel_id=1, source_target_pairs={{8,0},{16,24},{9,1},{17,25},{10,2},{18,26},{11,3},{19,27},{12,4},{... | collective-permute-start | bytes 1622024 | tf_op jit(solution)/shard_map/return1/ppermute | solution.py:34
  112.8 19.2 %collective-permute-start.22 = (bf16[704,384]{1,0:T(8,128)(2,1)S(1)}, bf16[704,384]{1,0:T(8,128)(2,1)S(1)}, u32[]{:S(2)}, u32[]{:S(2)}) collective-permute-start(bf16[704,384]{1,0:T(8,128)(2,1)S(1)} %get-tuple-element.80), channel_id=1, source_target_pairs={{0,2},{1,3},{2,0},{3,1},{4,6},{5,7},{6,4},{7,5},{8,10},{9,11},{10,... | collective-permute-start | bytes 1622024 | tf_op jit(solution)/shard_map/cross1/ppermute | solution.py:34
  114.4 17.6 %collective-permute-start.14 = (bf16[352,256]{1,0:T(8,128)(2,1)S(1)}, bf16[352,256]{1,0:T(8,128)(2,1)S(1)}, u32[]{:S(2)}, u32[]{:S(2)}) collective-permute-start(bf16[352,256]{1,0:T(8,128)(2,1)S(1)} %fusion.10), channel_id=1, source_target_pairs={{0,2},{1,3},{2,0},{3,1},{4,6},{5,7},{6,4},{7,5},{8,10},{9,11},{10,... | collective-permute-start | bytes 540680 | tf_op jit(solution)/shard_map/cross_after0/ppermute | solution.py:34
  115.9 37.4 %collective-permute-start.24 = (bf16[704,384]{1,0:T(8,128)(2,1)S(1)}, bf16[704,384]{1,0:T(8,128)(2,1)S(1)}, u32[]{:S(2)}, u32[]{:S(2)}) collective-permute-start(bf16[704,384]{1,0:T(8,128)(2,1)S(1)} %get-tuple-element.82), channel_id=1, source_target_pairs={{8,0},{16,24},{9,1},{17,25},{10,2},{18,26},{11,3},{19,27},{12,4},{... | collective-permute-start | bytes 1622024 | tf_op jit(solution)/shard_map/return2/ppermute | solution.py:34
  117.2 36.7 %collective-permute-start.26 = (bf16[704,384]{1,0:T(8,128)(2,1)S(1)}, bf16[704,384]{1,0:T(8,128)(2,1)S(1)}, u32[]{:S(2)}, u32[]{:S(2)}) collective-permute-start(bf16[704,384]{1,0:T(8,128)(2,1)S(1)} %get-tuple-element.85), channel_id=1, source_target_pairs={{0,2},{1,3},{2,0},{3,1},{4,6},{5,7},{6,4},{7,5},{8,10},{9,11},{10,... | collective-permute-start | bytes 1622024 | tf_op jit(solution)/shard_map/cross2/ppermute | solution.py:34
  132.2 21.0 %collective-permute-start.23 = (bf16[352,384]{1,0:T(8,128)(2,1)S(1)}, bf16[352,384]{1,0:T(8,128)(2,1)S(1)}, u32[]{:S(2)}, u32[]{:S(2)}) collective-permute-start(bf16[352,384]{1,0:T(8,128)(2,1)S(1)} %slice.127), channel_id=1, source_target_pairs={{8,0},{16,24},{9,1},{17,25},{10,2},{18,26},{11,3},{19,27},{12,4},{... | collective-permute-start | bytes 811016 | tf_op jit(solution)/shard_map/return_after1/ppermute | solution.py:34
  133.6 19.6 %collective-permute-start.21 = (bf16[352,384]{1,0:T(8,128)(2,1)S(1)}, bf16[352,384]{1,0:T(8,128)(2,1)S(1)}, u32[]{:S(2)}, u32[]{:S(2)}) collective-permute-start(bf16[352,384]{1,0:T(8,128)(2,1)S(1)} %fusion.8), channel_id=1, source_target_pairs={{0,2},{1,3},{2,0},{3,1},{4,6},{5,7},{6,4},{7,5},{8,10},{9,11},{10,... | collective-permute-start | bytes 811016 | tf_op jit(solution)/shard_map/cross_after1/ppermute | solution.py:34
  135.2 27.4 %collective-permute-start.28 = (bf16[176,512]{1,0:T(8,128)(2,1)S(1)}, bf16[176,512]{1,0:T(8,128)(2,1)S(1)}, u32[]{:S(2)}, u32[]{:S(2)}) collective-permute-start(bf16[176,512]{1,0:T(8,128)(2,1)S(1)} %get-tuple-element.104), channel_id=1, source_target_pairs={{0,1},{1,0},{2,3},{3,2},{4,5},{5,4},{6,7},{7,6},{8,9},{9,8},{10,11... | collective-permute-start | bytes 540680 | tf_op jit(solution)/shard_map/rest0/ppermute | solution.py:34
  153.4 6.8 %collective-permute-start.25 = (bf16[352,384]{1,0:T(8,128)(2,1)S(1)}, bf16[352,384]{1,0:T(8,128)(2,1)S(1)}, u32[]{:S(2)}, u32[]{:S(2)}) collective-permute-start(bf16[352,384]{1,0:T(8,128)(2,1)S(1)} %slice.131), channel_id=1, source_target_pairs={{0,2},{1,3},{2,0},{3,1},{4,6},{5,7},{6,4},{7,5},{8,10},{9,11},{10,... | collective-permute-start | bytes 811016 | tf_op jit(solution)/shard_map/cross_after2/ppermute | solution.py:34
  154.1 8.4 %collective-permute-start.27 = (bf16[352,384]{1,0:T(8,128)(2,1)S(1)}, bf16[352,384]{1,0:T(8,128)(2,1)S(1)}, u32[]{:S(2)}, u32[]{:S(2)}) collective-permute-start(bf16[352,384]{1,0:T(8,128)(2,1)S(1)} %slice.133), channel_id=1, source_target_pairs={{8,0},{16,24},{9,1},{17,25},{10,2},{18,26},{11,3},{19,27},{12,4},{... | collective-permute-start | bytes 811016 | tf_op jit(solution)/shard_map/return_after2/ppermute | solution.py:34
  155.6 7.1 %collective-permute-start.29 = (bf16[176,768]{1,0:T(8,128)(2,1)S(1)}, bf16[176,768]{1,0:T(8,128)(2,1)S(1)}, u32[]{:S(2)}, u32[]{:S(2)}) collective-permute-start(bf16[176,768]{1,0:T(8,128)(2,1)S(1)} %get-tuple-element.96), channel_id=1, source_target_pairs={{0,1},{1,0},{2,3},{3,2},{4,5},{5,4},{6,7},{7,6},{8,9},{9,8},{10,11... | collective-permute-start | bytes 811016 | tf_op jit(solution)/shard_map/rest1/ppermute | solution.py:34
  162.6 1.6 collective-permute-start.30
  (4 other events, 24.7 us)

commit v4 on v3

--- a/solution.py
+++ b/solution.py
@@ -44,11 +44,12 @@
 
 def prepare_kernel(n_blocks, base_ref, doc_ref, rescale_ref, *tables):
     slots = doc_ref.shape[1]
-    head = rescale_ref.shape[1]
-    half = head // 2
+    half = rescale_ref.shape[1]
+    head = 2 * half
+    rescale = jnp.concatenate([rescale_ref[...], rescale_ref[...]], axis=1)
     lane = lax.broadcasted_iota(jnp.int32, (1, head), 1)
     frequency = jnp.where(lane < half, lane, lane - half).astype(jnp.float32)
-    inverse = jnp.exp(-(frequency * (2.0 / head)) * math.log(ROPE_BASE)) / rescale_ref[...]
+    inverse = jnp.exp(-(frequency * (2.0 / head)) * math.log(ROPE_BASE)) / rescale
     sign = jnp.where(lane < half, -1.0, 1.0)
     docs = jnp.broadcast_to(doc_ref[...].astype(jnp.float32), (slots, slots))
     first = jnp.sum(jnp.where(docs < docs.T, 1.0, 0.0), axis=1, keepdims=True)
@@ -68,7 +69,7 @@
 def prepare(bases, block_rows, doc, rescale):
     vmem = pl.BlockSpec(memory_space=pltpu.VMEM)
     shapes = [
-        jax.ShapeDtypeStruct((rows, rescale.shape[1]), jnp.float32)
+        jax.ShapeDtypeStruct((rows, 2 * rescale.shape[1]), jnp.float32)
         for rows in [*block_rows, doc.shape[1]]
         for _ in range(2)
     ]
@@ -302,7 +303,7 @@
     ).astype(jnp.int32)
     weight = output_weight[0]
     width = weight.shape[1] // 2
-    place, is_inner, is_left, keep_at, give_at, weight, doubled = lax.optimization_barrier(
+    place, is_inner, is_left, keep_at, give_at, weight, factors = lax.optimization_barrier(
         (
             place,
             (dp == 1) | (dp == 2),
@@ -310,7 +311,7 @@
             (tp & 1) * width,
             (1 - (tp & 1)) * width,
             weight,
-            jnp.concatenate([rescale, rescale]).reshape(1, head),
+            rescale.reshape(1, head // 2),
         )
     )
 
@@ -358,7 +359,7 @@
     else:
         pairs = [lax.all_gather(raw, "ctx", axis=1, tiled=True)]
         block_rows = [n_ctx * long_rows, long_rows]
-    tables = prepare(place, block_rows, doc_ids, doubled)
+    tables = prepare(place, block_rows, doc_ids, factors)
     inputs = (place, q_long[0], q_short[0], short_key_value[0], doc_ids, tables, pairs)
     if n > 1:
         inputs = (after(place, both[1]), *inputs[1:])

time: 166 us -> 165 us (level)
  no operation moved by 1% of the time
where the time goes in v4:
time: 165 us
  waiting for transfers between devices  98.2 us (60%)
  starting transfers between devices  47 us (28%)
  Pallas kernels  12.6 us (8%)
  other arithmetic  3 us (2%)
  local copies, waits for them, and re-layouts  2.95 us (2%)
    ppermute x31, waiting for transfers between devices, send(): return lax.ppermute(x, axis, pairs)  98.2 us
    ppermute x31, starting transfers between devices, send(): return lax.ppermute(x, axis, pairs)  47 us
    pallas_call x1, Pallas kernels, attend(): pl.pallas_call(functools.partial(attend_kernel, len(pairs), len(tables)),...  5.35 us
  transfers between devices with their start and end apart: 31, of which 12 were waited for; matrix products, arithmetic and copies ran while one was open for 1% of the time, Pallas kernels for 6%

profile of v4, /device:TPU:0, one launch (start us, length us, event | category | flops | bytes accessed | tf_op | source)
XLA Modules:
  0.0 165.0 jit_solution(4372354146348235267)
XLA Ops:
  0.8 2.6 %constant_dynamic-slice_fusion.2 = (bf16[256,1024]{1,0:T(8,128)(2,1)S(1)}, bf16[256,1024]{1,0:T(8,128)(2,1)S(1)}, bf16[256,1024]{1,0:T(8,128)(2,1)S(1)}, bf16[256,1024]{1,0:T(8,128)(2,1)S(1)}) fusion(bf16[256,4096]{1,0:T(8,128)(2,1)} %bitcast.20, s32[]{:T(128)S(6)} %select_n.94, s32[]{:T(128)S(6)} %add.33, s32[]{:T(128)S(6)} %add.32, s32[]{:T(128)S(6)} %select_n.93), kind=kLoop, calls=%fused_computation.54 | loop fusion | bytes 4194320 | tf_op jit(solution)/shard_map/slice | solution.py:327
  4.0 1.5 collective-permute-done.2
  5.5 5.0 %collective-permute-start.3 = (bf16[512,512]{1,0:T(8,128)(2,1)S(1)}, bf16[512,512]{1,0:T(8,128)(2,1)S(1)}, u32[]{:S(2)}, u32[]{:S(2)}) collective-permute-start(bf16[512,512]{1,0:T(8,128)(2,1)S(1)} %get-tuple-element.60), channel_id=1, source_target_pairs={{0,8},{24,16},{1,9},{25,17},{2,10},{26,18},{3,11},{27,19},{4,12},{... | collective-permute-start | bytes 1572872 | tf_op jit(solution)/shard_map/near0/ppermute | solution.py:34
  11.6 1.6 collective-permute-start.1
  13.1 1.8 %prepare.1 = (f32[256,128]{1,0:T(8,128)S(1)}, f32[256,128]{1,0:T(8,128)S(1)}, f32[256,128]{1,0:T(8,128)S(1)}, f32[256,128]{1,0:T(8,128)S(1)}, f32[128,128]{1,0:T(8,128)S(1)}, /*index=5*/f32[128,128]{1,0:T(8,128)S(1)}) custom-call(s32[8]{0:T(128)S(1)} %stack.28.base_ref.scalar_ref.plane_ref, s32[1,128]{1,0:T(1,128)S(1)} %copy-done.4, f32[1,64]{1,0:T(1,128)S(1)} %bitcast.19), custom_call_target="tpu_custom_call" | custom-call | tf_op jit(solution)/shard_map/prepare/pallas_call | solution.py:76
  15.0 1.8 %collective-permute-done.1.rest_7_ = bf16[2,256,128]{2,1,0:T(8,128)(2,1)S(1)} collective-permute-done((bf16[2,256,128]{2,1,0:T(8,128)(2,1)S(1)}, bf16[2,256,128]{2,1,0:T(8,128)(2,1)S(1)}, u32[]{:S(2)}, u32[]{:S(2)}) %collective-permute-start.1) | collective-permute-done | bytes 131104 | tf_op jit(solution)/shard_map/keys/ppermute | solution.py:34
  16.9 5.3 %attend.1.rest_0_ = bf16[392,1024]{1,0:T(8,128)(2,1)S(1)} custom-call(s32[8]{0:T(128)S(1)} %stack.28.base_ref.scalar_ref.plane_ref, bf16[256,1024]{1,0:T(8,128)(2,1)S(1)} %bitcast.14, bf16[128,1024]{1,0:T(8,128)(2,1)S(1)} %bitcast.15, bf16[2,128,128]{2,1,0:T(8,128)(2,1)S(1)} %bitcast.18, s32[1,128]{1,0:T(1,128)S(1)} %copy-done.4, ...), custom_call_target="tpu_custom_call" | custom-call | tf_op jit(solution)/shard_map/attend/pallas_call | solution.py:151
  22.3 4.2 %collective-permute-start.5 = (bf16[392,1024]{1,0:T(8,128)(2,1)S(1)}, bf16[392,1024]{1,0:T(8,128)(2,1)S(1)}, u32[]{:S(2)}, u32[]{:S(2)}) collective-permute-start(bf16[392,1024]{1,0:T(8,128)(2,1)S(1)} %attend.1.rest_0_), channel_id=1, source_target_pairs={{0,8},{24,16},{1,9},{25,17},{2,10},{26,18},{3,11},{27,19},{4,12},{... | collective-permute-start | bytes 2408456 | tf_op jit(solution)/shard_map/hand/ppermute | solution.py:34
  26.4 1.6 collective-permute-start.4
  28.7 14.3 %collective-permute-done.5.rest_0_ = bf16[392,1024]{1,0:T(8,128)(2,1)S(1)} collective-permute-done((bf16[392,1024]{1,0:T(8,128)(2,1)S(1)}, bf16[392,1024]{1,0:T(8,128)(2,1)S(1)}, u32[]{:S(2)}, u32[]{:S(2)}) %collective-permute-start.5) | collective-permute-done | bytes 802848 | tf_op jit(solution)/shard_map/hand/ppermute | solution.py:34
  43.0 2.3 %collective-permute-done.4.rest_1_ = bf16[392,1024]{1,0:T(8,128)(2,1)S(1)} collective-permute-done((bf16[392,1024]{1,0:T(8,128)(2,1)S(1)}, bf16[392,1024]{1,0:T(8,128)(2,1)S(1)}, u32[]{:S(2)}, u32[]{:S(2)}) %collective-permute-start.4) | collective-permute-done | bytes 802848 | tf_op jit(solution)/shard_map/rows/ppermute | solution.py:34
  45.3 1.4 pack.2.refs_0_
  47.6 1.6 collective-permute-start.9
  49.2 7.9 %collective-permute-start.10 = (bf16[512,768]{1,0:T(8,128)(2,1)S(1)}, bf16[512,768]{1,0:T(8,128)(2,1)S(1)}, u32[]{:S(2)}, u32[]{:S(2)}) collective-permute-start(bf16[512,768]{1,0:T(8,128)(2,1)S(1)} %pad_maximum_fusion.2), channel_id=1, source_target_pairs={{0,8},{24,16},{1,9},{25,17},{2,10},{26,18},{3,11},{27,19},{4,12},{... | collective-permute-start | bytes 2359304 | tf_op jit(solution)/shard_map/near1/ppermute | solution.py:34
  57.1 16.8 %collective-permute-done.10.refs_8_ = bf16[512,768]{1,0:T(8,128)(2,1)S(1)} collective-permute-done((bf16[512,768]{1,0:T(8,128)(2,1)S(1)}, bf16[512,768]{1,0:T(8,128)(2,1)S(1)}, u32[]{:S(2)}, u32[]{:S(2)}) %collective-permute-start.10) | collective-permute-done | bytes 786464 | tf_op jit(solution)/shard_map/near1/ppermute | solution.py:34
  74.0 1.4 pack.3.refs_2_
  75.5 5.5 %collective-permute-start.18 = (bf16[512,768]{1,0:T(8,128)(2,1)S(1)}, bf16[512,768]{1,0:T(8,128)(2,1)S(1)}, u32[]{:S(2)}, u32[]{:S(2)}) collective-permute-start(bf16[512,768]{1,0:T(8,128)(2,1)S(1)} %fusion), channel_id=1, source_target_pairs={{0,8},{24,16},{1,9},{25,17},{2,10},{26,18},{3,11},{27,19},{4,12},{... | collective-permute-start | bytes 2359304 | tf_op jit(solution)/shard_map/near2/ppermute | solution.py:34
  81.9 1.6 collective-permute-start.15
  85.5 12.9 %collective-permute-done.18.refs_8_ = bf16[512,768]{1,0:T(8,128)(2,1)S(1)} collective-permute-done((bf16[512,768]{1,0:T(8,128)(2,1)S(1)}, bf16[512,768]{1,0:T(8,128)(2,1)S(1)}, u32[]{:S(2)}, u32[]{:S(2)}) %collective-permute-start.18) | collective-permute-done | bytes 786464 | tf_op jit(solution)/shard_map/near2/ppermute | solution.py:34
  99.2 1.3 collective-permute-start.16
  100.6 9.3 %collective-permute-done.16 = bf16[352,256]{1,0:T(8,128)(2,1)S(1)} collective-permute-done((bf16[352,256]{1,0:T(8,128)(2,1)S(1)}, bf16[352,256]{1,0:T(8,128)(2,1)S(1)}, u32[]{:S(2)}, u32[]{:S(2)}) %collective-permute-start.16) | collective-permute-done | bytes 180256 | tf_op jit(solution)/shard_map/return_after0/ppermute | solution.py:34
  110.7 1.3 collective-permute-start.19
  112.0 1.6 collective-permute-start.22
  115.1 1.3 collective-permute-start.24
  116.4 1.6 collective-permute-start.26
  118.0 13.2 %collective-permute-done.14 = bf16[352,256]{1,0:T(8,128)(2,1)S(1)} collective-permute-done((bf16[352,256]{1,0:T(8,128)(2,1)S(1)}, bf16[352,256]{1,0:T(8,128)(2,1)S(1)}, u32[]{:S(2)}, u32[]{:S(2)}) %collective-permute-start.14) | collective-permute-done | bytes 180256 | tf_op jit(solution)/shard_map/cross_after0/ppermute | solution.py:34
  131.4 1.3 collective-permute-start.23
  132.8 1.6 collective-permute-start.21
  134.5 17.8 %collective-permute-done.23 = bf16[352,384]{1,0:T(8,128)(2,1)S(1)} collective-permute-done((bf16[352,384]{1,0:T(8,128)(2,1)S(1)}, bf16[352,384]{1,0:T(8,128)(2,1)S(1)}, u32[]{:S(2)}, u32[]{:S(2)}) %collective-permute-start.23) | collective-permute-done | bytes 270368 | tf_op jit(solution)/shard_map/return_after1/ppermute | solution.py:34
  154.9 4.5 %collective-permute-done.25 = bf16[352,384]{1,0:T(8,128)(2,1)S(1)} collective-permute-done((bf16[352,384]{1,0:T(8,128)(2,1)S(1)}, bf16[352,384]{1,0:T(8,128)(2,1)S(1)}, u32[]{:S(2)}, u32[]{:S(2)}) %collective-permute-start.25) | collective-permute-done | bytes 270368 | tf_op jit(solution)/shard_map/cross_after2/ppermute | solution.py:34
  159.4 2.2 %collective-permute-done.27 = bf16[352,384]{1,0:T(8,128)(2,1)S(1)} collective-permute-done((bf16[352,384]{1,0:T(8,128)(2,1)S(1)}, bf16[352,384]{1,0:T(8,128)(2,1)S(1)}, u32[]{:S(2)}, u32[]{:S(2)}) %collective-permute-start.27) | collective-permute-done | bytes 270368 | tf_op jit(solution)/shard_map/return_after2/ppermute | solution.py:34
  161.9 1.5 collective-permute-done.30
  (83 shorter events, 14.2 us)
Async XLA Ops:
  3.4 2.1 %collective-permute-start.2 = (bf16[256,1024]{1,0:T(8,128)(2,1)S(1)}, bf16[256,1024]{1,0:T(8,128)(2,1)S(1)}, u32[]{:S(2)}, u32[]{:S(2)}) collective-permute-start(bf16[256,1024]{1,0:T(8,128)(2,1)S(1)} %get-tuple-element.87), channel_id=1, source_target_pairs={{0,1},{1,0},{2,3},{3,2},{4,5},{5,4},{6,7},{7,6},{8,9},{9,8},{10,11... | collective-permute-start | bytes 1572872 | tf_op jit(solution)/shard_map/trade0/ppermute | solution.py:34
  3.9 11.1 %collective-permute-start = (bf16[256,1024]{1,0:T(8,128)(2,1)S(1)}, bf16[256,1024]{1,0:T(8,128)(2,1)S(1)}, u32[]{:S(2)}, u32[]{:S(2)}) collective-permute-start(bf16[256,1024]{1,0:T(8,128)(2,1)S(1)} %get-tuple-element.88), channel_id=1, source_target_pairs={{0,1},{1,0},{2,3},{3,2},{4,5},{5,4},{6,7},{7,6},{8,9},{9,8},{10,11... | collective-permute-start | bytes 1572872 | tf_op jit(solution)/shard_map/trade1/ppermute | solution.py:34
  5.5 7.6 %copy-start.4 = (s32[1,128]{1,0:T(1,128)S(1)}, s32[1,128]{1,0:T(1,128)}, u32[]{:S(2)}) copy-start(s32[1,128]{1,0:T(1,128)} %doc_ref.3) | copy-start | bytes 1540
  5.5 16.7 %collective-permute-start.3 = (bf16[512,512]{1,0:T(8,128)(2,1)S(1)}, bf16[512,512]{1,0:T(8,128)(2,1)S(1)}, u32[]{:S(2)}, u32[]{:S(2)}) collective-permute-start(bf16[512,512]{1,0:T(8,128)(2,1)S(1)} %get-tuple-element.60), channel_id=1, source_target_pairs={{0,8},{24,16},{1,9},{25,17},{2,10},{26,18},{3,11},{27,19},{4,12},{... | collective-permute-start | bytes 1572872 | tf_op jit(solution)/shard_map/near0/ppermute | solution.py:34
  10.7 18.0 %collective-permute-start.7 = (bf16[512,1024]{1,0:T(8,128)(2,1)S(1)}, bf16[512,1024]{1,0:T(8,128)(2,1)S(1)}, u32[]{:S(2)}, u32[]{:S(2)}) collective-permute-start(bf16[512,1024]{1,0:T(8,128)(2,1)S(1)} %pad_maximum_fusion.1.refs_4_), channel_id=1, source_target_pairs={{8,16},{16,8},{9,17},{17,9},{10,18},{18,10},{11,19},{19,11},{12,20... | collective-permute-start | bytes 3145736 | tf_op jit(solution)/shard_map/twin0/ppermute | solution.py:34
  11.6 5.3 %collective-permute-start.1 = (bf16[2,256,128]{2,1,0:T(8,128)(2,1)S(1)}, bf16[2,256,128]{2,1,0:T(8,128)(2,1)S(1)}, u32[]{:S(2)}, u32[]{:S(2)}) collective-permute-start(bf16[2,256,128]{2,1,0:T(8,128)(2,1)S(1)} %bitcast.16), channel_id=1, source_target_pairs={{0,4},{4,0},{1,5},{5,1},{2,6},{6,2},{3,7},{7,3},{8,12},{12,8},{9,1... | collective-permute-start | bytes 393224 | tf_op jit(solution)/shard_map/keys/ppermute | solution.py:34
  22.3 20.7 %collective-permute-start.5 = (bf16[392,1024]{1,0:T(8,128)(2,1)S(1)}, bf16[392,1024]{1,0:T(8,128)(2,1)S(1)}, u32[]{:S(2)}, u32[]{:S(2)}) collective-permute-start(bf16[392,1024]{1,0:T(8,128)(2,1)S(1)} %attend.1.rest_0_), channel_id=1, source_target_pairs={{0,8},{24,16},{1,9},{25,17},{2,10},{26,18},{3,11},{27,19},{4,12},{... | collective-permute-start | bytes 2408456 | tf_op jit(solution)/shard_map/hand/ppermute | solution.py:34
  26.4 18.9 %collective-permute-start.4 = (bf16[392,1024]{1,0:T(8,128)(2,1)S(1)}, bf16[392,1024]{1,0:T(8,128)(2,1)S(1)}, u32[]{:S(2)}, u32[]{:S(2)}) collective-permute-start(bf16[392,1024]{1,0:T(8,128)(2,1)S(1)} %attend.1.rest_0_), channel_id=1, source_target_pairs={{0,4},{4,0},{1,5},{5,1},{2,6},{6,2},{3,7},{7,3},{8,12},{12,8},{9,1... | collective-permute-start | bytes 2408456 | tf_op jit(solution)/shard_map/rows/ppermute | solution.py:34
  28.0 0.7 collective-permute-start.6
  46.8 27.2 %collective-permute-start.8 = (bf16[704,1024]{1,0:T(8,128)(2,1)S(1)}, bf16[704,1024]{1,0:T(8,128)(2,1)S(1)}, u32[]{:S(2)}, u32[]{:S(2)}) collective-permute-start(bf16[704,1024]{1,0:T(8,128)(2,1)S(1)} %pack.2.refs_0_), channel_id=1, source_target_pairs={{0,1},{1,0},{2,3},{3,2},{4,5},{5,4},{6,7},{7,6},{8,9},{9,8},{10,11... | collective-permute-start | bytes 4325384 | tf_op jit(solution)/shard_map/own_rows/ppermute | solution.py:34
  46.8 27.1 %collective-permute-start.11 = (bf16[512,1024]{1,0:T(8,128)(2,1)S(1)}, bf16[512,1024]{1,0:T(8,128)(2,1)S(1)}, u32[]{:S(2)}, u32[]{:S(2)}) collective-permute-start(bf16[512,1024]{1,0:T(8,128)(2,1)S(1)} %pad_maximum_fusion.refs_5_), channel_id=1, source_target_pairs={{8,16},{16,8},{9,17},{17,9},{10,18},{18,10},{11,19},{19,11},{12,20... | collective-permute-start | bytes 3145736 | tf_op jit(solution)/shard_map/twin1/ppermute | solution.py:34
  47.6 26.3 %collective-permute-start.9 = (bf16[392,1024]{1,0:T(8,128)(2,1)S(1)}, bf16[392,1024]{1,0:T(8,128)(2,1)S(1)}, u32[]{:S(2)}, u32[]{:S(2)}) collective-permute-start(bf16[392,1024]{1,0:T(8,128)(2,1)S(1)} %collective-permute-done.5.rest_0_), channel_id=1, source_target_pairs={{0,4},{4,0},{1,5},{5,1},{2,6},{6,2},{3,7},{7,3},{8,12},{12,8},{9,1... | collective-permute-start | bytes 2408456 | tf_op jit(solution)/shard_map/other/ppermute | solution.py:34
  49.2 24.7 %collective-permute-start.10 = (bf16[512,768]{1,0:T(8,128)(2,1)S(1)}, bf16[512,768]{1,0:T(8,128)(2,1)S(1)}, u32[]{:S(2)}, u32[]{:S(2)}) collective-permute-start(bf16[512,768]{1,0:T(8,128)(2,1)S(1)} %pad_maximum_fusion.2), channel_id=1, source_target_pairs={{0,8},{24,16},{1,9},{25,17},{2,10},{26,18},{3,11},{27,19},{4,12},{... | collective-permute-start | bytes 2359304 | tf_op jit(solution)/shard_map/near1/ppermute | solution.py:34
  75.4 5.6 %collective-permute-start.12 = (bf16[704,1024]{1,0:T(8,128)(2,1)S(1)}, bf16[704,1024]{1,0:T(8,128)(2,1)S(1)}, u32[]{:S(2)}, u32[]{:S(2)}) collective-permute-start(bf16[704,1024]{1,0:T(8,128)(2,1)S(1)} %pack.3.refs_2_), channel_id=1, source_target_pairs={{0,1},{1,0},{2,3},{3,2},{4,5},{5,4},{6,7},{7,6},{8,9},{9,8},{10,11... | collective-permute-start | bytes 4325384 | tf_op jit(solution)/shard_map/other_rows/ppermute | solution.py:34
  75.5 22.9 %collective-permute-start.18 = (bf16[512,768]{1,0:T(8,128)(2,1)S(1)}, bf16[512,768]{1,0:T(8,128)(2,1)S(1)}, u32[]{:S(2)}, u32[]{:S(2)}) collective-permute-start(bf16[512,768]{1,0:T(8,128)(2,1)S(1)} %fusion), channel_id=1, source_target_pairs={{0,8},{24,16},{1,9},{25,17},{2,10},{26,18},{3,11},{27,19},{4,12},{... | collective-permute-start | bytes 2359304 | tf_op jit(solution)/shard_map/near2/ppermute | solution.py:34
  81.9 17.2 %collective-permute-start.15 = (bf16[704,256]{1,0:T(8,128)(2,1)S(1)}, bf16[704,256]{1,0:T(8,128)(2,1)S(1)}, u32[]{:S(2)}, u32[]{:S(2)}) collective-permute-start(bf16[704,256]{1,0:T(8,128)(2,1)S(1)} %get-tuple-element.70), channel_id=1, source_target_pairs={{0,2},{1,3},{2,0},{3,1},{4,6},{5,7},{6,4},{7,5},{8,10},{9,11},{10,... | collective-permute-start | bytes 1081352 | tf_op jit(solution)/shard_map/cross0/ppermute | solution.py:34
  83.4 17.1 %collective-permute-start.13 = (bf16[704,256]{1,0:T(8,128)(2,1)S(1)}, bf16[704,256]{1,0:T(8,128)(2,1)S(1)}, u32[]{:S(2)}, u32[]{:S(2)}) collective-permute-start(bf16[704,256]{1,0:T(8,128)(2,1)S(1)} %get-tuple-element.68), channel_id=1, source_target_pairs={{8,0},{16,24},{9,1},{17,25},{10,2},{18,26},{11,3},{19,27},{12,4},{... | collective-permute-start | bytes 1081352 | tf_op jit(solution)/shard_map/return0/ppermute | solution.py:34
  84.7 25.2 %collective-permute-start.17 = (bf16[512,768]{1,0:T(8,128)(2,1)S(1)}, bf16[512,768]{1,0:T(8,128)(2,1)S(1)}, u32[]{:S(2)}, u32[]{:S(2)}) collective-permute-start(bf16[512,768]{1,0:T(8,128)(2,1)S(1)} %collective-permute-done.10.refs_8_), channel_id=1, source_target_pairs={{8,16},{16,8},{9,17},{17,9},{10,18},{18,10},{11,19},{19,11},{12,20... | collective-permute-start | bytes 2359304 | tf_op jit(solution)/shard_map/far1/ppermute | solution.py:34
  98.4 15.7 %collective-permute-start.20 = (bf16[512,768]{1,0:T(8,128)(2,1)S(1)}, bf16[512,768]{1,0:T(8,128)(2,1)S(1)}, u32[]{:S(2)}, u32[]{:S(2)}) collective-permute-start(bf16[512,768]{1,0:T(8,128)(2,1)S(1)} %collective-permute-done.18.refs_8_), channel_id=1, source_target_pairs={{8,16},{16,8},{9,17},{17,9},{10,18},{18,10},{11,19},{19,11},{12,20... | collective-permute-start | bytes 2359304 | tf_op jit(solution)/shard_map/far2/ppermute | solution.py:34
  99.2 10.7 %collective-permute-start.16 = (bf16[352,256]{1,0:T(8,128)(2,1)S(1)}, bf16[352,256]{1,0:T(8,128)(2,1)S(1)}, u32[]{:S(2)}, u32[]{:S(2)}) collective-permute-start(bf16[352,256]{1,0:T(8,128)(2,1)S(1)} %slice.119), channel_id=1, source_target_pairs={{8,0},{16,24},{9,1},{17,25},{10,2},{18,26},{11,3},{19,27},{12,4},{... | collective-permute-start | bytes 540680 | tf_op jit(solution)/shard_map/return_after0/ppermute | solution.py:34
  110.7 20.5 %collective-permute-start.19 = (bf16[704,384]{1,0:T(8,128)(2,1)S(1)}, bf16[704,384]{1,0:T(8,128)(2,1)S(1)}, u32[]{:S(2)}, u32[]{:S(2)}) collective-permute-start(bf16[704,384]{1,0:T(8,128)(2,1)S(1)} %get-tuple-element.75), channel_id=1, source_target_pairs={{8,0},{16,24},{9,1},{17,25},{10,2},{18,26},{11,3},{19,27},{12,4},{... | collective-permute-start | bytes 1622024 | tf_op jit(solution)/shard_map/return1/ppermute | solution.py:34
  112.0 19.2 %collective-permute-start.22 = (bf16[704,384]{1,0:T(8,128)(2,1)S(1)}, bf16[704,384]{1,0:T(8,128)(2,1)S(1)}, u32[]{:S(2)}, u32[]{:S(2)}) collective-permute-start(bf16[704,384]{1,0:T(8,128)(2,1)S(1)} %get-tuple-element.80), channel_id=1, source_target_pairs={{0,2},{1,3},{2,0},{3,1},{4,6},{5,7},{6,4},{7,5},{8,10},{9,11},{10,... | collective-permute-start | bytes 1622024 | tf_op jit(solution)/shard_map/cross1/ppermute | solution.py:34
  113.6 17.6 %collective-permute-start.14 = (bf16[352,256]{1,0:T(8,128)(2,1)S(1)}, bf16[352,256]{1,0:T(8,128)(2,1)S(1)}, u32[]{:S(2)}, u32[]{:S(2)}) collective-permute-start(bf16[352,256]{1,0:T(8,128)(2,1)S(1)} %fusion.10), channel_id=1, source_target_pairs={{0,2},{1,3},{2,0},{3,1},{4,6},{5,7},{6,4},{7,5},{8,10},{9,11},{10,... | collective-permute-start | bytes 540680 | tf_op jit(solution)/shard_map/cross_after0/ppermute | solution.py:34
  115.1 37.4 %collective-permute-start.24 = (bf16[704,384]{1,0:T(8,128)(2,1)S(1)}, bf16[704,384]{1,0:T(8,128)(2,1)S(1)}, u32[]{:S(2)}, u32[]{:S(2)}) collective-permute-start(bf16[704,384]{1,0:T(8,128)(2,1)S(1)} %get-tuple-element.82), channel_id=1, source_target_pairs={{8,0},{16,24},{9,1},{17,25},{10,2},{18,26},{11,3},{19,27},{12,4},{... | collective-permute-start | bytes 1622024 | tf_op jit(solution)/shard_map/return2/ppermute | solution.py:34
  116.4 36.7 %collective-permute-start.26 = (bf16[704,384]{1,0:T(8,128)(2,1)S(1)}, bf16[704,384]{1,0:T(8,128)(2,1)S(1)}, u32[]{:S(2)}, u32[]{:S(2)}) collective-permute-start(bf16[704,384]{1,0:T(8,128)(2,1)S(1)} %get-tuple-element.85), channel_id=1, source_target_pairs={{0,2},{1,3},{2,0},{3,1},{4,6},{5,7},{6,4},{7,5},{8,10},{9,11},{10,... | collective-permute-start | bytes 1622024 | tf_op jit(solution)/shard_map/cross2/ppermute | solution.py:34
  131.4 21.0 %collective-permute-start.23 = (bf16[352,384]{1,0:T(8,128)(2,1)S(1)}, bf16[352,384]{1,0:T(8,128)(2,1)S(1)}, u32[]{:S(2)}, u32[]{:S(2)}) collective-permute-start(bf16[352,384]{1,0:T(8,128)(2,1)S(1)} %slice.127), channel_id=1, source_target_pairs={{8,0},{16,24},{9,1},{17,25},{10,2},{18,26},{11,3},{19,27},{12,4},{... | collective-permute-start | bytes 811016 | tf_op jit(solution)/shard_map/return_after1/ppermute | solution.py:34
  132.8 19.6 %collective-permute-start.21 = (bf16[352,384]{1,0:T(8,128)(2,1)S(1)}, bf16[352,384]{1,0:T(8,128)(2,1)S(1)}, u32[]{:S(2)}, u32[]{:S(2)}) collective-permute-start(bf16[352,384]{1,0:T(8,128)(2,1)S(1)} %fusion.8), channel_id=1, source_target_pairs={{0,2},{1,3},{2,0},{3,1},{4,6},{5,7},{6,4},{7,5},{8,10},{9,11},{10,... | collective-permute-start | bytes 811016 | tf_op jit(solution)/shard_map/cross_after1/ppermute | solution.py:34
  134.5 27.4 %collective-permute-start.28 = (bf16[176,512]{1,0:T(8,128)(2,1)S(1)}, bf16[176,512]{1,0:T(8,128)(2,1)S(1)}, u32[]{:S(2)}, u32[]{:S(2)}) collective-permute-start(bf16[176,512]{1,0:T(8,128)(2,1)S(1)} %get-tuple-element.104), channel_id=1, source_target_pairs={{0,1},{1,0},{2,3},{3,2},{4,5},{5,4},{6,7},{7,6},{8,9},{9,8},{10,11... | collective-permute-start | bytes 540680 | tf_op jit(solution)/shard_map/rest0/ppermute | solution.py:34
  152.6 6.8 %collective-permute-start.25 = (bf16[352,384]{1,0:T(8,128)(2,1)S(1)}, bf16[352,384]{1,0:T(8,128)(2,1)S(1)}, u32[]{:S(2)}, u32[]{:S(2)}) collective-permute-start(bf16[352,384]{1,0:T(8,128)(2,1)S(1)} %slice.131), channel_id=1, source_target_pairs={{0,2},{1,3},{2,0},{3,1},{4,6},{5,7},{6,4},{7,5},{8,10},{9,11},{10,... | collective-permute-start | bytes 811016 | tf_op jit(solution)/shard_map/cross_after2/ppermute | solution.py:34
  153.3 8.4 %collective-permute-start.27 = (bf16[352,384]{1,0:T(8,128)(2,1)S(1)}, bf16[352,384]{1,0:T(8,128)(2,1)S(1)}, u32[]{:S(2)}, u32[]{:S(2)}) collective-permute-start(bf16[352,384]{1,0:T(8,128)(2,1)S(1)} %slice.133), channel_id=1, source_target_pairs={{8,0},{16,24},{9,1},{17,25},{10,2},{18,26},{11,3},{19,27},{12,4},{... | collective-permute-start | bytes 811016 | tf_op jit(solution)/shard_map/return_after2/ppermute | solution.py:34
  154.8 7.1 %collective-permute-start.29 = (bf16[176,768]{1,0:T(8,128)(2,1)S(1)}, bf16[176,768]{1,0:T(8,128)(2,1)S(1)}, u32[]{:S(2)}, u32[]{:S(2)}) collective-permute-start(bf16[176,768]{1,0:T(8,128)(2,1)S(1)} %get-tuple-element.96), channel_id=1, source_target_pairs={{0,1},{1,0},{2,3},{3,2},{4,5},{5,4},{6,7},{7,6},{8,9},{9,8},{10,11... | collective-permute-start | bytes 811016 | tf_op jit(solution)/shard_map/rest1/ppermute | solution.py:34
  161.8 1.6 collective-permute-start.30
  (5 other events, 32.3 us)

commit v5 on v4

--- a/solution.py
+++ b/solution.py
@@ -433,12 +433,12 @@
             seconds.append(second_hop(i - 1, hops[i - 1], *gates)) if i < DEEP else None
             leaving = [seconds[-1][k] for k in ("kept", "mine") if k in seconds[-1]]
             later = [near[i + 1]] if i + 1 < n else []
-            far[i] = after(far[i], *leaving, *later)
+            far[i] = after(far[i], *leaving, *later, *([gate] if i > 1 else []))
             forward(i + 1)
         hop, gate = first_hop(i)
         hops.append(hop)
     for i in range(len(seconds), n):
-        gates = list(seconds[-1].values()) if i else []
+        gates = [v for k, v in seconds[-1].items() if k in ("kept", "mine")] if i else []
         seconds.append(second_hop(i, hops[i], gate, *gates))
     quarter = half // 2
     mine, theirs = [], []

time: 165 us -> 165 us (level)
  no operation moved by 1% of the time
where the time goes in v5:
time: 165 us
  waiting for transfers between devices  98.2 us (60%)
  starting transfers between devices  47 us (28%)
  Pallas kernels  12.6 us (8%)
  other arithmetic  3 us (2%)
  local copies, waits for them, and re-layouts  2.95 us (2%)
    ppermute x31, waiting for transfers between devices, send(): return lax.ppermute(x, axis, pairs)  98.2 us
    ppermute x31, starting transfers between devices, send(): return lax.ppermute(x, axis, pairs)  47 us
    pallas_call x1, Pallas kernels, attend(): pl.pallas_call(functools.partial(attend_kernel, len(pairs), len(tables)),...  5.35 us
  transfers between devices with their start and end apart: 31, of which 12 were waited for; matrix products, arithmetic and copies ran while one was open for 1% of the time, Pallas kernels for 6%

profile of v5, /device:TPU:0, one launch (start us, length us, event | category | flops | bytes accessed | tf_op | source)
XLA Modules:
  0.0 165.0 jit_solution(11935883610636985392)
XLA Ops:
  0.8 2.6 %constant_dynamic-slice_fusion.2 = (bf16[256,1024]{1,0:T(8,128)(2,1)S(1)}, bf16[256,1024]{1,0:T(8,128)(2,1)S(1)}, bf16[256,1024]{1,0:T(8,128)(2,1)S(1)}, bf16[256,1024]{1,0:T(8,128)(2,1)S(1)}) fusion(bf16[256,4096]{1,0:T(8,128)(2,1)} %bitcast.20, s32[]{:T(128)S(6)} %select_n.94, s32[]{:T(128)S(6)} %add.33, s32[]{:T(128)S(6)} %add.32, s32[]{:T(128)S(6)} %select_n.93), kind=kLoop, calls=%fused_computation.54 | loop fusion | bytes 4194320 | tf_op jit(solution)/shard_map/slice | solution.py:327
  4.0 1.5 collective-permute-done.2
  5.5 5.0 %collective-permute-start.3 = (bf16[512,512]{1,0:T(8,128)(2,1)S(1)}, bf16[512,512]{1,0:T(8,128)(2,1)S(1)}, u32[]{:S(2)}, u32[]{:S(2)}) collective-permute-start(bf16[512,512]{1,0:T(8,128)(2,1)S(1)} %get-tuple-element.60), channel_id=1, source_target_pairs={{0,8},{24,16},{1,9},{25,17},{2,10},{26,18},{3,11},{27,19},{4,12},{... | collective-permute-start | bytes 1572872 | tf_op jit(solution)/shard_map/near0/ppermute | solution.py:34
  11.6 1.6 collective-permute-start.1
  13.1 1.8 %prepare.1 = (f32[256,128]{1,0:T(8,128)S(1)}, f32[256,128]{1,0:T(8,128)S(1)}, f32[256,128]{1,0:T(8,128)S(1)}, f32[256,128]{1,0:T(8,128)S(1)}, f32[128,128]{1,0:T(8,128)S(1)}, /*index=5*/f32[128,128]{1,0:T(8,128)S(1)}) custom-call(s32[8]{0:T(128)S(1)} %stack.28.base_ref.scalar_ref.plane_ref, s32[1,128]{1,0:T(1,128)S(1)} %copy-done.4, f32[1,64]{1,0:T(1,128)S(1)} %bitcast.19), custom_call_target="tpu_custom_call" | custom-call | tf_op jit(solution)/shard_map/prepare/pallas_call | solution.py:76
  15.0 1.8 %collective-permute-done.1.rest_7_ = bf16[2,256,128]{2,1,0:T(8,128)(2,1)S(1)} collective-permute-done((bf16[2,256,128]{2,1,0:T(8,128)(2,1)S(1)}, bf16[2,256,128]{2,1,0:T(8,128)(2,1)S(1)}, u32[]{:S(2)}, u32[]{:S(2)}) %collective-permute-start.1) | collective-permute-done | bytes 131104 | tf_op jit(solution)/shard_map/keys/ppermute | solution.py:34
  16.9 5.3 %attend.1.rest_0_ = bf16[392,1024]{1,0:T(8,128)(2,1)S(1)} custom-call(s32[8]{0:T(128)S(1)} %stack.28.base_ref.scalar_ref.plane_ref, bf16[256,1024]{1,0:T(8,128)(2,1)S(1)} %bitcast.14, bf16[128,1024]{1,0:T(8,128)(2,1)S(1)} %bitcast.15, bf16[2,128,128]{2,1,0:T(8,128)(2,1)S(1)} %bitcast.18, s32[1,128]{1,0:T(1,128)S(1)} %copy-done.4, ...), custom_call_target="tpu_custom_call" | custom-call | tf_op jit(solution)/shard_map/attend/pallas_call | solution.py:151
  22.3 4.2 %collective-permute-start.5 = (bf16[392,1024]{1,0:T(8,128)(2,1)S(1)}, bf16[392,1024]{1,0:T(8,128)(2,1)S(1)}, u32[]{:S(2)}, u32[]{:S(2)}) collective-permute-start(bf16[392,1024]{1,0:T(8,128)(2,1)S(1)} %attend.1.rest_0_), channel_id=1, source_target_pairs={{0,8},{24,16},{1,9},{25,17},{2,10},{26,18},{3,11},{27,19},{4,12},{... | collective-permute-start | bytes 2408456 | tf_op jit(solution)/shard_map/hand/ppermute | solution.py:34
  26.4 1.6 collective-permute-start.4
  28.7 14.3 %collective-permute-done.5.rest_0_ = bf16[392,1024]{1,0:T(8,128)(2,1)S(1)} collective-permute-done((bf16[392,1024]{1,0:T(8,128)(2,1)S(1)}, bf16[392,1024]{1,0:T(8,128)(2,1)S(1)}, u32[]{:S(2)}, u32[]{:S(2)}) %collective-permute-start.5) | collective-permute-done | bytes 802848 | tf_op jit(solution)/shard_map/hand/ppermute | solution.py:34
  43.0 2.3 %collective-permute-done.4.rest_1_ = bf16[392,1024]{1,0:T(8,128)(2,1)S(1)} collective-permute-done((bf16[392,1024]{1,0:T(8,128)(2,1)S(1)}, bf16[392,1024]{1,0:T(8,128)(2,1)S(1)}, u32[]{:S(2)}, u32[]{:S(2)}) %collective-permute-start.4) | collective-permute-done | bytes 802848 | tf_op jit(solution)/shard_map/rows/ppermute | solution.py:34
  45.3 1.4 pack.2.refs_0_
  47.6 1.6 collective-permute-start.9
  49.2 7.9 %collective-permute-start.10 = (bf16[512,768]{1,0:T(8,128)(2,1)S(1)}, bf16[512,768]{1,0:T(8,128)(2,1)S(1)}, u32[]{:S(2)}, u32[]{:S(2)}) collective-permute-start(bf16[512,768]{1,0:T(8,128)(2,1)S(1)} %pad_maximum_fusion.2), channel_id=1, source_target_pairs={{0,8},{24,16},{1,9},{25,17},{2,10},{26,18},{3,11},{27,19},{4,12},{... | collective-permute-start | bytes 2359304 | tf_op jit(solution)/shard_map/near1/ppermute | solution.py:34
  57.1 16.8 %collective-permute-done.10.refs_8_ = bf16[512,768]{1,0:T(8,128)(2,1)S(1)} collective-permute-done((bf16[512,768]{1,0:T(8,128)(2,1)S(1)}, bf16[512,768]{1,0:T(8,128)(2,1)S(1)}, u32[]{:S(2)}, u32[]{:S(2)}) %collective-permute-start.10) | collective-permute-done | bytes 786464 | tf_op jit(solution)/shard_map/near1/ppermute | solution.py:34
  74.0 1.4 pack.3.refs_2_
  75.5 5.5 %collective-permute-start.18 = (bf16[512,768]{1,0:T(8,128)(2,1)S(1)}, bf16[512,768]{1,0:T(8,128)(2,1)S(1)}, u32[]{:S(2)}, u32[]{:S(2)}) collective-permute-start(bf16[512,768]{1,0:T(8,128)(2,1)S(1)} %fusion), channel_id=1, source_target_pairs={{0,8},{24,16},{1,9},{25,17},{2,10},{26,18},{3,11},{27,19},{4,12},{... | collective-permute-start | bytes 2359304 | tf_op jit(solution)/shard_map/near2/ppermute | solution.py:34
  81.9 1.6 collective-permute-start.15
  85.5 12.9 %collective-permute-done.18.refs_8_ = bf16[512,768]{1,0:T(8,128)(2,1)S(1)} collective-permute-done((bf16[512,768]{1,0:T(8,128)(2,1)S(1)}, bf16[512,768]{1,0:T(8,128)(2,1)S(1)}, u32[]{:S(2)}, u32[]{:S(2)}) %collective-permute-start.18) | collective-permute-done | bytes 786464 | tf_op jit(solution)/shard_map/near2/ppermute | solution.py:34
  99.2 1.3 collective-permute-start.16
  100.6 9.3 %collective-permute-done.16 = bf16[352,256]{1,0:T(8,128)(2,1)S(1)} collective-permute-done((bf16[352,256]{1,0:T(8,128)(2,1)S(1)}, bf16[352,256]{1,0:T(8,128)(2,1)S(1)}, u32[]{:S(2)}, u32[]{:S(2)}) %collective-permute-start.16) | collective-permute-done | bytes 180256 | tf_op jit(solution)/shard_map/return_after0/ppermute | solution.py:34
  110.7 1.3 collective-permute-start.19
  112.0 1.6 collective-permute-start.22
  115.1 1.3 collective-permute-start.24
  116.4 1.6 collective-permute-start.26
  118.0 13.2 %collective-permute-done.14 = bf16[352,256]{1,0:T(8,128)(2,1)S(1)} collective-permute-done((bf16[352,256]{1,0:T(8,128)(2,1)S(1)}, bf16[352,256]{1,0:T(8,128)(2,1)S(1)}, u32[]{:S(2)}, u32[]{:S(2)}) %collective-permute-start.14) | collective-permute-done | bytes 180256 | tf_op jit(solution)/shard_map/cross_after0/ppermute | solution.py:34
  133.0 1.6 collective-permute-start.21
  134.5 17.8 %collective-permute-done.23 = bf16[352,384]{1,0:T(8,128)(2,1)S(1)} collective-permute-done((bf16[352,384]{1,0:T(8,128)(2,1)S(1)}, bf16[352,384]{1,0:T(8,128)(2,1)S(1)}, u32[]{:S(2)}, u32[]{:S(2)}) %collective-permute-start.23) | collective-permute-done | bytes 270368 | tf_op jit(solution)/shard_map/return_after1/ppermute | solution.py:34
  153.3 1.3 collective-permute-start.27
  154.9 4.5 %collective-permute-done.25 = bf16[352,384]{1,0:T(8,128)(2,1)S(1)} collective-permute-done((bf16[352,384]{1,0:T(8,128)(2,1)S(1)}, bf16[352,384]{1,0:T(8,128)(2,1)S(1)}, u32[]{:S(2)}, u32[]{:S(2)}) %collective-permute-start.25) | collective-permute-done | bytes 270368 | tf_op jit(solution)/shard_map/cross_after2/ppermute | solution.py:34
  159.4 2.2 %collective-permute-done.27 = bf16[352,384]{1,0:T(8,128)(2,1)S(1)} collective-permute-done((bf16[352,384]{1,0:T(8,128)(2,1)S(1)}, bf16[352,384]{1,0:T(8,128)(2,1)S(1)}, u32[]{:S(2)}, u32[]{:S(2)}) %collective-permute-start.27) | collective-permute-done | bytes 270368 | tf_op jit(solution)/shard_map/return_after2/ppermute | solution.py:34
  161.9 1.5 collective-permute-done.30
  (83 shorter events, 14.2 us)
Async XLA Ops:
  3.4 2.1 %collective-permute-start.2 = (bf16[256,1024]{1,0:T(8,128)(2,1)S(1)}, bf16[256,1024]{1,0:T(8,128)(2,1)S(1)}, u32[]{:S(2)}, u32[]{:S(2)}) collective-permute-start(bf16[256,1024]{1,0:T(8,128)(2,1)S(1)} %get-tuple-element.87), channel_id=1, source_target_pairs={{0,1},{1,0},{2,3},{3,2},{4,5},{5,4},{6,7},{7,6},{8,9},{9,8},{10,11... | collective-permute-start | bytes 1572872 | tf_op jit(solution)/shard_map/trade0/ppermute | solution.py:34
  3.9 11.1 %collective-permute-start = (bf16[256,1024]{1,0:T(8,128)(2,1)S(1)}, bf16[256,1024]{1,0:T(8,128)(2,1)S(1)}, u32[]{:S(2)}, u32[]{:S(2)}) collective-permute-start(bf16[256,1024]{1,0:T(8,128)(2,1)S(1)} %get-tuple-element.88), channel_id=1, source_target_pairs={{0,1},{1,0},{2,3},{3,2},{4,5},{5,4},{6,7},{7,6},{8,9},{9,8},{10,11... | collective-permute-start | bytes 1572872 | tf_op jit(solution)/shard_map/trade1/ppermute | solution.py:34
  5.5 7.6 %copy-start.4 = (s32[1,128]{1,0:T(1,128)S(1)}, s32[1,128]{1,0:T(1,128)}, u32[]{:S(2)}) copy-start(s32[1,128]{1,0:T(1,128)} %doc_ref.3) | copy-start | bytes 1540
  5.5 16.7 %collective-permute-start.3 = (bf16[512,512]{1,0:T(8,128)(2,1)S(1)}, bf16[512,512]{1,0:T(8,128)(2,1)S(1)}, u32[]{:S(2)}, u32[]{:S(2)}) collective-permute-start(bf16[512,512]{1,0:T(8,128)(2,1)S(1)} %get-tuple-element.60), channel_id=1, source_target_pairs={{0,8},{24,16},{1,9},{25,17},{2,10},{26,18},{3,11},{27,19},{4,12},{... | collective-permute-start | bytes 1572872 | tf_op jit(solution)/shard_map/near0/ppermute | solution.py:34
  10.7 18.0 %collective-permute-start.7 = (bf16[512,1024]{1,0:T(8,128)(2,1)S(1)}, bf16[512,1024]{1,0:T(8,128)(2,1)S(1)}, u32[]{:S(2)}, u32[]{:S(2)}) collective-permute-start(bf16[512,1024]{1,0:T(8,128)(2,1)S(1)} %pad_maximum_fusion.1.refs_4_), channel_id=1, source_target_pairs={{8,16},{16,8},{9,17},{17,9},{10,18},{18,10},{11,19},{19,11},{12,20... | collective-permute-start | bytes 3145736 | tf_op jit(solution)/shard_map/twin0/ppermute | solution.py:34
  11.6 5.3 %collective-permute-start.1 = (bf16[2,256,128]{2,1,0:T(8,128)(2,1)S(1)}, bf16[2,256,128]{2,1,0:T(8,128)(2,1)S(1)}, u32[]{:S(2)}, u32[]{:S(2)}) collective-permute-start(bf16[2,256,128]{2,1,0:T(8,128)(2,1)S(1)} %bitcast.16), channel_id=1, source_target_pairs={{0,4},{4,0},{1,5},{5,1},{2,6},{6,2},{3,7},{7,3},{8,12},{12,8},{9,1... | collective-permute-start | bytes 393224 | tf_op jit(solution)/shard_map/keys/ppermute | solution.py:34
  22.3 20.7 %collective-permute-start.5 = (bf16[392,1024]{1,0:T(8,128)(2,1)S(1)}, bf16[392,1024]{1,0:T(8,128)(2,1)S(1)}, u32[]{:S(2)}, u32[]{:S(2)}) collective-permute-start(bf16[392,1024]{1,0:T(8,128)(2,1)S(1)} %attend.1.rest_0_), channel_id=1, source_target_pairs={{0,8},{24,16},{1,9},{25,17},{2,10},{26,18},{3,11},{27,19},{4,12},{... | collective-permute-start | bytes 2408456 | tf_op jit(solution)/shard_map/hand/ppermute | solution.py:34
  26.4 18.9 %collective-permute-start.4 = (bf16[392,1024]{1,0:T(8,128)(2,1)S(1)}, bf16[392,1024]{1,0:T(8,128)(2,1)S(1)}, u32[]{:S(2)}, u32[]{:S(2)}) collective-permute-start(bf16[392,1024]{1,0:T(8,128)(2,1)S(1)} %attend.1.rest_0_), channel_id=1, source_target_pairs={{0,4},{4,0},{1,5},{5,1},{2,6},{6,2},{3,7},{7,3},{8,12},{12,8},{9,1... | collective-permute-start | bytes 2408456 | tf_op jit(solution)/shard_map/rows/ppermute | solution.py:34
  28.0 0.7 collective-permute-start.6
  46.8 27.2 %collective-permute-start.8 = (bf16[704,1024]{1,0:T(8,128)(2,1)S(1)}, bf16[704,1024]{1,0:T(8,128)(2,1)S(1)}, u32[]{:S(2)}, u32[]{:S(2)}) collective-permute-start(bf16[704,1024]{1,0:T(8,128)(2,1)S(1)} %pack.2.refs_0_), channel_id=1, source_target_pairs={{0,1},{1,0},{2,3},{3,2},{4,5},{5,4},{6,7},{7,6},{8,9},{9,8},{10,11... | collective-permute-start | bytes 4325384 | tf_op jit(solution)/shard_map/own_rows/ppermute | solution.py:34
  46.8 27.1 %collective-permute-start.11 = (bf16[512,1024]{1,0:T(8,128)(2,1)S(1)}, bf16[512,1024]{1,0:T(8,128)(2,1)S(1)}, u32[]{:S(2)}, u32[]{:S(2)}) collective-permute-start(bf16[512,1024]{1,0:T(8,128)(2,1)S(1)} %pad_maximum_fusion.refs_5_), channel_id=1, source_target_pairs={{8,16},{16,8},{9,17},{17,9},{10,18},{18,10},{11,19},{19,11},{12,20... | collective-permute-start | bytes 3145736 | tf_op jit(solution)/shard_map/twin1/ppermute | solution.py:34
  47.6 26.3 %collective-permute-start.9 = (bf16[392,1024]{1,0:T(8,128)(2,1)S(1)}, bf16[392,1024]{1,0:T(8,128)(2,1)S(1)}, u32[]{:S(2)}, u32[]{:S(2)}) collective-permute-start(bf16[392,1024]{1,0:T(8,128)(2,1)S(1)} %collective-permute-done.5.rest_0_), channel_id=1, source_target_pairs={{0,4},{4,0},{1,5},{5,1},{2,6},{6,2},{3,7},{7,3},{8,12},{12,8},{9,1... | collective-permute-start | bytes 2408456 | tf_op jit(solution)/shard_map/other/ppermute | solution.py:34
  49.2 24.7 %collective-permute-start.10 = (bf16[512,768]{1,0:T(8,128)(2,1)S(1)}, bf16[512,768]{1,0:T(8,128)(2,1)S(1)}, u32[]{:S(2)}, u32[]{:S(2)}) collective-permute-start(bf16[512,768]{1,0:T(8,128)(2,1)S(1)} %pad_maximum_fusion.2), channel_id=1, source_target_pairs={{0,8},{24,16},{1,9},{25,17},{2,10},{26,18},{3,11},{27,19},{4,12},{... | collective-permute-start | bytes 2359304 | tf_op jit(solution)/shard_map/near1/ppermute | solution.py:34
  75.4 5.6 %collective-permute-start.12 = (bf16[704,1024]{1,0:T(8,128)(2,1)S(1)}, bf16[704,1024]{1,0:T(8,128)(2,1)S(1)}, u32[]{:S(2)}, u32[]{:S(2)}) collective-permute-start(bf16[704,1024]{1,0:T(8,128)(2,1)S(1)} %pack.3.refs_2_), channel_id=1, source_target_pairs={{0,1},{1,0},{2,3},{3,2},{4,5},{5,4},{6,7},{7,6},{8,9},{9,8},{10,11... | collective-permute-start | bytes 4325384 | tf_op jit(solution)/shard_map/other_rows/ppermute | solution.py:34
  75.5 22.9 %collective-permute-start.18 = (bf16[512,768]{1,0:T(8,128)(2,1)S(1)}, bf16[512,768]{1,0:T(8,128)(2,1)S(1)}, u32[]{:S(2)}, u32[]{:S(2)}) collective-permute-start(bf16[512,768]{1,0:T(8,128)(2,1)S(1)} %fusion), channel_id=1, source_target_pairs={{0,8},{24,16},{1,9},{25,17},{2,10},{26,18},{3,11},{27,19},{4,12},{... | collective-permute-start | bytes 2359304 | tf_op jit(solution)/shard_map/near2/ppermute | solution.py:34
  81.9 17.2 %collective-permute-start.15 = (bf16[704,256]{1,0:T(8,128)(2,1)S(1)}, bf16[704,256]{1,0:T(8,128)(2,1)S(1)}, u32[]{:S(2)}, u32[]{:S(2)}) collective-permute-start(bf16[704,256]{1,0:T(8,128)(2,1)S(1)} %get-tuple-element.70), channel_id=1, source_target_pairs={{0,2},{1,3},{2,0},{3,1},{4,6},{5,7},{6,4},{7,5},{8,10},{9,11},{10,... | collective-permute-start | bytes 1081352 | tf_op jit(solution)/shard_map/cross0/ppermute | solution.py:34
  83.4 17.1 %collective-permute-start.13 = (bf16[704,256]{1,0:T(8,128)(2,1)S(1)}, bf16[704,256]{1,0:T(8,128)(2,1)S(1)}, u32[]{:S(2)}, u32[]{:S(2)}) collective-permute-start(bf16[704,256]{1,0:T(8,128)(2,1)S(1)} %get-tuple-element.68), channel_id=1, source_target_pairs={{8,0},{16,24},{9,1},{17,25},{10,2},{18,26},{11,3},{19,27},{12,4},{... | collective-permute-start | bytes 1081352 | tf_op jit(solution)/shard_map/return0/ppermute | solution.py:34
  84.7 25.2 %collective-permute-start.17 = (bf16[512,768]{1,0:T(8,128)(2,1)S(1)}, bf16[512,768]{1,0:T(8,128)(2,1)S(1)}, u32[]{:S(2)}, u32[]{:S(2)}) collective-permute-start(bf16[512,768]{1,0:T(8,128)(2,1)S(1)} %collective-permute-done.10.refs_8_), channel_id=1, source_target_pairs={{8,16},{16,8},{9,17},{17,9},{10,18},{18,10},{11,19},{19,11},{12,20... | collective-permute-start | bytes 2359304 | tf_op jit(solution)/shard_map/far1/ppermute | solution.py:34
  98.4 15.7 %collective-permute-start.20 = (bf16[512,768]{1,0:T(8,128)(2,1)S(1)}, bf16[512,768]{1,0:T(8,128)(2,1)S(1)}, u32[]{:S(2)}, u32[]{:S(2)}) collective-permute-start(bf16[512,768]{1,0:T(8,128)(2,1)S(1)} %collective-permute-done.18.refs_8_), channel_id=1, source_target_pairs={{8,16},{16,8},{9,17},{17,9},{10,18},{18,10},{11,19},{19,11},{12,20... | collective-permute-start | bytes 2359304 | tf_op jit(solution)/shard_map/far2/ppermute | solution.py:34
  99.2 10.7 %collective-permute-start.16 = (bf16[352,256]{1,0:T(8,128)(2,1)S(1)}, bf16[352,256]{1,0:T(8,128)(2,1)S(1)}, u32[]{:S(2)}, u32[]{:S(2)}) collective-permute-start(bf16[352,256]{1,0:T(8,128)(2,1)S(1)} %slice.119), channel_id=1, source_target_pairs={{8,0},{16,24},{9,1},{17,25},{10,2},{18,26},{11,3},{19,27},{12,4},{... | collective-permute-start | bytes 540680 | tf_op jit(solution)/shard_map/return_after0/ppermute | solution.py:34
  110.7 20.6 %collective-permute-start.19 = (bf16[704,384]{1,0:T(8,128)(2,1)S(1)}, bf16[704,384]{1,0:T(8,128)(2,1)S(1)}, u32[]{:S(2)}, u32[]{:S(2)}) collective-permute-start(bf16[704,384]{1,0:T(8,128)(2,1)S(1)} %get-tuple-element.75), channel_id=1, source_target_pairs={{8,0},{16,24},{9,1},{17,25},{10,2},{18,26},{11,3},{19,27},{12,4},{... | collective-permute-start | bytes 1622024 | tf_op jit(solution)/shard_map/return1/ppermute | solution.py:34
  112.0 19.4 %collective-permute-start.22 = (bf16[704,384]{1,0:T(8,128)(2,1)S(1)}, bf16[704,384]{1,0:T(8,128)(2,1)S(1)}, u32[]{:S(2)}, u32[]{:S(2)}) collective-permute-start(bf16[704,384]{1,0:T(8,128)(2,1)S(1)} %get-tuple-element.80), channel_id=1, source_target_pairs={{0,2},{1,3},{2,0},{3,1},{4,6},{5,7},{6,4},{7,5},{8,10},{9,11},{10,... | collective-permute-start | bytes 1622024 | tf_op jit(solution)/shard_map/cross1/ppermute | solution.py:34
  113.6 17.6 %collective-permute-start.14 = (bf16[352,256]{1,0:T(8,128)(2,1)S(1)}, bf16[352,256]{1,0:T(8,128)(2,1)S(1)}, u32[]{:S(2)}, u32[]{:S(2)}) collective-permute-start(bf16[352,256]{1,0:T(8,128)(2,1)S(1)} %fusion.10), channel_id=1, source_target_pairs={{0,2},{1,3},{2,0},{3,1},{4,6},{5,7},{6,4},{7,5},{8,10},{9,11},{10,... | collective-permute-start | bytes 540680 | tf_op jit(solution)/shard_map/cross_after0/ppermute | solution.py:34
  115.1 37.4 %collective-permute-start.24 = (bf16[704,384]{1,0:T(8,128)(2,1)S(1)}, bf16[704,384]{1,0:T(8,128)(2,1)S(1)}, u32[]{:S(2)}, u32[]{:S(2)}) collective-permute-start(bf16[704,384]{1,0:T(8,128)(2,1)S(1)} %get-tuple-element.82), channel_id=1, source_target_pairs={{8,0},{16,24},{9,1},{17,25},{10,2},{18,26},{11,3},{19,27},{12,4},{... | collective-permute-start | bytes 1622024 | tf_op jit(solution)/shard_map/return2/ppermute | solution.py:34
  116.4 36.7 %collective-permute-start.26 = (bf16[704,384]{1,0:T(8,128)(2,1)S(1)}, bf16[704,384]{1,0:T(8,128)(2,1)S(1)}, u32[]{:S(2)}, u32[]{:S(2)}) collective-permute-start(bf16[704,384]{1,0:T(8,128)(2,1)S(1)} %get-tuple-element.85), channel_id=1, source_target_pairs={{0,2},{1,3},{2,0},{3,1},{4,6},{5,7},{6,4},{7,5},{8,10},{9,11},{10,... | collective-permute-start | bytes 1622024 | tf_op jit(solution)/shard_map/cross2/ppermute | solution.py:34
  131.3 30.6 %collective-permute-start.28 = (bf16[176,512]{1,0:T(8,128)(2,1)S(1)}, bf16[176,512]{1,0:T(8,128)(2,1)S(1)}, u32[]{:S(2)}, u32[]{:S(2)}) collective-permute-start(bf16[176,512]{1,0:T(8,128)(2,1)S(1)} %get-tuple-element.104), channel_id=1, source_target_pairs={{0,1},{1,0},{2,3},{3,2},{4,5},{5,4},{6,7},{7,6},{8,9},{9,8},{10,11... | collective-permute-start | bytes 540680 | tf_op jit(solution)/shard_map/rest0/ppermute | solution.py:34
  131.5 20.8 %collective-permute-start.23 = (bf16[352,384]{1,0:T(8,128)(2,1)S(1)}, bf16[352,384]{1,0:T(8,128)(2,1)S(1)}, u32[]{:S(2)}, u32[]{:S(2)}) collective-permute-start(bf16[352,384]{1,0:T(8,128)(2,1)S(1)} %slice.127), channel_id=1, source_target_pairs={{8,0},{16,24},{9,1},{17,25},{10,2},{18,26},{11,3},{19,27},{12,4},{... | collective-permute-start | bytes 811016 | tf_op jit(solution)/shard_map/return_after1/ppermute | solution.py:34
  133.0 21.6 %collective-permute-start.21 = (bf16[352,384]{1,0:T(8,128)(2,1)S(1)}, bf16[352,384]{1,0:T(8,128)(2,1)S(1)}, u32[]{:S(2)}, u32[]{:S(2)}) collective-permute-start(bf16[352,384]{1,0:T(8,128)(2,1)S(1)} %fusion.8), channel_id=1, source_target_pairs={{0,2},{1,3},{2,0},{3,1},{4,6},{5,7},{6,4},{7,5},{8,10},{9,11},{10,... | collective-permute-start | bytes 811016 | tf_op jit(solution)/shard_map/cross_after1/ppermute | solution.py:34
  152.5 6.8 %collective-permute-start.25 = (bf16[352,384]{1,0:T(8,128)(2,1)S(1)}, bf16[352,384]{1,0:T(8,128)(2,1)S(1)}, u32[]{:S(2)}, u32[]{:S(2)}) collective-permute-start(bf16[352,384]{1,0:T(8,128)(2,1)S(1)} %slice.131), channel_id=1, source_target_pairs={{0,2},{1,3},{2,0},{3,1},{4,6},{5,7},{6,4},{7,5},{8,10},{9,11},{10,... | collective-permute-start | bytes 811016 | tf_op jit(solution)/shard_map/cross_after2/ppermute | solution.py:34
  153.3 8.4 %collective-permute-start.27 = (bf16[352,384]{1,0:T(8,128)(2,1)S(1)}, bf16[352,384]{1,0:T(8,128)(2,1)S(1)}, u32[]{:S(2)}, u32[]{:S(2)}) collective-permute-start(bf16[352,384]{1,0:T(8,128)(2,1)S(1)} %slice.133), channel_id=1, source_target_pairs={{8,0},{16,24},{9,1},{17,25},{10,2},{18,26},{11,3},{19,27},{12,4},{... | collective-permute-start | bytes 811016 | tf_op jit(solution)/shard_map/return_after2/ppermute | solution.py:34
  154.8 7.1 %collective-permute-start.29 = (bf16[176,768]{1,0:T(8,128)(2,1)S(1)}, bf16[176,768]{1,0:T(8,128)(2,1)S(1)}, u32[]{:S(2)}, u32[]{:S(2)}) collective-permute-start(bf16[176,768]{1,0:T(8,128)(2,1)S(1)} %get-tuple-element.96), channel_id=1, source_target_pairs={{0,1},{1,0},{2,3},{3,2},{4,5},{5,4},{6,7},{7,6},{8,9},{9,8},{10,11... | collective-permute-start | bytes 811016 | tf_op jit(solution)/shard_map/rest1/ppermute | solution.py:34
  161.8 1.6 collective-permute-start.30
  (5 other events, 32.3 us)
